TPU v7x, 256 devices: a whole 4x4x8 slice. The times are simulated.
256 devices in a mesh: wide: 64 (over y, z, core), narrow: 4 (over x).
Axes of the slice: x: 4, y: 4, z: 8, core: 2. Of those that a mesh axis runs over, the one named last changes fastest.
Arguments:
- diag_block: float32 [256, 512, 512], P('wide', None, 'narrow'), as said below
- panel: float32 [256, 1024, 512], P('wide', None, 'narrow'), may hold values from -2 to 2
- panel_count: int32 [256], P('wide'), may hold values from 1 to 8, 1152 in all
- pair_owner: int32 [9216, 1], P('wide'), may hold values from 0 to 63; in each aligned block of 144 rows (0 to 143, 144 to 287, ...) at most 3 rows name the same one
- pair_slot: int32 [9216], P('wide'), may hold values from 0 to 7
- ancestor: float32 [512, 128, 128], P(('wide', 'narrow')), may hold values from -6 to 6
Outputs:
- factor: float32 [256, 512, 512], P('wide', None, 'narrow')
- lower_panel: float32 [256, 1024, 512], P('wide', None, 'narrow')
- updated: float32 [512, 128, 128], P(('wide', 'narrow'))
Inputs may be any that keep to these rules, and one draw needn't show every extreme that they name: Each diag_block[s] is symmetric, and its least eigenvalue is 0.2 or more. `pair_owner`: among the rows of one index of wide no owner is named more than 3 times, a bound that some block reaches.
All inputs are finite; a program needn't handle non-finite values. No bound on the sum of `panel_count` on one device may be relied on, other than what follows from the above.
Results may differ from a plain program's by a relative error of at most 0.00016.
Values sent between devices are 32-bit elements; how exact they have to be, the bound alone decides.
A program may use at most 128 MiB of HBM per device.

v0:
```python
import functools

import jax
import jax.numpy as jnp
import numpy as np
from jax import lax
from jax.experimental import pallas as pl
from jax.experimental.pallas import tpu as pltpu
from jax.sharding import PartitionSpec as P

MESH = pl.DeviceIdType.MESH

W = 512
B = 128
P_SIZE = 8
T_DEV = 2


def pair_lists(count):
    first = []
    second = []
    for outer in range(count):
        for inner in range(outer + 1):
            first.append(outer)
            second.append(inner)
    return (np.array(first, np.int32), np.array(second, np.int32))


def columns_out_kernel(x_ref, y_ref, send_sem, recv_sem, own_sem, *, count, group, width):
    me = lax.axis_index("narrow")
    wide = lax.axis_index("wide")
    barrier = pltpu.get_barrier_semaphore()
    for d in range(1, count):
        peer = lax.rem(me + d, count)
        pl.semaphore_signal(barrier, inc=1, device_id=(wide, peer), device_id_type=MESH)
    pl.semaphore_wait(barrier, count - 1)
    mine = y_ref.at[pl.ds(me * group, group)]
    own = pltpu.make_async_copy(
        x_ref.at[:, :, pl.ds(pl.multiple_of(me * width, width), width)], mine, own_sem
    )
    own.start()
    copies = []
    for d in range(1, count):
        peer = lax.rem(me + d, count)
        copy = pltpu.make_async_remote_copy(
            src_ref=x_ref.at[:, :, pl.ds(pl.multiple_of(peer * width, width), width)],
            dst_ref=mine,
            send_sem=send_sem.at[d - 1],
            recv_sem=recv_sem.at[d - 1],
            device_id=(wide, peer),
            device_id_type=MESH,
        )
        copy.start()
        copies.append(copy)
    own.wait()
    for copy in copies:
        copy.wait()


def columns_out(x, count, width, collective_id):
    group, rows, _ = x.shape
    nbytes = x.size * 4
    return pl.pallas_call(
        functools.partial(columns_out_kernel, count=count, group=group, width=width),
        out_shape=jax.ShapeDtypeStruct((group * count, rows, width), x.dtype),
        in_specs=[pl.BlockSpec(memory_space=pl.ANY)],
        out_specs=pl.BlockSpec(memory_space=pl.ANY),
        scratch_shapes=[
            pltpu.SemaphoreType.DMA((count - 1,)),
            pltpu.SemaphoreType.DMA((count - 1,)),
            pltpu.SemaphoreType.DMA,
        ],
        compiler_params=pltpu.CompilerParams(collective_id=collective_id, has_side_effects=True),
        cost_estimate=pl.CostEstimate(flops=0, bytes_accessed=2 * nbytes, transcendentals=0),
    )(x)


def block_chol_kernel(a_ref, l_ref, inv_ref, work, upper, elim):
    n = a_ref.shape[0]
    work[...] = a_ref[...]
    rows = lax.broadcasted_iota(jnp.int32, (n, n), 0)
    cols = lax.broadcasted_iota(jnp.int32, (n, n), 1)
    elim[...] = (rows == cols).astype(jnp.float32)
    lane = lax.broadcasted_iota(jnp.int32, (1, n), 1)
    row_id = lax.broadcasted_iota(jnp.int32, (n, 1), 0)

    def step(j, carry):
        r = work[pl.ds(j, 1), :]
        piv = jnp.sum(jnp.where(lane == j, r, 0.0), axis=1, keepdims=True)
        root = jnp.sqrt(piv)
        scale = 1.0 / root
        u_row = jnp.where(lane >= j, r * scale, 0.0)
        upper[pl.ds(j, 1), :] = u_row
        e_row = elim[pl.ds(j, 1), :]
        inv_ref[pl.ds(j, 1), :] = e_row * scale
        u_col = jnp.transpose(jnp.broadcast_to(u_row, (8, n)))[:, 0:1]
        work[...] = work[...] - u_col * u_row
        mult = jnp.where(row_id > j, u_col * scale, 0.0)
        elim[...] = elim[...] - mult * e_row
        return carry

    lax.fori_loop(0, n, step, 0)
    l_ref[...] = jnp.transpose(upper[...])


def block_chol(a):
    n = a.shape[-1]
    return pl.pallas_call(
        block_chol_kernel,
        out_shape=(jax.ShapeDtypeStruct((n, n), jnp.float32), jax.ShapeDtypeStruct((n, n), jnp.float32)),
        in_specs=[pl.BlockSpec(memory_space=pltpu.VMEM)],
        out_specs=(pl.BlockSpec(memory_space=pltpu.VMEM), pl.BlockSpec(memory_space=pltpu.VMEM)),
        scratch_shapes=[pltpu.VMEM((n, n), jnp.float32)] * 3,
    )(a)


def mm(a, b):
    return jnp.einsum("sik,skj->sij", a, b, precision=lax.Precision.HIGHEST)


def mm_t(a, b):
    return jnp.einsum("sik,sjk->sij", a, b, precision=lax.Precision.HIGHEST)


def blocked_cholesky(matrix):
    batch, size, _ = matrix.shape
    nblk = size // B
    eye = jnp.broadcast_to(jnp.eye(B, dtype=jnp.float32), (batch, B, B))
    trailing = matrix
    diag_l, diag_inv, below = [], [], []
    inverse_rows = []
    for k in range(nblk):
        head = trailing[:, :B, :B]
        pieces = [block_chol(head[b]) for b in range(batch)]
        l_kk = jnp.stack([p[0] for p in pieces])
        i_kk = jnp.stack([p[1] for p in pieces])
        diag_l.append(l_kk)
        diag_inv.append(i_kk)
        if k > 0:
            left = jnp.concatenate([below[j][:, (k - j - 1) * B:(k - j) * B, :] for j in range(k)], axis=2)
            upper = jnp.concatenate(inverse_rows, axis=1)
            rest = -mm(left, upper)
            rest = jnp.concatenate([rest[:, :, :k * B], eye, rest[:, :, (k + 1) * B:]], axis=2)
            inverse_rows.append(mm(i_kk, rest))
        else:
            inverse_rows.append(jnp.concatenate(
                [i_kk, jnp.zeros((batch, B, size - B), jnp.float32)], axis=2))
        if k < nblk - 1:
            panel_k = mm_t(trailing[:, B:, :B], i_kk)
            below.append(panel_k)
            trailing = trailing[:, B:, B:] - mm_t(panel_k, panel_k)
    columns = []
    for k in range(nblk):
        parts = []
        if k > 0:
            parts.append(jnp.zeros((batch, k * B, B), jnp.float32))
        parts.append(diag_l[k])
        if k < nblk - 1:
            parts.append(below[k])
        columns.append(jnp.concatenate(parts, axis=1))
    factor = jnp.concatenate(columns, axis=2)
    inverse = jnp.concatenate(inverse_rows, axis=1)
    return factor, inverse


def local(diag_block, panel, panel_count, pair_owner, pair_slot, ancestor):
    supers_here = diag_block.shape[0]
    col_width = diag_block.shape[2]
    diag_rows = diag_block.shape[1]
    narrow_index = lax.axis_index("narrow")
    narrow_count = lax.axis_size("narrow")
    wide_count = lax.axis_size("wide")
    group = supers_here // narrow_count

    whole_diag = lax.all_to_all(diag_block, "narrow", split_axis=0, concat_axis=2, tiled=True)
    whole_panel = lax.all_to_all(panel, "narrow", split_axis=0, concat_axis=2, tiled=True)

    factor, inverse = blocked_cholesky(whole_diag)
    lower_panel = jnp.einsum(
        "srk,sck->src", whole_panel, inverse, precision=lax.Precision.HIGHEST
    )
    counts = lax.dynamic_slice_in_dim(panel_count, narrow_index * group, group)
    block_index = jnp.arange(P_SIZE * B, dtype=jnp.int32) // B
    live = (block_index[None, :] < counts[:, None]).astype(jnp.float32)
    lower_panel = lower_panel * live[:, :, None]

    first, second = pair_lists(P_SIZE)
    npair = len(first)
    blocks = lower_panel.reshape(group, P_SIZE, B, W)
    gram = jnp.einsum("siac,sjbc->sijab", blocks, blocks, precision=lax.Precision.HIGHEST)
    gram = gram.reshape(group, P_SIZE * P_SIZE, B, B)
    contribution = gram[:, first * P_SIZE + second]

    quarters = lax.all_to_all(contribution, "narrow", split_axis=2, concat_axis=0, tiled=True)
    quarter_rows = quarters.shape[2]
    pair_rows = supers_here * npair
    quarters = quarters.reshape(pair_rows, quarter_rows, B)

    capacity = max(2, (pair_rows + wide_count - 1) // wide_count)
    owners = pair_owner[:, 0]
    owner_table = (owners[:, None] == jnp.arange(wide_count, dtype=jnp.int32)[None, :]).astype(
        jnp.int32
    )
    earlier = jnp.cumsum(owner_table, axis=0) - owner_table
    rank_here = jnp.sum(earlier * owner_table, axis=1)
    position = owners * capacity + rank_here
    buffer_rows = wide_count * capacity
    row_slots = T_DEV * narrow_count
    slot_ids = jnp.full((buffer_rows,), -1.0, jnp.float32).at[position].set(
        pair_slot.astype(jnp.float32)
    )
    source_row = jnp.zeros((buffer_rows,), jnp.int32).at[position].set(
        jnp.arange(pair_rows, dtype=jnp.int32)
    )
    filled = jnp.zeros((buffer_rows,), jnp.bool_).at[position].set(True)
    send_buffer = jnp.where(filled[:, None, None], quarters[source_row], 0.0)
    meta = jnp.zeros((wide_count, 8, B), jnp.float32)
    meta = meta.at[:, 0, :capacity].set(slot_ids.reshape(wide_count, capacity))
    send_buffer = jnp.concatenate(
        [send_buffer.reshape(wide_count, capacity * quarter_rows, B), meta], axis=1
    )
    send_buffer, factor, lower_panel = lax.optimization_barrier((send_buffer, factor, lower_panel))
    received = lax.all_to_all(send_buffer, "wide", split_axis=0, concat_axis=0, tiled=True)
    factor_back = columns_out(factor, narrow_count, col_width, 0)
    lower_back = columns_out(lower_panel, narrow_count, col_width, 1)
    received, factor_back, lower_back = lax.optimization_barrier((received, factor_back, lower_back))
    got_slots = received[:, capacity * quarter_rows, :capacity].reshape(buffer_rows)
    got_slots = got_slots.astype(jnp.int32)
    received = received[:, : capacity * quarter_rows, :].reshape(buffer_rows, quarter_rows, B)
    slot_table = (got_slots[:, None] == jnp.arange(row_slots, dtype=jnp.int32)[None, :]).astype(
        jnp.float32
    )
    slot_sums = jnp.einsum("ri,rab->iab", slot_table, received, precision=lax.Precision.HIGHEST)
    slot_sums = slot_sums.reshape(narrow_count, T_DEV, quarter_rows, B)
    summed = lax.all_to_all(slot_sums, "narrow", split_axis=0, concat_axis=2, tiled=True)
    summed = summed.reshape(T_DEV, B, B)
    return (factor_back, lower_back, ancestor - summed)


def solution(mesh):
    placed = (
        P("wide", None, "narrow"),
        P("wide", None, "narrow"),
        P("wide"),
        P("wide", None),
        P("wide"),
        P(("wide", "narrow"), None, None),
    )
    return jax.shard_map(
        local,
        mesh=mesh,
        in_specs=placed,
        out_specs=(
            P("wide", None, "narrow"),
            P("wide", None, "narrow"),
            P(("wide", "narrow"), None, None),
        ),
        check_vma=False,
    )
```

profile of v0, /device:TPU:9, one launch (start us, length us, event | category | flops | bytes accessed | tf_op | source)
XLA Modules:
  0.0 385.9 jit_solution(13740786664237806100)
XLA Ops:
  0.7 4.2 %all-to-all-start = ((f32[4,512,128]{2,1,0:T(8,128)}), f32[4,512,128]{2,1,0:T(8,128)S(1)}, u32[]{:S(2)}, u32[]{:S(2)}) async-start(f32[4,512,128]{2,1,0:T(8,128)} %param.10), calls=%async_computation | async-start | bytes 2097152 | tf_op jit(solution)/shard_map/all_to_all | solution.py:175
  4.8 1.8 copy.68
  8.5 10.5 %all-to-all-done = f32[4,512,128]{2,1,0:T(8,128)S(1)} async-done(((f32[4,512,128]{2,1,0:T(8,128)}), f32[4,512,128]{2,1,0:T(8,128)S(1)}, u32[]{:S(2)}, u32[]{:S(2)}) %all-to-all-start) | async-done | bytes 1048608 | tf_op jit(solution)/shard_map/all_to_all | solution.py:175
  19.0 3.6 all-to-all-start.1
  24.4 39.2 %shard_map.103 = (f32[128,128]{1,0:T(8,128)}, f32[128,128]{1,0:T(8,128)}) custom-call(f32[128,128]{1,0:T(8,128)} %slice_bitcast_fusion.10.a_ref), custom_call_target="tpu_custom_call" | custom-call | tf_op jit(solution)/shard_map/pallas_call | solution.py:108
  65.1 1.7 fusion.3
  67.5 39.2 %shard_map.104 = (f32[128,128]{1,0:T(8,128)}, f32[128,128]{1,0:T(8,128)}) custom-call(f32[128,128]{1,0:T(8,128)} %slice_bitcast_fusion.9.a_ref), custom_call_target="tpu_custom_call" | custom-call | tf_op jit(solution)/shard_map/pallas_call | solution.py:108
  112.3 1.5 fusion.72
  117.3 39.2 %shard_map.105 = (f32[128,128]{1,0:T(8,128)}, f32[128,128]{1,0:T(8,128)}) custom-call(f32[128,128]{1,0:T(8,128)} %slice_bitcast_fusion.6.a_ref), custom_call_target="tpu_custom_call" | custom-call | tf_op jit(solution)/shard_map/pallas_call | solution.py:108
  156.6 1.4 convolution_bitcast_fusion.3
  159.1 1.5 fusion.4
  161.3 1.7 fusion.9.a_ref
  163.0 39.2 %shard_map.106 = (f32[128,128]{1,0:T(8,128)}, f32[128,128]{1,0:T(8,128)}) custom-call(f32[128,128]{1,0:T(8,128)} %fusion.9.a_ref), custom_call_target="tpu_custom_call" | custom-call | tf_op jit(solution)/shard_map/pallas_call | solution.py:108
  202.3 1.4 convolution_bitcast_fusion.2
  205.0 5.1 %convolution_multiply_fusion = f32[512,1024]{0,1:T(8,128)S(1)} fusion(f32[1024,512]{0,1:T(8,128)} %bitcast.189, f32[1,128,512]{2,1,0:T(8,128)S(1)} %convolution_bitcast_fusion.2, f32[1,128,512]{2,1,0:T(8,128)S(1)} %convolution_bitcast_fusion.3, f32[1,128,512]{2,1,0:T(8,128)S(1)} %convolution_bitcast_fusion.5, f32[1,128,512]{2,1,0:T(8,128)S(1)} %concatenate.47, ...), kind=kOutput, calls=%fused_computation.12 | convolution fusion | flops 3222536192 | bytes 5246976 | tf_op jit(solution)/shard_map/srk,sck->src/dot_general | solution.py:179
  210.2 9.0 %convolution_bitcast_fusion = f32[1,8,8,128,128]{3,4,1,2,0:T(8,128)} fusion(f32[8,128,512,1]{2,1,3,0:T(8,128)S(1)} %bitcast.180, f32[8,128,512,1]{2,1,0,3:T(8,128)S(1)} %bitcast.181), kind=kOutput, calls=%fused_computation.11 | convolution fusion | flops 6442450944 | bytes 8388608 | tf_op jit(solution)/shard_map/siac,sjbc->sijab/dot_general | solution.py:190
  219.1 5.4 %copy.70 = f32[1,8,8,128,128]{4,3,2,1,0:T(8,128)} copy(f32[1,8,8,128,128]{3,4,1,2,0:T(8,128)} %convolution_bitcast_fusion) | data formatting | bytes 8388608 | tf_op jit(solution)/shard_map/siac,sjbc->sijab/transpose | solution.py:190
  224.5 2.9 gather_fusion
  227.4 3.8 copy.71
  231.3 4.3 %all-to-all-start.2 = ((f32[1,36,128,128]{3,0,1,2:T(1,128)}), f32[1,36,128,128]{3,0,1,2:T(1,128)S(1)}, u32[]{:S(2)}, u32[]{:S(2)}) async-start(f32[1,36,128,128]{3,0,1,2:T(1,128)} %copy.71), calls=%async_computation.2 | async-start | bytes 4718592 | tf_op jit(solution)/shard_map/all_to_all | solution.py:194
  241.6 20.8 %all-to-all-done.2 = f32[1,36,128,128]{3,0,1,2:T(1,128)S(1)} async-done(((f32[1,36,128,128]{3,0,1,2:T(1,128)}), f32[1,36,128,128]{3,0,1,2:T(1,128)S(1)}, u32[]{:S(2)}, u32[]{:S(2)}) %all-to-all-start.2) | async-done | bytes 2359328 | tf_op jit(solution)/shard_map/all_to_all | solution.py:194
  262.9 2.5 gather_fusion.1
  265.5 3.2 bitcast_select_fusion
  268.7 2.0 select_maximum_fusion
  270.6 15.1 %all-to-all-start.3 = ((f32[64,104,128]{2,1,0:T(8,128)}), f32[64,104,128]{2,1,0:T(8,128)S(1)}, u32[]{:S(2)}, u32[]{:S(2)}) async-start(f32[64,104,128]{2,1,0:T(8,128)} %select_maximum_fusion), calls=%async_computation.3 | async-start | bytes 6815744 | tf_op jit(solution)/shard_map/all_to_all | solution.py:223
  285.7 26.4 %shard_map.108 = f32[4,1024,128]{2,1,0:T(8,128)} custom-call(f32[1,1024,512]{2,1,0:T(8,128)} %bitcast.182), custom_call_target="tpu_custom_call" | custom-call | bytes 4194304 | tf_op jit(solution)/shard_map/pallas_call | solution.py:63
  312.2 14.3 %shard_map.107 = f32[4,512,128]{2,1,0:T(8,128)} custom-call(f32[1,512,512]{2,1,0:T(8,128)} %select_maximum_fusion.1.x_ref), custom_call_target="tpu_custom_call" | custom-call | bytes 2097152 | tf_op jit(solution)/shard_map/pallas_call | solution.py:63
  326.5 38.2 %all-to-all-done.3 = f32[64,104,128]{2,1,0:T(8,128)S(1)} async-done(((f32[64,104,128]{2,1,0:T(8,128)}), f32[64,104,128]{2,1,0:T(8,128)S(1)}, u32[]{:S(2)}, u32[]{:S(2)}) %all-to-all-start.3) | async-done | bytes 3407904 | tf_op jit(solution)/shard_map/all_to_all | solution.py:223
  364.7 2.0 slice.118
  368.4 4.8 %fusion = f32[4,2,32,128]{3,0,2,1:T(4,128)S(1)} fusion(f32[192,32,128]{2,1,0:T(8,128)} %bitcast.184, s32[4,2]{0,1:T(2,128)S(1)} %multiply_add_fusion, s32[192]{0:T(256)S(1)} %convert_element_type.46), kind=kOutput, calls=%fused_computation.7 | convolution fusion | flops 75499008 | bytes 3277600 | tf_op jit(solution)/shard_map/ri,rab->iab/dot_general | solution.py:233
  373.8 3.3 all-to-all-start.4
  377.2 5.7 %all-to-all-done.4 = f32[4,2,32,128]{3,2,1,0:T(8,128)S(1)} async-done(((f32[4,2,32,128]{3,2,1,0:T(8,128)}), f32[4,2,32,128]{3,2,1,0:T(8,128)S(1)}, u32[]{:S(2)}, u32[]{:S(2)}) %all-to-all-start.4) | async-done | bytes 131104 | tf_op jit(solution)/shard_map/all_to_all | solution.py:235
  (95 shorter events, 29.6 us)
Async XLA Ops:
  0.6 7.2 %copy-start.16 = (s32[36]{0:T(128)S(1)}, s32[36]{0:T(128)}, u32[]{:S(2)}) copy-start(s32[36]{0:T(128)} %constant.104) | copy-start | bytes 436
  0.6 4.2 %copy-start.5 = (f32[4,1024,128]{2,1,0:T(8,128)S(1)}, f32[4,1024,128]{2,1,0:T(8,128)}, u32[]{:S(2)}) copy-start(f32[4,1024,128]{2,1,0:T(8,128)} %param.11) | copy-start | bytes 6291460
  0.7 6.0 %copy-start.17 = (s32[4]{0:T(128)S(1)}, s32[4]{0:T(128)}, u32[]{:S(2)}) copy-start(s32[4]{0:T(128)} %param.12) | copy-start | bytes 52
  0.7 18.3 %all-to-all-start = ((f32[4,512,128]{2,1,0:T(8,128)}), f32[4,512,128]{2,1,0:T(8,128)S(1)}, u32[]{:S(2)}, u32[]{:S(2)}) async-start(f32[4,512,128]{2,1,0:T(8,128)} %param.10), calls=%async_computation | async-start | bytes 2097152 | tf_op jit(solution)/shard_map/all_to_all | solution.py:175
  19.0 184.7 %all-to-all-start.1 = ((f32[4,1024,128]{1,2,0:T(8,128)}), f32[4,1024,128]{1,2,0:T(8,128)S(1)}, u32[]{:S(2)}, u32[]{:S(2)}) async-start(f32[4,1024,128]{1,2,0:T(8,128)} %copy.68), calls=%async_computation.1 | async-start | bytes 4194304 | tf_op jit(solution)/shard_map/all_to_all | solution.py:176
  22.8 1.0 copy-start.4
  63.6 47.4 %copy-start.8 = (f32[128,128]{1,0:T(8,128)S(1)}, f32[128,128]{1,0:T(8,128)}, u32[]{:S(2)}) copy-start(f32[128,128]{1,0:T(8,128)} %get-tuple-element.29) | copy-start | bytes 196612
  116.0 0.7 copy-start.7
  203.7 1.3 copy-start.1
  210.1 9.0 %copy-start = (f32[512,1024]{0,1:T(8,128)}, f32[512,1024]{0,1:T(8,128)S(1)}, u32[]{:S(2)}) copy-start(f32[512,1024]{0,1:T(8,128)S(1)} %convolution_multiply_fusion) | copy-start | bytes 6291460
  231.2 4.4 %copy-start.14 = (s32[144,1]{0,1:T(1,128)S(1)}, s32[144,1]{0,1:T(1,128)}, u32[]{:S(2)}) copy-start(s32[144,1]{0,1:T(1,128)} %param.13) | copy-start | bytes 1732
  231.2 7.9 %copy-start.15 = (s32[144]{0:T(256)S(1)}, s32[144]{0:T(256)}, u32[]{:S(2)}) copy-start(s32[144]{0:T(256)} %param.14) | copy-start | bytes 1732
  231.3 9.2 %copy-start.6 = (f32[256,128]{1,0:T(8,128)S(1)}, f32[256,128]{1,0:T(8,128)}, u32[]{:S(2)}) copy-start(f32[256,128]{1,0:T(8,128)} %copy.67) | copy-start | bytes 393220
  231.3 9.2 %copy-start.10 = (f32[128,128]{1,0:T(8,128)S(1)}, f32[128,128]{1,0:T(8,128)}, u32[]{:S(2)}) copy-start(f32[128,128]{1,0:T(8,128)} %get-tuple-element.33) | copy-start | bytes 196612
  231.3 9.2 %copy-start.11 = (f32[128,128]{1,0:T(8,128)S(1)}, f32[128,128]{1,0:T(8,128)}, u32[]{:S(2)}) copy-start(f32[128,128]{1,0:T(8,128)} %get-tuple-element.34) | copy-start | bytes 196612
  231.3 9.2 %copy-start.12 = (f32[128,128]{1,0:T(8,128)S(1)}, f32[128,128]{1,0:T(8,128)}, u32[]{:S(2)}) copy-start(f32[128,128]{1,0:T(8,128)} %get-tuple-element.35) | copy-start | bytes 196612
  231.3 9.2 %copy-start.13 = (f32[128,128]{1,0:T(8,128)S(1)}, f32[128,128]{1,0:T(8,128)}, u32[]{:S(2)}) copy-start(f32[128,128]{1,0:T(8,128)} %get-tuple-element.36) | copy-start | bytes 196612
  231.3 31.1 %all-to-all-start.2 = ((f32[1,36,128,128]{3,0,1,2:T(1,128)}), f32[1,36,128,128]{3,0,1,2:T(1,128)S(1)}, u32[]{:S(2)}, u32[]{:S(2)}) async-start(f32[1,36,128,128]{3,0,1,2:T(1,128)} %copy.71), calls=%async_computation.2 | async-start | bytes 4718592 | tf_op jit(solution)/shard_map/all_to_all | solution.py:194
  270.6 94.0 %all-to-all-start.3 = ((f32[64,104,128]{2,1,0:T(8,128)}), f32[64,104,128]{2,1,0:T(8,128)S(1)}, u32[]{:S(2)}, u32[]{:S(2)}) async-start(f32[64,104,128]{2,1,0:T(8,128)} %select_maximum_fusion), calls=%async_computation.3 | async-start | bytes 6815744 | tf_op jit(solution)/shard_map/all_to_all | solution.py:223
  366.7 16.2 %copy-start.9 = (f32[2,128,128]{2,1,0:T(8,128)S(1)}, f32[2,128,128]{2,1,0:T(8,128)}, u32[]{:S(2)}) copy-start(f32[2,128,128]{2,1,0:T(8,128)} %param.15) | copy-start | bytes 393220
  367.4 16.2 %copy-start.3 = (f32[4,512,128]{2,1,0:T(8,128)S(1)}, f32[4,512,128]{2,1,0:T(8,128)}, u32[]{:S(2)}) copy-start(f32[4,512,128]{2,1,0:T(8,128)} %shard_map.107) | copy-start | bytes 3145732
  368.4 16.2 %copy-start.2 = (f32[4,1024,128]{2,1,0:T(8,128)S(1)}, f32[4,1024,128]{2,1,0:T(8,128)}, u32[]{:S(2)}) copy-start(f32[4,1024,128]{2,1,0:T(8,128)} %shard_map.108) | copy-start | bytes 6291460
  373.8 9.1 %all-to-all-start.4 = ((f32[4,2,32,128]{3,2,1,0:T(8,128)}), f32[4,2,32,128]{3,2,1,0:T(8,128)S(1)}, u32[]{:S(2)}, u32[]{:S(2)}) async-start(f32[4,2,32,128]{3,2,1,0:T(8,128)} %copy.76), calls=%async_computation.4 | async-start | bytes 262144 | tf_op jit(solution)/shard_map/all_to_all | solution.py:235
where the time goes:
time: 387 us; the launch traced here: 386 us
  Pallas kernels  198 us (51%)
  waiting for transfers between devices  75.3 us (19%)
  local copies, waits for them, and re-layouts  38.2 us (10%)
  matrix products  33.4 us (9%)
  starting transfers between devices  30.5 us (8%)
  other arithmetic  9.67 us (2%)
    pallas_call x4, Pallas kernels, block_chol(): pl.pallas_call(block_chol_kernel, out_shape=(jax.ShapeDtypeStruct((n, n),...  157 us
    pallas_call x2, Pallas kernels, columns_out(): pl.pallas_call(functools.partial(columns_out_kernel, count=count, group=g...  40.7 us
    all_to_all x1, waiting for transfers between devices, local(): lax.all_to_all(send_buffer, 'wide', split_axis=0, concat_axis=0, tiled=True)  38.2 us
    all_to_all x1, waiting for transfers between devices, local(): lax.all_to_all(contribution, 'narrow', split_axis=2, concat_axis=0, tiled...  20.8 us
    all_to_all x1, starting transfers between devices, local(): lax.all_to_all(send_buffer, 'wide', split_axis=0, concat_axis=0, tiled=True)  15.1 us
    all_to_all x1, waiting for transfers between devices, local(): lax.all_to_all(diag_block, 'narrow', split_axis=0, concat_axis=2, tiled=T...  10.5 us
    dot_general x1, matrix products, local(): jnp.einsum('siac,sjbc->sijab', blocks, blocks, precision=lax.Precision.HI...  8.97 us
  transfers between devices with their start and end apart: 5, of which 4 were waited for; matrix products, arithmetic and copies ran while one was open for 8% of the time, Pallas kernels for 51%

commit v1 on v0

--- a/solution.py
+++ b/solution.py
@@ -93,8 +93,10 @@
         upper[pl.ds(j, 1), :] = u_row
         e_row = elim[pl.ds(j, 1), :]
         inv_ref[pl.ds(j, 1), :] = e_row * scale
-        u_col = jnp.transpose(jnp.broadcast_to(u_row, (8, n)))[:, 0:1]
-        work[...] = work[...] - u_col * u_row
+        whole = work[...]
+        u_col = jnp.sum(jnp.where(cols == j, whole, 0.0), axis=1, keepdims=True) * scale
+        u_col = jnp.where(row_id >= j, u_col, 0.0)
+        work[...] = whole - u_col * u_row
         mult = jnp.where(row_id > j, u_col * scale, 0.0)
         elim[...] = elim[...] - mult * e_row
         return carry

time: 387 us -> 296 us (0.76)
  Pallas kernels: 198 us -> 107 us
    pallas_call x4, Pallas kernels: 157 us -> 65.9 us  [block_chol(): pl.pallas_call(block_chol_kernel, out_shape=(jax.ShapeDtypeStruct((n, n),...]
  transfers between devices with their start and end apart: 5 -> 5, of which waited for: 4 -> 4; matrix products, arithmetic and copies ran while one was open for 8% -> 11% of each run, Pallas kernels for 51% -> 36%
where the time goes in v1:
time: 296 us; the launch traced here: 295 us
  Pallas kernels  107 us (36%)
  waiting for transfers between devices  75.3 us (25%)
  local copies, waits for them, and re-layouts  38.2 us (13%)
  matrix products  33.3 us (11%)
  starting transfers between devices  30.5 us (10%)
  other arithmetic  9.67 us (3%)
    pallas_call x4, Pallas kernels, block_chol(): pl.pallas_call(block_chol_kernel, out_shape=(jax.ShapeDtypeStruct((n, n),...  65.9 us
    pallas_call x2, Pallas kernels, columns_out(): pl.pallas_call(functools.partial(columns_out_kernel, count=count, group=g...  40.7 us
    all_to_all x1, waiting for transfers between devices, local(): lax.all_to_all(send_buffer, 'wide', split_axis=0, concat_axis=0, tiled=True)  38.2 us
    all_to_all x1, waiting for transfers between devices, local(): lax.all_to_all(contribution, 'narrow', split_axis=2, concat_axis=0, tiled...  20.8 us
    all_to_all x1, starting transfers between devices, local(): lax.all_to_all(send_buffer, 'wide', split_axis=0, concat_axis=0, tiled=True)  15.1 us
    all_to_all x1, waiting for transfers between devices, local(): lax.all_to_all(diag_block, 'narrow', split_axis=0, concat_axis=2, tiled=T...  10.5 us
    dot_general x1, matrix products, local(): jnp.einsum('siac,sjbc->sijab', blocks, blocks, precision=lax.Precision.HI...  8.77 us
    dot_general x6, matrix products, mm_t(): return jnp.einsum('sik,sjk->sij', a, b, precision=lax.Precision.HIGHEST)  7.51 us
  transfers between devices with their start and end apart: 5, of which 4 were waited for; matrix products, arithmetic and copies ran while one was open for 11% of the time, Pallas kernels for 36%

profile of v1, /device:TPU:9, one launch (start us, length us, event | category | flops | bytes accessed | tf_op | source)
XLA Modules:
  0.0 294.7 jit_solution(8248594405708779833)
XLA Ops:
  0.7 4.2 %all-to-all-start = ((f32[4,512,128]{2,1,0:T(8,128)}), f32[4,512,128]{2,1,0:T(8,128)S(1)}, u32[]{:S(2)}, u32[]{:S(2)}) async-start(f32[4,512,128]{2,1,0:T(8,128)} %param.10), calls=%async_computation | async-start | bytes 2097152 | tf_op jit(solution)/shard_map/all_to_all | solution.py:177
  4.8 1.8 copy.68
  8.5 10.5 %all-to-all-done = f32[4,512,128]{2,1,0:T(8,128)S(1)} async-done(((f32[4,512,128]{2,1,0:T(8,128)}), f32[4,512,128]{2,1,0:T(8,128)S(1)}, u32[]{:S(2)}, u32[]{:S(2)}) %all-to-all-start) | async-done | bytes 1048608 | tf_op jit(solution)/shard_map/all_to_all | solution.py:177
  19.0 3.6 %all-to-all-start.1 = ((f32[4,1024,128]{1,2,0:T(8,128)}), f32[4,1024,128]{1,2,0:T(8,128)S(1)}, u32[]{:S(2)}, u32[]{:S(2)}) async-start(f32[4,1024,128]{1,2,0:T(8,128)} %copy.68), calls=%async_computation.1 | async-start | bytes 4194304 | tf_op jit(solution)/shard_map/all_to_all | solution.py:178
  24.4 16.5 %shard_map.103 = (f32[128,128]{1,0:T(8,128)}, f32[128,128]{1,0:T(8,128)}) custom-call(f32[128,128]{1,0:T(8,128)} %slice_bitcast_fusion.10.a_ref), custom_call_target="tpu_custom_call" | custom-call | tf_op jit(solution)/shard_map/pallas_call | solution.py:110
  40.9 1.4 fusion.37
  42.4 1.7 fusion.3
  44.7 16.5 %shard_map.104 = (f32[128,128]{1,0:T(8,128)}, f32[128,128]{1,0:T(8,128)}) custom-call(f32[128,128]{1,0:T(8,128)} %slice_bitcast_fusion.9.a_ref), custom_call_target="tpu_custom_call" | custom-call | tf_op jit(solution)/shard_map/pallas_call | solution.py:110
  66.8 1.5 fusion.72
  71.8 16.5 %shard_map.105 = (f32[128,128]{1,0:T(8,128)}, f32[128,128]{1,0:T(8,128)}) custom-call(f32[128,128]{1,0:T(8,128)} %slice_bitcast_fusion.6.a_ref), custom_call_target="tpu_custom_call" | custom-call | tf_op jit(solution)/shard_map/pallas_call | solution.py:110
  88.3 1.4 convolution_bitcast_fusion.3
  90.8 1.5 fusion.4
  93.0 1.7 fusion.9.a_ref
  94.8 16.5 %shard_map.106 = (f32[128,128]{1,0:T(8,128)}, f32[128,128]{1,0:T(8,128)}) custom-call(f32[128,128]{1,0:T(8,128)} %fusion.9.a_ref), custom_call_target="tpu_custom_call" | custom-call | tf_op jit(solution)/shard_map/pallas_call | solution.py:110
  113.9 5.1 %convolution_multiply_fusion = f32[512,1024]{0,1:T(8,128)S(1)} fusion(f32[1024,512]{0,1:T(8,128)} %bitcast.189, f32[1,128,512]{2,1,0:T(8,128)S(1)} %convolution_bitcast_fusion.2, f32[1,128,512]{2,1,0:T(8,128)S(1)} %convolution_bitcast_fusion.3, f32[1,128,512]{2,1,0:T(8,128)S(1)} %convolution_bitcast_fusion.5, f32[1,128,512]{2,1,0:T(8,128)S(1)} %concatenate.47, ...), kind=kOutput, calls=%fused_computation.12 | convolution fusion | flops 3222536192 | bytes 5246976 | tf_op jit(solution)/shard_map/srk,sck->src/dot_general | solution.py:181
  119.1 8.8 %convolution_bitcast_fusion = f32[1,8,8,128,128]{3,4,1,2,0:T(8,128)} fusion(f32[8,128,512,1]{2,1,3,0:T(8,128)S(1)} %bitcast.180, f32[8,128,512,1]{2,1,0,3:T(8,128)S(1)} %bitcast.181), kind=kOutput, calls=%fused_computation.11 | convolution fusion | flops 6442450944 | bytes 8388608 | tf_op jit(solution)/shard_map/siac,sjbc->sijab/dot_general | solution.py:192
  127.9 5.4 %copy.70 = f32[1,8,8,128,128]{4,3,2,1,0:T(8,128)} copy(f32[1,8,8,128,128]{3,4,1,2,0:T(8,128)} %convolution_bitcast_fusion) | data formatting | bytes 8388608 | tf_op jit(solution)/shard_map/siac,sjbc->sijab/transpose | solution.py:192
  133.3 2.9 gather_fusion
  136.2 3.8 %copy.71 = f32[1,36,128,128]{3,0,1,2:T(1,128)} copy(f32[1,36,128,128]{3,2,1,0:T(8,128)S(1)} %bitcast.187) | data formatting | bytes 4718592 | tf_op jit(solution)/shard_map/gather | solution.py:194
  140.0 4.3 %all-to-all-start.2 = ((f32[1,36,128,128]{3,0,1,2:T(1,128)}), f32[1,36,128,128]{3,0,1,2:T(1,128)S(1)}, u32[]{:S(2)}, u32[]{:S(2)}) async-start(f32[1,36,128,128]{3,0,1,2:T(1,128)} %copy.71), calls=%async_computation.2 | async-start | bytes 4718592 | tf_op jit(solution)/shard_map/all_to_all | solution.py:196
  150.3 20.8 %all-to-all-done.2 = f32[1,36,128,128]{3,0,1,2:T(1,128)S(1)} async-done(((f32[1,36,128,128]{3,0,1,2:T(1,128)}), f32[1,36,128,128]{3,0,1,2:T(1,128)S(1)}, u32[]{:S(2)}, u32[]{:S(2)}) %all-to-all-start.2) | async-done | bytes 2359328 | tf_op jit(solution)/shard_map/all_to_all | solution.py:196
  171.7 2.5 gather_fusion.1
  174.2 3.2 %bitcast_select_fusion = f32[64,96,128]{2,1,0:T(8,128)S(1)} fusion(pred[64,96]{1,0:T(8,128)(4,1)S(1)} %copy.64, f32[64,96,128]{2,1,0:T(8,128)} %bitcast.185), kind=kLoop, calls=%fused_computation.9 | loop fusion | flops 786432 | bytes 6297600 | tf_op jit(solution)/shard_map/jit(_where)/select_n | solution.py:218
  177.4 2.0 select_maximum_fusion
  179.4 15.1 %all-to-all-start.3 = ((f32[64,104,128]{2,1,0:T(8,128)}), f32[64,104,128]{2,1,0:T(8,128)S(1)}, u32[]{:S(2)}, u32[]{:S(2)}) async-start(f32[64,104,128]{2,1,0:T(8,128)} %select_maximum_fusion), calls=%async_computation.3 | async-start | bytes 6815744 | tf_op jit(solution)/shard_map/all_to_all | solution.py:225
  194.5 26.4 %shard_map.108 = f32[4,1024,128]{2,1,0:T(8,128)} custom-call(f32[1,1024,512]{2,1,0:T(8,128)} %bitcast.182), custom_call_target="tpu_custom_call" | custom-call | bytes 4194304 | tf_op jit(solution)/shard_map/pallas_call | solution.py:63
  220.9 14.3 %shard_map.107 = f32[4,512,128]{2,1,0:T(8,128)} custom-call(f32[1,512,512]{2,1,0:T(8,128)} %select_maximum_fusion.1.x_ref), custom_call_target="tpu_custom_call" | custom-call | bytes 2097152 | tf_op jit(solution)/shard_map/pallas_call | solution.py:63
  235.2 38.2 %all-to-all-done.3 = f32[64,104,128]{2,1,0:T(8,128)S(1)} async-done(((f32[64,104,128]{2,1,0:T(8,128)}), f32[64,104,128]{2,1,0:T(8,128)S(1)}, u32[]{:S(2)}, u32[]{:S(2)}) %all-to-all-start.3) | async-done | bytes 3407904 | tf_op jit(solution)/shard_map/all_to_all | solution.py:225
  273.4 2.0 slice.118
  277.2 4.8 %fusion = f32[4,2,32,128]{3,0,2,1:T(4,128)S(1)} fusion(f32[192,32,128]{2,1,0:T(8,128)} %bitcast.184, s32[4,2]{0,1:T(2,128)S(1)} %multiply_add_fusion, s32[192]{0:T(256)S(1)} %convert_element_type.46), kind=kOutput, calls=%fused_computation.7 | convolution fusion | flops 75499008 | bytes 3277600 | tf_op jit(solution)/shard_map/ri,rab->iab/dot_general | solution.py:235
  282.6 3.3 %all-to-all-start.4 = ((f32[4,2,32,128]{3,2,1,0:T(8,128)}), f32[4,2,32,128]{3,2,1,0:T(8,128)S(1)}, u32[]{:S(2)}, u32[]{:S(2)}) async-start(f32[4,2,32,128]{3,2,1,0:T(8,128)} %copy.76), calls=%async_computation.4 | async-start | bytes 262144 | tf_op jit(solution)/shard_map/all_to_all | solution.py:237
  285.9 5.7 %all-to-all-done.4 = f32[4,2,32,128]{3,2,1,0:T(8,128)S(1)} async-done(((f32[4,2,32,128]{3,2,1,0:T(8,128)}), f32[4,2,32,128]{3,2,1,0:T(8,128)S(1)}, u32[]{:S(2)}, u32[]{:S(2)}) %all-to-all-start.4) | async-done | bytes 131104 | tf_op jit(solution)/shard_map/all_to_all | solution.py:237
  (95 shorter events, 29.6 us)
Async XLA Ops:
  0.6 7.2 %copy-start.16 = (s32[36]{0:T(128)S(1)}, s32[36]{0:T(128)}, u32[]{:S(2)}) copy-start(s32[36]{0:T(128)} %constant.104) | copy-start | bytes 436
  0.6 4.2 %copy-start.5 = (f32[4,1024,128]{2,1,0:T(8,128)S(1)}, f32[4,1024,128]{2,1,0:T(8,128)}, u32[]{:S(2)}) copy-start(f32[4,1024,128]{2,1,0:T(8,128)} %param.11) | copy-start | bytes 6291460
  0.7 6.0 %copy-start.17 = (s32[4]{0:T(128)S(1)}, s32[4]{0:T(128)}, u32[]{:S(2)}) copy-start(s32[4]{0:T(128)} %param.12) | copy-start | bytes 52
  0.7 18.3 %all-to-all-start = ((f32[4,512,128]{2,1,0:T(8,128)}), f32[4,512,128]{2,1,0:T(8,128)S(1)}, u32[]{:S(2)}, u32[]{:S(2)}) async-start(f32[4,512,128]{2,1,0:T(8,128)} %param.10), calls=%async_computation | async-start | bytes 2097152 | tf_op jit(solution)/shard_map/all_to_all | solution.py:177
  19.0 93.6 %all-to-all-start.1 = ((f32[4,1024,128]{1,2,0:T(8,128)}), f32[4,1024,128]{1,2,0:T(8,128)S(1)}, u32[]{:S(2)}, u32[]{:S(2)}) async-start(f32[4,1024,128]{1,2,0:T(8,128)} %copy.68), calls=%async_computation.1 | async-start | bytes 4194304 | tf_op jit(solution)/shard_map/all_to_all | solution.py:178
  22.8 1.0 copy-start.4
  40.9 24.6 %copy-start.8 = (f32[128,128]{1,0:T(8,128)S(1)}, f32[128,128]{1,0:T(8,128)}, u32[]{:S(2)}) copy-start(f32[128,128]{1,0:T(8,128)} %get-tuple-element.29) | copy-start | bytes 196612
  70.5 0.7 copy-start.7
  112.6 1.3 copy-start.1
  119.1 8.8 %copy-start = (f32[512,1024]{0,1:T(8,128)}, f32[512,1024]{0,1:T(8,128)S(1)}, u32[]{:S(2)}) copy-start(f32[512,1024]{0,1:T(8,128)S(1)} %convolution_multiply_fusion) | copy-start | bytes 6291460
  140.0 4.4 %copy-start.14 = (s32[144,1]{0,1:T(1,128)S(1)}, s32[144,1]{0,1:T(1,128)}, u32[]{:S(2)}) copy-start(s32[144,1]{0,1:T(1,128)} %param.13) | copy-start | bytes 1732
  140.0 7.9 %copy-start.15 = (s32[144]{0:T(256)S(1)}, s32[144]{0:T(256)}, u32[]{:S(2)}) copy-start(s32[144]{0:T(256)} %param.14) | copy-start | bytes 1732
  140.0 9.2 %copy-start.6 = (f32[256,128]{1,0:T(8,128)S(1)}, f32[256,128]{1,0:T(8,128)}, u32[]{:S(2)}) copy-start(f32[256,128]{1,0:T(8,128)} %copy.67) | copy-start | bytes 393220
  140.0 9.2 %copy-start.10 = (f32[128,128]{1,0:T(8,128)S(1)}, f32[128,128]{1,0:T(8,128)}, u32[]{:S(2)}) copy-start(f32[128,128]{1,0:T(8,128)} %get-tuple-element.33) | copy-start | bytes 196612
  140.0 9.2 %copy-start.11 = (f32[128,128]{1,0:T(8,128)S(1)}, f32[128,128]{1,0:T(8,128)}, u32[]{:S(2)}) copy-start(f32[128,128]{1,0:T(8,128)} %get-tuple-element.34) | copy-start | bytes 196612
  140.0 9.2 %copy-start.12 = (f32[128,128]{1,0:T(8,128)S(1)}, f32[128,128]{1,0:T(8,128)}, u32[]{:S(2)}) copy-start(f32[128,128]{1,0:T(8,128)} %get-tuple-element.35) | copy-start | bytes 196612
  140.0 9.2 %copy-start.13 = (f32[128,128]{1,0:T(8,128)S(1)}, f32[128,128]{1,0:T(8,128)}, u32[]{:S(2)}) copy-start(f32[128,128]{1,0:T(8,128)} %get-tuple-element.36) | copy-start | bytes 196612
  140.0 31.1 %all-to-all-start.2 = ((f32[1,36,128,128]{3,0,1,2:T(1,128)}), f32[1,36,128,128]{3,0,1,2:T(1,128)S(1)}, u32[]{:S(2)}, u32[]{:S(2)}) async-start(f32[1,36,128,128]{3,0,1,2:T(1,128)} %copy.71), calls=%async_computation.2 | async-start | bytes 4718592 | tf_op jit(solution)/shard_map/all_to_all | solution.py:196
  179.4 94.1 %all-to-all-start.3 = ((f32[64,104,128]{2,1,0:T(8,128)}), f32[64,104,128]{2,1,0:T(8,128)S(1)}, u32[]{:S(2)}, u32[]{:S(2)}) async-start(f32[64,104,128]{2,1,0:T(8,128)} %select_maximum_fusion), calls=%async_computation.3 | async-start | bytes 6815744 | tf_op jit(solution)/shard_map/all_to_all | solution.py:225
  275.5 16.2 %copy-start.9 = (f32[2,128,128]{2,1,0:T(8,128)S(1)}, f32[2,128,128]{2,1,0:T(8,128)}, u32[]{:S(2)}) copy-start(f32[2,128,128]{2,1,0:T(8,128)} %param.15) | copy-start | bytes 393220
  276.2 16.2 %copy-start.3 = (f32[4,512,128]{2,1,0:T(8,128)S(1)}, f32[4,512,128]{2,1,0:T(8,128)}, u32[]{:S(2)}) copy-start(f32[4,512,128]{2,1,0:T(8,128)} %shard_map.107) | copy-start | bytes 3145732
  277.2 16.2 %copy-start.2 = (f32[4,1024,128]{2,1,0:T(8,128)S(1)}, f32[4,1024,128]{2,1,0:T(8,128)}, u32[]{:S(2)}) copy-start(f32[4,1024,128]{2,1,0:T(8,128)} %shard_map.108) | copy-start | bytes 6291460
  282.6 9.1 %all-to-all-start.4 = ((f32[4,2,32,128]{3,2,1,0:T(8,128)}), f32[4,2,32,128]{3,2,1,0:T(8,128)S(1)}, u32[]{:S(2)}, u32[]{:S(2)}) async-start(f32[4,2,32,128]{3,2,1,0:T(8,128)} %copy.76), calls=%async_computation.4 | async-start | bytes 262144 | tf_op jit(solution)/shard_map/all_to_all | solution.py:237

commit v2 on v0

--- a/solution.py
+++ b/solution.py
@@ -77,29 +77,36 @@
 
 def block_chol_kernel(a_ref, l_ref, inv_ref, work, upper, elim):
     n = a_ref.shape[0]
+    phase = 32
     work[...] = a_ref[...]
     rows = lax.broadcasted_iota(jnp.int32, (n, n), 0)
     cols = lax.broadcasted_iota(jnp.int32, (n, n), 1)
     elim[...] = (rows == cols).astype(jnp.float32)
     lane = lax.broadcasted_iota(jnp.int32, (1, n), 1)
-    row_id = lax.broadcasted_iota(jnp.int32, (n, 1), 0)
-
-    def step(j, carry):
-        r = work[pl.ds(j, 1), :]
-        piv = jnp.sum(jnp.where(lane == j, r, 0.0), axis=1, keepdims=True)
-        root = jnp.sqrt(piv)
-        scale = 1.0 / root
-        u_row = jnp.where(lane >= j, r * scale, 0.0)
-        upper[pl.ds(j, 1), :] = u_row
-        e_row = elim[pl.ds(j, 1), :]
-        inv_ref[pl.ds(j, 1), :] = e_row * scale
-        u_col = jnp.transpose(jnp.broadcast_to(u_row, (8, n)))[:, 0:1]
-        work[...] = work[...] - u_col * u_row
-        mult = jnp.where(row_id > j, u_col * scale, 0.0)
-        elim[...] = elim[...] - mult * e_row
-        return carry
-
-    lax.fori_loop(0, n, step, 0)
+
+    for top in range(0, n, phase):
+        height = n - top
+        tail_cols = lax.broadcasted_iota(jnp.int32, (height, n), 1)
+        tail_rows = top + lax.broadcasted_iota(jnp.int32, (height, 1), 0)
+
+        def step(j, carry, top=top, height=height, tail_cols=tail_cols, tail_rows=tail_rows):
+            r = work[pl.ds(j, 1), :]
+            piv = jnp.sum(jnp.where(lane == j, r, 0.0), axis=1, keepdims=True)
+            root = jnp.sqrt(piv)
+            scale = 1.0 / root
+            u_row = jnp.where(lane >= j, r * scale, 0.0)
+            upper[pl.ds(j, 1), :] = u_row
+            e_row = elim[pl.ds(j, 1), :]
+            inv_ref[pl.ds(j, 1), :] = e_row * scale
+            whole = work[top:, :]
+            u_col = jnp.sum(jnp.where(tail_cols == j, whole, 0.0), axis=1, keepdims=True) * scale
+            u_col = jnp.where(tail_rows >= j, u_col, 0.0)
+            work[top:, :] = whole - u_col * u_row
+            mult = jnp.where(tail_rows > j, u_col * scale, 0.0)
+            elim[top:, :] = elim[top:, :] - mult * e_row
+            return carry
+
+        lax.fori_loop(top, top + phase, step, 0)
     l_ref[...] = jnp.transpose(upper[...])
 
 

time: 387 us -> 292 us (0.75)
  Pallas kernels: 198 us -> 103 us
    pallas_call x4, Pallas kernels: 157 us -> 61.9 us  [block_chol(): pl.pallas_call(block_chol_kernel, out_shape=(jax.ShapeDtypeStruct((n, n),...]
  transfers between devices with their start and end apart: 5 -> 5, of which waited for: 4 -> 4; matrix products, arithmetic and copies ran while one was open for 8% -> 11% of each run, Pallas kernels for 51% -> 35%
where the time goes in v2:
time: 292 us; the launch traced here: 291 us
  Pallas kernels  103 us (35%)
  waiting for transfers between devices  75.2 us (26%)
  local copies, waits for them, and re-layouts  38.2 us (13%)
  matrix products  33.4 us (11%)
  starting transfers between devices  30.6 us (10%)
  other arithmetic  9.67 us (3%)
    pallas_call x4, Pallas kernels, block_chol(): pl.pallas_call(block_chol_kernel, out_shape=(jax.ShapeDtypeStruct((n, n),...  61.9 us
    pallas_call x2, Pallas kernels, columns_out(): pl.pallas_call(functools.partial(columns_out_kernel, count=count, group=g...  40.7 us
    all_to_all x1, waiting for transfers between devices, local(): lax.all_to_all(send_buffer, 'wide', split_axis=0, concat_axis=0, tiled=True)  38.2 us
    all_to_all x1, waiting for transfers between devices, local(): lax.all_to_all(contribution, 'narrow', split_axis=2, concat_axis=0, tiled...  20.8 us
    all_to_all x1, starting transfers between devices, local(): lax.all_to_all(send_buffer, 'wide', split_axis=0, concat_axis=0, tiled=True)  15.1 us
    all_to_all x1, waiting for transfers between devices, local(): lax.all_to_all(diag_block, 'narrow', split_axis=0, concat_axis=2, tiled=T...  10.5 us
    dot_general x1, matrix products, local(): jnp.einsum('siac,sjbc->sijab', blocks, blocks, precision=lax.Precision.HI...  8.96 us
    dot_general x6, matrix products, mm_t(): return jnp.einsum('sik,sjk->sij', a, b, precision=lax.Precision.HIGHEST)  7.5 us
  transfers between devices with their start and end apart: 5, of which 4 were waited for; matrix products, arithmetic and copies ran while one was open for 11% of the time, Pallas kernels for 35%

profile of v2, /device:TPU:9, one launch (start us, length us, event | category | flops | bytes accessed | tf_op | source)
XLA Modules:
  0.0 290.9 jit_solution(15087340278076754965)
XLA Ops:
  0.7 4.2 %all-to-all-start = ((f32[4,512,128]{2,1,0:T(8,128)}), f32[4,512,128]{2,1,0:T(8,128)S(1)}, u32[]{:S(2)}, u32[]{:S(2)}) async-start(f32[4,512,128]{2,1,0:T(8,128)} %param.10), calls=%async_computation | async-start | bytes 2097152 | tf_op jit(solution)/shard_map/all_to_all | solution.py:182
  4.8 1.8 copy.68
  8.5 10.5 %all-to-all-done = f32[4,512,128]{2,1,0:T(8,128)S(1)} async-done(((f32[4,512,128]{2,1,0:T(8,128)}), f32[4,512,128]{2,1,0:T(8,128)S(1)}, u32[]{:S(2)}, u32[]{:S(2)}) %all-to-all-start) | async-done | bytes 1048608 | tf_op jit(solution)/shard_map/all_to_all | solution.py:182
  19.0 3.6 %all-to-all-start.1 = ((f32[4,1024,128]{1,2,0:T(8,128)}), f32[4,1024,128]{1,2,0:T(8,128)S(1)}, u32[]{:S(2)}, u32[]{:S(2)}) async-start(f32[4,1024,128]{1,2,0:T(8,128)} %copy.68), calls=%async_computation.1 | async-start | bytes 4194304 | tf_op jit(solution)/shard_map/all_to_all | solution.py:183
  24.4 15.5 %shard_map.103 = (f32[128,128]{1,0:T(8,128)}, f32[128,128]{1,0:T(8,128)}) custom-call(f32[128,128]{1,0:T(8,128)} %slice_bitcast_fusion.10.a_ref), custom_call_target="tpu_custom_call" | custom-call | tf_op jit(solution)/shard_map/pallas_call | solution.py:115
  41.4 1.7 fusion.3
  43.7 15.5 %shard_map.104 = (f32[128,128]{1,0:T(8,128)}, f32[128,128]{1,0:T(8,128)}) custom-call(f32[128,128]{1,0:T(8,128)} %slice_bitcast_fusion.9.a_ref), custom_call_target="tpu_custom_call" | custom-call | tf_op jit(solution)/shard_map/pallas_call | solution.py:115
  64.8 1.5 fusion.72
  69.8 15.5 %shard_map.105 = (f32[128,128]{1,0:T(8,128)}, f32[128,128]{1,0:T(8,128)}) custom-call(f32[128,128]{1,0:T(8,128)} %slice_bitcast_fusion.6.a_ref), custom_call_target="tpu_custom_call" | custom-call | tf_op jit(solution)/shard_map/pallas_call | solution.py:115
  85.3 1.4 convolution_bitcast_fusion.3
  87.8 1.5 fusion.4
  90.0 1.7 fusion.9.a_ref
  91.8 15.5 %shard_map.106 = (f32[128,128]{1,0:T(8,128)}, f32[128,128]{1,0:T(8,128)}) custom-call(f32[128,128]{1,0:T(8,128)} %fusion.9.a_ref), custom_call_target="tpu_custom_call" | custom-call | tf_op jit(solution)/shard_map/pallas_call | solution.py:115
  107.3 1.4 convolution_bitcast_fusion.2
  110.0 5.1 %convolution_multiply_fusion = f32[512,1024]{0,1:T(8,128)S(1)} fusion(f32[1024,512]{0,1:T(8,128)} %bitcast.189, f32[1,128,512]{2,1,0:T(8,128)S(1)} %convolution_bitcast_fusion.2, f32[1,128,512]{2,1,0:T(8,128)S(1)} %convolution_bitcast_fusion.3, f32[1,128,512]{2,1,0:T(8,128)S(1)} %convolution_bitcast_fusion.5, f32[1,128,512]{2,1,0:T(8,128)S(1)} %concatenate.47, ...), kind=kOutput, calls=%fused_computation.12 | convolution fusion | flops 3222536192 | bytes 5246976 | tf_op jit(solution)/shard_map/srk,sck->src/dot_general | solution.py:186
  115.1 9.0 %convolution_bitcast_fusion = f32[1,8,8,128,128]{3,4,1,2,0:T(8,128)} fusion(f32[8,128,512,1]{2,1,3,0:T(8,128)S(1)} %bitcast.180, f32[8,128,512,1]{2,1,0,3:T(8,128)S(1)} %bitcast.181), kind=kOutput, calls=%fused_computation.11 | convolution fusion | flops 6442450944 | bytes 8388608 | tf_op jit(solution)/shard_map/siac,sjbc->sijab/dot_general | solution.py:197
  124.1 5.4 %copy.70 = f32[1,8,8,128,128]{4,3,2,1,0:T(8,128)} copy(f32[1,8,8,128,128]{3,4,1,2,0:T(8,128)} %convolution_bitcast_fusion) | data formatting | bytes 8388608 | tf_op jit(solution)/shard_map/siac,sjbc->sijab/transpose | solution.py:197
  129.5 2.9 gather_fusion
  132.4 3.8 %copy.71 = f32[1,36,128,128]{3,0,1,2:T(1,128)} copy(f32[1,36,128,128]{3,2,1,0:T(8,128)S(1)} %bitcast.187) | data formatting | bytes 4718592 | tf_op jit(solution)/shard_map/gather | solution.py:199
  136.3 4.3 %all-to-all-start.2 = ((f32[1,36,128,128]{3,0,1,2:T(1,128)}), f32[1,36,128,128]{3,0,1,2:T(1,128)S(1)}, u32[]{:S(2)}, u32[]{:S(2)}) async-start(f32[1,36,128,128]{3,0,1,2:T(1,128)} %copy.71), calls=%async_computation.2 | async-start | bytes 4718592 | tf_op jit(solution)/shard_map/all_to_all | solution.py:201
  146.5 20.8 %all-to-all-done.2 = f32[1,36,128,128]{3,0,1,2:T(1,128)S(1)} async-done(((f32[1,36,128,128]{3,0,1,2:T(1,128)}), f32[1,36,128,128]{3,0,1,2:T(1,128)S(1)}, u32[]{:S(2)}, u32[]{:S(2)}) %all-to-all-start.2) | async-done | bytes 2359328 | tf_op jit(solution)/shard_map/all_to_all | solution.py:201
  167.9 2.5 gather_fusion.1
  170.5 3.2 %bitcast_select_fusion = f32[64,96,128]{2,1,0:T(8,128)S(1)} fusion(pred[64,96]{1,0:T(8,128)(4,1)S(1)} %copy.64, f32[64,96,128]{2,1,0:T(8,128)} %bitcast.185), kind=kLoop, calls=%fused_computation.9 | loop fusion | flops 786432 | bytes 6297600 | tf_op jit(solution)/shard_map/jit(_where)/select_n | solution.py:223
  173.6 2.0 select_maximum_fusion
  175.6 15.1 %all-to-all-start.3 = ((f32[64,104,128]{2,1,0:T(8,128)}), f32[64,104,128]{2,1,0:T(8,128)S(1)}, u32[]{:S(2)}, u32[]{:S(2)}) async-start(f32[64,104,128]{2,1,0:T(8,128)} %select_maximum_fusion), calls=%async_computation.3 | async-start | bytes 6815744 | tf_op jit(solution)/shard_map/all_to_all | solution.py:230
  190.7 26.4 %shard_map.108 = f32[4,1024,128]{2,1,0:T(8,128)} custom-call(f32[1,1024,512]{2,1,0:T(8,128)} %bitcast.182), custom_call_target="tpu_custom_call" | custom-call | bytes 4194304 | tf_op jit(solution)/shard_map/pallas_call | solution.py:63
  217.2 14.3 %shard_map.107 = f32[4,512,128]{2,1,0:T(8,128)} custom-call(f32[1,512,512]{2,1,0:T(8,128)} %select_maximum_fusion.1.x_ref), custom_call_target="tpu_custom_call" | custom-call | bytes 2097152 | tf_op jit(solution)/shard_map/pallas_call | solution.py:63
  231.4 38.2 %all-to-all-done.3 = f32[64,104,128]{2,1,0:T(8,128)S(1)} async-done(((f32[64,104,128]{2,1,0:T(8,128)}), f32[64,104,128]{2,1,0:T(8,128)S(1)}, u32[]{:S(2)}, u32[]{:S(2)}) %all-to-all-start.3) | async-done | bytes 3407904 | tf_op jit(solution)/shard_map/all_to_all | solution.py:230
  269.7 2.0 slice.118
  273.4 4.8 %fusion = f32[4,2,32,128]{3,0,2,1:T(4,128)S(1)} fusion(f32[192,32,128]{2,1,0:T(8,128)} %bitcast.184, s32[4,2]{0,1:T(2,128)S(1)} %multiply_add_fusion, s32[192]{0:T(256)S(1)} %convert_element_type.46), kind=kOutput, calls=%fused_computation.7 | convolution fusion | flops 75499008 | bytes 3277600 | tf_op jit(solution)/shard_map/ri,rab->iab/dot_general | solution.py:240
  278.8 3.3 %all-to-all-start.4 = ((f32[4,2,32,128]{3,2,1,0:T(8,128)}), f32[4,2,32,128]{3,2,1,0:T(8,128)S(1)}, u32[]{:S(2)}, u32[]{:S(2)}) async-start(f32[4,2,32,128]{3,2,1,0:T(8,128)} %copy.76), calls=%async_computation.4 | async-start | bytes 262144 | tf_op jit(solution)/shard_map/all_to_all | solution.py:242
  282.2 5.7 %all-to-all-done.4 = f32[4,2,32,128]{3,2,1,0:T(8,128)S(1)} async-done(((f32[4,2,32,128]{3,2,1,0:T(8,128)}), f32[4,2,32,128]{3,2,1,0:T(8,128)S(1)}, u32[]{:S(2)}, u32[]{:S(2)}) %all-to-all-start.4) | async-done | bytes 131104 | tf_op jit(solution)/shard_map/all_to_all | solution.py:242
  (95 shorter events, 29.6 us)
Async XLA Ops:
  0.6 7.2 %copy-start.16 = (s32[36]{0:T(128)S(1)}, s32[36]{0:T(128)}, u32[]{:S(2)}) copy-start(s32[36]{0:T(128)} %constant.104) | copy-start | bytes 436
  0.6 4.2 %copy-start.5 = (f32[4,1024,128]{2,1,0:T(8,128)S(1)}, f32[4,1024,128]{2,1,0:T(8,128)}, u32[]{:S(2)}) copy-start(f32[4,1024,128]{2,1,0:T(8,128)} %param.11) | copy-start | bytes 6291460
  0.7 6.0 %copy-start.17 = (s32[4]{0:T(128)S(1)}, s32[4]{0:T(128)}, u32[]{:S(2)}) copy-start(s32[4]{0:T(128)} %param.12) | copy-start | bytes 52
  0.7 18.3 %all-to-all-start = ((f32[4,512,128]{2,1,0:T(8,128)}), f32[4,512,128]{2,1,0:T(8,128)S(1)}, u32[]{:S(2)}, u32[]{:S(2)}) async-start(f32[4,512,128]{2,1,0:T(8,128)} %param.10), calls=%async_computation | async-start | bytes 2097152 | tf_op jit(solution)/shard_map/all_to_all | solution.py:182
  19.0 89.6 %all-to-all-start.1 = ((f32[4,1024,128]{1,2,0:T(8,128)}), f32[4,1024,128]{1,2,0:T(8,128)S(1)}, u32[]{:S(2)}, u32[]{:S(2)}) async-start(f32[4,1024,128]{1,2,0:T(8,128)} %copy.68), calls=%async_computation.1 | async-start | bytes 4194304 | tf_op jit(solution)/shard_map/all_to_all | solution.py:183
  22.8 1.0 copy-start.4
  39.9 23.6 %copy-start.8 = (f32[128,128]{1,0:T(8,128)S(1)}, f32[128,128]{1,0:T(8,128)}, u32[]{:S(2)}) copy-start(f32[128,128]{1,0:T(8,128)} %get-tuple-element.29) | copy-start | bytes 196612
  68.5 0.7 copy-start.7
  108.7 1.3 copy-start.1
  115.1 9.0 %copy-start = (f32[512,1024]{0,1:T(8,128)}, f32[512,1024]{0,1:T(8,128)S(1)}, u32[]{:S(2)}) copy-start(f32[512,1024]{0,1:T(8,128)S(1)} %convolution_multiply_fusion) | copy-start | bytes 6291460
  136.2 4.4 %copy-start.14 = (s32[144,1]{0,1:T(1,128)S(1)}, s32[144,1]{0,1:T(1,128)}, u32[]{:S(2)}) copy-start(s32[144,1]{0,1:T(1,128)} %param.13) | copy-start | bytes 1732
  136.2 7.9 %copy-start.15 = (s32[144]{0:T(256)S(1)}, s32[144]{0:T(256)}, u32[]{:S(2)}) copy-start(s32[144]{0:T(256)} %param.14) | copy-start | bytes 1732
  136.2 9.2 %copy-start.6 = (f32[256,128]{1,0:T(8,128)S(1)}, f32[256,128]{1,0:T(8,128)}, u32[]{:S(2)}) copy-start(f32[256,128]{1,0:T(8,128)} %copy.67) | copy-start | bytes 393220
  136.2 9.2 %copy-start.10 = (f32[128,128]{1,0:T(8,128)S(1)}, f32[128,128]{1,0:T(8,128)}, u32[]{:S(2)}) copy-start(f32[128,128]{1,0:T(8,128)} %get-tuple-element.33) | copy-start | bytes 196612
  136.2 9.2 %copy-start.11 = (f32[128,128]{1,0:T(8,128)S(1)}, f32[128,128]{1,0:T(8,128)}, u32[]{:S(2)}) copy-start(f32[128,128]{1,0:T(8,128)} %get-tuple-element.34) | copy-start | bytes 196612
  136.3 9.2 %copy-start.12 = (f32[128,128]{1,0:T(8,128)S(1)}, f32[128,128]{1,0:T(8,128)}, u32[]{:S(2)}) copy-start(f32[128,128]{1,0:T(8,128)} %get-tuple-element.35) | copy-start | bytes 196612
  136.3 9.2 %copy-start.13 = (f32[128,128]{1,0:T(8,128)S(1)}, f32[128,128]{1,0:T(8,128)}, u32[]{:S(2)}) copy-start(f32[128,128]{1,0:T(8,128)} %get-tuple-element.36) | copy-start | bytes 196612
  136.3 31.1 %all-to-all-start.2 = ((f32[1,36,128,128]{3,0,1,2:T(1,128)}), f32[1,36,128,128]{3,0,1,2:T(1,128)S(1)}, u32[]{:S(2)}, u32[]{:S(2)}) async-start(f32[1,36,128,128]{3,0,1,2:T(1,128)} %copy.71), calls=%async_computation.2 | async-start | bytes 4718592 | tf_op jit(solution)/shard_map/all_to_all | solution.py:201
  175.6 94.1 %all-to-all-start.3 = ((f32[64,104,128]{2,1,0:T(8,128)}), f32[64,104,128]{2,1,0:T(8,128)S(1)}, u32[]{:S(2)}, u32[]{:S(2)}) async-start(f32[64,104,128]{2,1,0:T(8,128)} %select_maximum_fusion), calls=%async_computation.3 | async-start | bytes 6815744 | tf_op jit(solution)/shard_map/all_to_all | solution.py:230
  271.7 16.2 %copy-start.9 = (f32[2,128,128]{2,1,0:T(8,128)S(1)}, f32[2,128,128]{2,1,0:T(8,128)}, u32[]{:S(2)}) copy-start(f32[2,128,128]{2,1,0:T(8,128)} %param.15) | copy-start | bytes 393220
  272.4 16.2 %copy-start.3 = (f32[4,512,128]{2,1,0:T(8,128)S(1)}, f32[4,512,128]{2,1,0:T(8,128)}, u32[]{:S(2)}) copy-start(f32[4,512,128]{2,1,0:T(8,128)} %shard_map.107) | copy-start | bytes 3145732
  273.4 16.2 %copy-start.2 = (f32[4,1024,128]{2,1,0:T(8,128)S(1)}, f32[4,1024,128]{2,1,0:T(8,128)}, u32[]{:S(2)}) copy-start(f32[4,1024,128]{2,1,0:T(8,128)} %shard_map.108) | copy-start | bytes 6291460
  278.8 9.1 %all-to-all-start.4 = ((f32[4,2,32,128]{3,2,1,0:T(8,128)}), f32[4,2,32,128]{3,2,1,0:T(8,128)S(1)}, u32[]{:S(2)}, u32[]{:S(2)}) async-start(f32[4,2,32,128]{3,2,1,0:T(8,128)} %copy.76), calls=%async_computation.4 | async-start | bytes 262144 | tf_op jit(solution)/shard_map/all_to_all | solution.py:242

commit v3 on v2

--- a/solution.py
+++ b/solution.py
@@ -194,11 +194,17 @@
     first, second = pair_lists(P_SIZE)
     npair = len(first)
     blocks = lower_panel.reshape(group, P_SIZE, B, W)
-    gram = jnp.einsum("siac,sjbc->sijab", blocks, blocks, precision=lax.Precision.HIGHEST)
-    gram = gram.reshape(group, P_SIZE * P_SIZE, B, B)
-    contribution = gram[:, first * P_SIZE + second]
-
-    quarters = lax.all_to_all(contribution, "narrow", split_axis=2, concat_axis=0, tiled=True)
+    split = int(np.searchsorted(first, 5))
+    pieces = []
+    for lo, hi in ((0, split), (split, npair)):
+        part = jnp.einsum(
+            "spac,spbc->spab",
+            blocks[:, first[lo:hi]],
+            blocks[:, second[lo:hi]],
+            precision=lax.Precision.HIGHEST,
+        )
+        pieces.append(lax.all_to_all(part, "narrow", split_axis=2, concat_axis=0, tiled=True))
+    quarters = jnp.concatenate(pieces, axis=1)
     quarter_rows = quarters.shape[2]
     pair_rows = supers_here * npair
     quarters = quarters.reshape(pair_rows, quarter_rows, B)

time: 292 us -> 297 us (1.017)
  waiting for transfers between devices: 75.2 us -> 60.4 us
  matrix products: 33.4 us -> 40.7 us
  local copies, waits for them, and re-layouts: 38.2 us -> 43.6 us
  starting transfers between devices: 30.6 us -> 35.2 us
    all_to_all x1 -> x2, waiting for transfers between devices: 20.8 us -> 8.81 us  [local(): lax.all_to_all(part, 'narrow', split_axis=2, concat_axis=0, tiled=True)]
    dot_general x1 -> x2, matrix products: 8.96 us -> 16.4 us  [local(): jnp.einsum('spac,spbc->spab', blocks[:, first[lo:hi]], blocks[:, second[l...]
    transpose x1 -> x0, local copies, waits for them, and re-layouts: 5.39 us -> none  [local(): jnp.einsum('siac,sjbc->sijab', blocks, blocks, precision=lax.Precision.HI...]
    gather x2 -> x4, local copies, waits for them, and re-layouts: 6.73 us -> 12 us  [the longest x2 6.04 us: local(): blocks[:, second[lo:hi]]]
    dot_general x0 -> x2, local copies, waits for them, and re-layouts: none -> 4.46 us  [local(): jnp.einsum('spac,spbc->spab', blocks[:, first[lo:hi]], blocks[:, second[l...]
    all_to_all x1 -> x2, starting transfers between devices: 4.35 us -> 8.43 us  [local(): lax.all_to_all(part, 'narrow', split_axis=2, concat_axis=0, tiled=True)]
    unnamed x39 -> x53, local copies, waits for them, and re-layouts: 7.14 us -> 7.18 us
  transfers between devices with their start and end apart: 5 -> 6, of which waited for: 4 -> 4; matrix products, arithmetic and copies ran while one was open for 11% -> 18% of each run, Pallas kernels for 35% -> 35%
where the time goes in v3:
time: 297 us; the launch traced here: 296 us
  Pallas kernels  103 us (35%)
  waiting for transfers between devices  60.4 us (20%)
  local copies, waits for them, and re-layouts  43.6 us (15%)
  matrix products  40.7 us (14%)
  starting transfers between devices  35.2 us (12%)
  other arithmetic  11.9 us (4%)
    pallas_call x4, Pallas kernels, block_chol(): pl.pallas_call(block_chol_kernel, out_shape=(jax.ShapeDtypeStruct((n, n),...  62.1 us
    pallas_call x2, Pallas kernels, columns_out(): pl.pallas_call(functools.partial(columns_out_kernel, count=count, group=g...  40.7 us
    all_to_all x1, waiting for transfers between devices, local(): lax.all_to_all(send_buffer, 'wide', split_axis=0, concat_axis=0, tiled=True)  38.2 us
    dot_general x2, matrix products, local(): jnp.einsum('spac,spbc->spab', blocks[:, first[lo:hi]], blocks[:, second[l...  16.4 us
    all_to_all x1, starting transfers between devices, local(): lax.all_to_all(send_buffer, 'wide', split_axis=0, concat_axis=0, tiled=True)  15.7 us
    all_to_all x2, waiting for transfers between devices, local(): lax.all_to_all(part, 'narrow', split_axis=2, concat_axis=0, tiled=True)  8.81 us
    all_to_all x2, starting transfers between devices, local(): lax.all_to_all(part, 'narrow', split_axis=2, concat_axis=0, tiled=True)  8.43 us
    all_to_all x1, waiting for transfers between devices, local(): lax.all_to_all(diag_block, 'narrow', split_axis=0, concat_axis=2, tiled=T...  7.64 us
  transfers between devices with their start and end apart: 6, of which 4 were waited for; matrix products, arithmetic and copies ran while one was open for 18% of the time, Pallas kernels for 35%

profile of v3, /device:TPU:9, one launch (start us, length us, event | category | flops | bytes accessed | tf_op | source)
XLA Modules:
  0.0 295.8 jit_solution(12185818124920467880)
XLA Ops:
  0.7 4.2 %all-to-all-start = ((f32[4,512,128]{2,1,0:T(8,128)}), f32[4,512,128]{2,1,0:T(8,128)S(1)}, u32[]{:S(2)}, u32[]{:S(2)}) async-start(f32[4,512,128]{2,1,0:T(8,128)} %param.16), calls=%async_computation | async-start | bytes 2097152 | tf_op jit(solution)/shard_map/all_to_all | solution.py:182
  7.7 1.8 copy.75
  11.4 7.6 %all-to-all-done = f32[4,512,128]{2,1,0:T(8,128)S(1)} async-done(((f32[4,512,128]{2,1,0:T(8,128)}), f32[4,512,128]{2,1,0:T(8,128)S(1)}, u32[]{:S(2)}, u32[]{:S(2)}) %all-to-all-start) | async-done | bytes 1048608 | tf_op jit(solution)/shard_map/all_to_all | solution.py:182
  19.0 3.6 %all-to-all-start.1 = ((f32[4,1024,128]{1,2,0:T(8,128)}), f32[4,1024,128]{1,2,0:T(8,128)S(1)}, u32[]{:S(2)}, u32[]{:S(2)}) async-start(f32[4,1024,128]{1,2,0:T(8,128)} %copy.75), calls=%async_computation.1 | async-start | bytes 4194304 | tf_op jit(solution)/shard_map/all_to_all | solution.py:183
  24.4 15.5 %shard_map.157 = (f32[128,128]{1,0:T(8,128)}, f32[128,128]{1,0:T(8,128)}) custom-call(f32[128,128]{1,0:T(8,128)} %slice_bitcast_fusion.10.a_ref), custom_call_target="tpu_custom_call" | custom-call | tf_op jit(solution)/shard_map/pallas_call | solution.py:115
  41.2 1.7 fusion.3
  43.8 15.5 %shard_map.158 = (f32[128,128]{1,0:T(8,128)}, f32[128,128]{1,0:T(8,128)}) custom-call(f32[128,128]{1,0:T(8,128)} %slice_bitcast_fusion.9.a_ref), custom_call_target="tpu_custom_call" | custom-call | tf_op jit(solution)/shard_map/pallas_call | solution.py:115
  69.8 15.5 %shard_map.159 = (f32[128,128]{1,0:T(8,128)}, f32[128,128]{1,0:T(8,128)}) custom-call(f32[128,128]{1,0:T(8,128)} %slice_bitcast_fusion.6.a_ref), custom_call_target="tpu_custom_call" | custom-call | tf_op jit(solution)/shard_map/pallas_call | solution.py:115
  88.2 15.6 %shard_map.160 = (f32[128,128]{1,0:T(8,128)}, f32[128,128]{1,0:T(8,128)}) custom-call(f32[128,128]{1,0:T(8,128)} %fusion.9.a_ref), custom_call_target="tpu_custom_call" | custom-call | tf_op jit(solution)/shard_map/pallas_call | solution.py:115
  109.3 5.1 %convolution_multiply_fusion = f32[512,1024]{0,1:T(8,128)S(1)} fusion(f32[1024,512]{0,1:T(8,128)} %bitcast.191, f32[1,128,512]{2,1,0:T(8,128)S(1)} %convolution_bitcast_fusion.3, f32[1,128,512]{2,1,0:T(8,128)S(1)} %convolution_bitcast_fusion.4, f32[1,128,512]{2,1,0:T(8,128)S(1)} %convolution_bitcast_fusion.6, f32[1,128,512]{2,1,0:T(8,128)S(1)} %concatenate.50, ...), kind=kOutput, calls=%fused_computation.15 | convolution fusion | flops 3222536192 | bytes 5246976 | tf_op jit(solution)/shard_map/srk,sck->src/dot_general | solution.py:186
  114.5 2.7 gather_fusion
  117.1 2.7 gather_fusion.1
  119.8 7.0 %convolution_bitcast_fusion.1 = f32[1,15,128,128]{3,2,1,0:T(8,128)S(1)} fusion(f32[15,128,512]{2,1,0:T(8,128)} %gather_fusion, f32[15,128,512]{2,1,0:T(8,128)} %gather_fusion.1), kind=kOutput, calls=%fused_computation.17 | convolution fusion | flops 1509949440 | bytes 8847360 | tf_op jit(solution)/shard_map/spac,spbc->spab/dot_general | solution.py:200
  126.9 2.0 copy.77
  128.8 4.2 %all-to-all-start.2 = ((f32[1,15,128,128]{3,0,1,2:T(1,128)}), f32[1,15,128,128]{3,0,1,2:T(1,128)S(1)}, u32[]{:S(2)}, u32[]{:S(2)}) async-start(f32[1,15,128,128]{3,0,1,2:T(1,128)} %copy.77), calls=%async_computation.2 | async-start | bytes 1966080 | tf_op jit(solution)/shard_map/all_to_all | solution.py:206
  133.1 3.3 %gather_fusion.2 = f32[21,128,512]{2,1,0:T(8,128)} fusion(f32[8,128,512]{2,1,0:T(8,128)S(1)} %bitcast.185, s32[1024]{0:T(1024)S(1)} %pad_clamp_fusion.2), kind=kCustom, calls=%fused_computation.2 | custom fusion | bytes 11010132 | tf_op jit(solution)/shard_map/gather | solution.py:202
  136.4 3.4 %gather_fusion.3 = f32[21,128,512]{2,1,0:T(8,128)} fusion(f32[8,128,512]{2,1,0:T(8,128)S(1)} %bitcast.186, s32[1024]{0:T(1024)S(1)} %pad_clamp_fusion.1), kind=kCustom, calls=%fused_computation.3 | custom fusion | bytes 11010132 | tf_op jit(solution)/shard_map/gather | solution.py:203
  139.7 9.3 %convolution_bitcast_fusion = f32[1,21,128,128]{3,2,1,0:T(8,128)S(1)} fusion(f32[21,128,512]{2,1,0:T(8,128)} %gather_fusion.2, f32[21,128,512]{2,1,0:T(8,128)} %gather_fusion.3), kind=kOutput, calls=%fused_computation.16 | convolution fusion | flops 2113929216 | bytes 12386304 | tf_op jit(solution)/shard_map/spac,spbc->spab/dot_general | solution.py:200
  149.2 2.5 copy.79
  151.7 4.2 %all-to-all-start.3 = ((f32[1,21,128,128]{3,0,1,2:T(1,128)}), f32[1,21,128,128]{3,0,1,2:T(1,128)S(1)}, u32[]{:S(2)}, u32[]{:S(2)}) async-start(f32[1,21,128,128]{3,0,1,2:T(1,128)} %copy.79), calls=%async_computation.3 | async-start | bytes 2752512 | tf_op jit(solution)/shard_map/all_to_all | solution.py:206
  162.7 8.8 %all-to-all-done.3 = f32[1,21,128,128]{3,0,1,2:T(1,128)S(1)} async-done(((f32[1,21,128,128]{3,0,1,2:T(1,128)}), f32[1,21,128,128]{3,0,1,2:T(1,128)S(1)}, u32[]{:S(2)}, u32[]{:S(2)}) %all-to-all-start.3) | async-done | bytes 1376288 | tf_op jit(solution)/shard_map/all_to_all | solution.py:206
  172.2 2.6 gather_fusion.4
  174.8 3.2 %bitcast_select_fusion = f32[64,96,128]{2,1,0:T(8,128)S(1)} fusion(pred[64,96]{1,0:T(8,128)(4,1)S(1)} %copy.71, f32[64,96,128]{2,1,0:T(8,128)} %bitcast.190), kind=kLoop, calls=%fused_computation.12 | loop fusion | flops 786432 | bytes 6297600 | tf_op jit(solution)/shard_map/jit(_where)/select_n | solution.py:229
  178.0 1.9 select_maximum_fusion
  180.0 15.7 %all-to-all-start.4 = ((f32[64,104,128]{2,1,0:T(8,128)}), f32[64,104,128]{2,1,0:T(8,128)S(1)}, u32[]{:S(2)}, u32[]{:S(2)}) async-start(f32[64,104,128]{2,1,0:T(8,128)} %select_maximum_fusion), calls=%async_computation.4 | async-start | bytes 6815744 | tf_op jit(solution)/shard_map/all_to_all | solution.py:236
  195.6 15.2 %shard_map.161 = f32[4,512,128]{2,1,0:T(8,128)} custom-call(f32[1,512,512]{2,1,0:T(8,128)} %select_maximum_fusion.1.x_ref), custom_call_target="tpu_custom_call" | custom-call | bytes 2097152 | tf_op jit(solution)/shard_map/pallas_call | solution.py:63
  210.8 25.5 %shard_map.162 = f32[4,1024,128]{2,1,0:T(8,128)} custom-call(f32[1,1024,512]{2,1,0:T(8,128)} %bitcast.187), custom_call_target="tpu_custom_call" | custom-call | bytes 4194304 | tf_op jit(solution)/shard_map/pallas_call | solution.py:63
  236.4 38.2 %all-to-all-done.4 = f32[64,104,128]{2,1,0:T(8,128)S(1)} async-done(((f32[64,104,128]{2,1,0:T(8,128)}), f32[64,104,128]{2,1,0:T(8,128)S(1)}, u32[]{:S(2)}, u32[]{:S(2)}) %all-to-all-start.4) | async-done | bytes 3407904 | tf_op jit(solution)/shard_map/all_to_all | solution.py:236
  274.6 2.1 slice.118
  278.3 4.8 %fusion = f32[4,2,32,128]{3,0,2,1:T(4,128)S(1)} fusion(f32[192,32,128]{2,1,0:T(8,128)} %bitcast.189, s32[4,2]{0,1:T(2,128)S(1)} %multiply_add_fusion, s32[192]{0:T(256)S(1)} %convert_element_type.46), kind=kOutput, calls=%fused_computation.10 | convolution fusion | flops 75499008 | bytes 3277600 | tf_op jit(solution)/shard_map/ri,rab->iab/dot_general | solution.py:246
  283.8 3.3 %all-to-all-start.5 = ((f32[4,2,32,128]{3,2,1,0:T(8,128)}), f32[4,2,32,128]{3,2,1,0:T(8,128)S(1)}, u32[]{:S(2)}, u32[]{:S(2)}) async-start(f32[4,2,32,128]{3,2,1,0:T(8,128)} %copy.84), calls=%async_computation.5 | async-start | bytes 262144 | tf_op jit(solution)/shard_map/all_to_all | solution.py:248
  287.1 5.7 %all-to-all-done.5 = f32[4,2,32,128]{3,2,1,0:T(8,128)S(1)} async-done(((f32[4,2,32,128]{3,2,1,0:T(8,128)}), f32[4,2,32,128]{3,2,1,0:T(8,128)S(1)}, u32[]{:S(2)}, u32[]{:S(2)}) %all-to-all-start.5) | async-done | bytes 131104 | tf_op jit(solution)/shard_map/all_to_all | solution.py:248
  (121 shorter events, 40.2 us)
Async XLA Ops:
  0.6 10.1 %copy-start.23 = (s32[15]{0:T(128)S(1)}, s32[15]{0:T(128)}, u32[]{:S(2)}) copy-start(s32[15]{0:T(128)} %constant.119) | copy-start | bytes 184
  0.6 10.1 %copy-start.22 = (s32[15]{0:T(128)S(1)}, s32[15]{0:T(128)}, u32[]{:S(2)}) copy-start(s32[15]{0:T(128)} %constant.120) | copy-start | bytes 184
  0.7 7.0 %copy-start.6 = (f32[4,1024,128]{2,1,0:T(8,128)S(1)}, f32[4,1024,128]{2,1,0:T(8,128)}, u32[]{:S(2)}) copy-start(f32[4,1024,128]{2,1,0:T(8,128)} %param.17) | copy-start | bytes 6291460
  0.7 8.8 %copy-start.24 = (s32[4]{0:T(128)S(1)}, s32[4]{0:T(128)}, u32[]{:S(2)}) copy-start(s32[4]{0:T(128)} %param.18) | copy-start | bytes 52
  0.7 18.3 %all-to-all-start = ((f32[4,512,128]{2,1,0:T(8,128)}), f32[4,512,128]{2,1,0:T(8,128)S(1)}, u32[]{:S(2)}, u32[]{:S(2)}) async-start(f32[4,512,128]{2,1,0:T(8,128)} %param.16), calls=%async_computation | async-start | bytes 2097152 | tf_op jit(solution)/shard_map/all_to_all | solution.py:182
  6.2 12.9 %copy-start.10 = (s32[64,2,128]{2,0,1:T(8,128)}, s32[64,2,128]{2,0,1:T(8,128)S(1)}, u32[]{:S(2)}) copy-start(s32[64,2,128]{2,0,1:T(8,128)S(1)} %reduce-window.6) | copy-start | bytes 196612
  6.4 12.6 %copy-start.19 = (s32[64,3]{0,1:T(4,128)}, s32[64,3]{0,1:T(4,128)S(1)}, u32[]{:S(2)}) copy-start(s32[64,3]{0,1:T(4,128)S(1)} %reduce-window.9) | copy-start | bytes 2308
  19.0 89.0 %all-to-all-start.1 = ((f32[4,1024,128]{1,2,0:T(8,128)}), f32[4,1024,128]{1,2,0:T(8,128)S(1)}, u32[]{:S(2)}, u32[]{:S(2)}) async-start(f32[4,1024,128]{1,2,0:T(8,128)} %copy.75), calls=%async_computation.1 | async-start | bytes 4194304 | tf_op jit(solution)/shard_map/all_to_all | solution.py:183
  22.8 1.0 copy-start.5
  39.9 22.9 %copy-start.9 = (f32[128,128]{1,0:T(8,128)S(1)}, f32[128,128]{1,0:T(8,128)}, u32[]{:S(2)}) copy-start(f32[128,128]{1,0:T(8,128)} %get-tuple-element.29) | copy-start | bytes 196612
  68.5 0.7 copy-start.8
  108.0 1.3 copy-start.1
  114.5 21.9 %copy-start = (f32[512,1024]{0,1:T(8,128)}, f32[512,1024]{0,1:T(8,128)S(1)}, u32[]{:S(2)}) copy-start(f32[512,1024]{0,1:T(8,128)S(1)} %convolution_multiply_fusion) | copy-start | bytes 6291460
  126.8 6.2 %copy-start.21 = (s32[21]{0:T(128)S(1)}, s32[21]{0:T(128)}, u32[]{:S(2)}) copy-start(s32[21]{0:T(128)} %constant.121) | copy-start | bytes 256
  126.9 6.2 %copy-start.20 = (s32[21]{0:T(128)S(1)}, s32[21]{0:T(128)}, u32[]{:S(2)}) copy-start(s32[21]{0:T(128)} %constant.122) | copy-start | bytes 256
  128.8 22.8 %all-to-all-start.2 = ((f32[1,15,128,128]{3,0,1,2:T(1,128)}), f32[1,15,128,128]{3,0,1,2:T(1,128)S(1)}, u32[]{:S(2)}, u32[]{:S(2)}) async-start(f32[1,15,128,128]{3,0,1,2:T(1,128)} %copy.77), calls=%async_computation.2 | async-start | bytes 1966080 | tf_op jit(solution)/shard_map/all_to_all | solution.py:206
  149.1 6.8 %copy-start.11 = (s32[64,2,128]{2,0,1:T(8,128)S(1)}, s32[64,2,128]{2,0,1:T(8,128)}, u32[]{:S(2)}) copy-start(s32[64,2,128]{2,0,1:T(8,128)} %copy-done.10) | copy-start | bytes 196612
  149.1 6.8 %slice-start = ((s32[64,3]{0,1:T(4,128)}), s32[64,2]{0,1:T(2,128)S(1)}, s32[]{:S(2)}) async-start(s32[64,3]{0,1:T(4,128)} %copy-done.19), calls=%async_computation.6 | async-start | bytes 2048 | tf_op jit(solution)/shard_map/slice.45
  149.1 6.9 %copy-start.18 = (s32[144,1]{0,1:T(1,128)S(1)}, s32[144,1]{0,1:T(1,128)}, u32[]{:S(2)}) copy-start(s32[144,1]{0,1:T(1,128)} %param.19) | copy-start | bytes 1732
  149.1 11.5 %copy-start.7 = (f32[256,128]{1,0:T(8,128)S(1)}, f32[256,128]{1,0:T(8,128)}, u32[]{:S(2)}) copy-start(f32[256,128]{1,0:T(8,128)} %copy.74) | copy-start | bytes 393220
  149.1 11.5 %copy-start.14 = (f32[128,128]{1,0:T(8,128)S(1)}, f32[128,128]{1,0:T(8,128)}, u32[]{:S(2)}) copy-start(f32[128,128]{1,0:T(8,128)} %get-tuple-element.33) | copy-start | bytes 196612
  149.1 11.5 %copy-start.15 = (f32[128,128]{1,0:T(8,128)S(1)}, f32[128,128]{1,0:T(8,128)}, u32[]{:S(2)}) copy-start(f32[128,128]{1,0:T(8,128)} %get-tuple-element.34) | copy-start | bytes 196612
  149.1 11.5 %copy-start.16 = (f32[128,128]{1,0:T(8,128)S(1)}, f32[128,128]{1,0:T(8,128)}, u32[]{:S(2)}) copy-start(f32[128,128]{1,0:T(8,128)} %get-tuple-element.35) | copy-start | bytes 196612
  149.1 11.5 %copy-start.17 = (f32[128,128]{1,0:T(8,128)S(1)}, f32[128,128]{1,0:T(8,128)}, u32[]{:S(2)}) copy-start(f32[128,128]{1,0:T(8,128)} %get-tuple-element.36) | copy-start | bytes 196612
  151.7 19.9 %all-to-all-start.3 = ((f32[1,21,128,128]{3,0,1,2:T(1,128)}), f32[1,21,128,128]{3,0,1,2:T(1,128)S(1)}, u32[]{:S(2)}, u32[]{:S(2)}) async-start(f32[1,21,128,128]{3,0,1,2:T(1,128)} %copy.79), calls=%async_computation.3 | async-start | bytes 2752512 | tf_op jit(solution)/shard_map/all_to_all | solution.py:206
  162.7 9.0 %copy-start.4 = (f32[1,15,128,128]{3,2,1,0:T(8,128)S(1)}, f32[1,15,128,128]{3,2,1,0:T(8,128)}, u32[]{:S(2)}) copy-start(f32[1,15,128,128]{3,2,1,0:T(8,128)} %copy.78) | copy-start | bytes 2949124
  174.8 3.2 %copy-start.12 = (f32[64,1,3]{2,0,1:T(8,128)S(1)}, f32[64,1,3]{2,0,1:T(8,128)}, u32[]{:S(2)}) copy-start(f32[64,1,3]{2,0,1:T(8,128)} %reshape.261) | copy-start | bytes 2308
  180.0 94.6 %all-to-all-start.4 = ((f32[64,104,128]{2,1,0:T(8,128)}), f32[64,104,128]{2,1,0:T(8,128)S(1)}, u32[]{:S(2)}, u32[]{:S(2)}) async-start(f32[64,104,128]{2,1,0:T(8,128)} %select_maximum_fusion), calls=%async_computation.4 | async-start | bytes 6815744 | tf_op jit(solution)/shard_map/all_to_all | solution.py:236
  276.6 16.2 %copy-start.13 = (f32[2,128,128]{2,1,0:T(8,128)S(1)}, f32[2,128,128]{2,1,0:T(8,128)}, u32[]{:S(2)}) copy-start(f32[2,128,128]{2,1,0:T(8,128)} %param.21) | copy-start | bytes 393220
  277.4 16.2 %copy-start.3 = (f32[4,512,128]{2,1,0:T(8,128)S(1)}, f32[4,512,128]{2,1,0:T(8,128)}, u32[]{:S(2)}) copy-start(f32[4,512,128]{2,1,0:T(8,128)} %shard_map.161) | copy-start | bytes 3145732
  278.3 16.2 %copy-start.2 = (f32[4,1024,128]{2,1,0:T(8,128)S(1)}, f32[4,1024,128]{2,1,0:T(8,128)}, u32[]{:S(2)}) copy-start(f32[4,1024,128]{2,1,0:T(8,128)} %shard_map.162) | copy-start | bytes 6291460
  283.8 9.1 %all-to-all-start.5 = ((f32[4,2,32,128]{3,2,1,0:T(8,128)}), f32[4,2,32,128]{3,2,1,0:T(8,128)S(1)}, u32[]{:S(2)}, u32[]{:S(2)}) async-start(f32[4,2,32,128]{3,2,1,0:T(8,128)} %copy.84), calls=%async_computation.5 | async-start | bytes 262144 | tf_op jit(solution)/shard_map/all_to_all | solution.py:248

commit v4 on v2

--- a/solution.py
+++ b/solution.py
@@ -89,21 +89,20 @@
         tail_cols = lax.broadcasted_iota(jnp.int32, (height, n), 1)
         tail_rows = top + lax.broadcasted_iota(jnp.int32, (height, 1), 0)
 
-        def step(j, carry, top=top, height=height, tail_cols=tail_cols, tail_rows=tail_rows):
+        def step(j, carry, top=top, tail_cols=tail_cols, tail_rows=tail_rows):
             r = work[pl.ds(j, 1), :]
+            whole = work[top:, :]
+            col = jnp.sum(jnp.where(tail_cols == j, whole, 0.0), axis=1, keepdims=True)
             piv = jnp.sum(jnp.where(lane == j, r, 0.0), axis=1, keepdims=True)
-            root = jnp.sqrt(piv)
-            scale = 1.0 / root
-            u_row = jnp.where(lane >= j, r * scale, 0.0)
-            upper[pl.ds(j, 1), :] = u_row
+            inv_piv = 1.0 / piv
+            r_live = jnp.where(lane >= j, r, 0.0)
+            mult = jnp.where(tail_rows > j, col * inv_piv, 0.0)
+            work[top:, :] = whole - mult * r_live
             e_row = elim[pl.ds(j, 1), :]
+            elim[top:, :] = elim[top:, :] - mult * e_row
+            scale = 1.0 / jnp.sqrt(piv)
+            upper[pl.ds(j, 1), :] = r_live * scale
             inv_ref[pl.ds(j, 1), :] = e_row * scale
-            whole = work[top:, :]
-            u_col = jnp.sum(jnp.where(tail_cols == j, whole, 0.0), axis=1, keepdims=True) * scale
-            u_col = jnp.where(tail_rows >= j, u_col, 0.0)
-            work[top:, :] = whole - u_col * u_row
-            mult = jnp.where(tail_rows > j, u_col * scale, 0.0)
-            elim[top:, :] = elim[top:, :] - mult * e_row
             return carry
 
         lax.fori_loop(top, top + phase, step, 0)

time: 292 us -> 287 us (0.983)
  Pallas kernels: 103 us -> 97.4 us
    pallas_call x4, Pallas kernels: 61.9 us -> 56.7 us  [block_chol(): pl.pallas_call(block_chol_kernel, out_shape=(jax.ShapeDtypeStruct((n, n),...]
  transfers between devices with their start and end apart: 5 -> 5, of which waited for: 4 -> 4; matrix products, arithmetic and copies ran while one was open for 11% -> 11% of each run, Pallas kernels for 35% -> 34%
where the time goes in v4:
time: 287 us; the launch traced here: 286 us
  Pallas kernels  97.4 us (34%)
  waiting for transfers between devices  75.3 us (26%)
  local copies, waits for them, and re-layouts  38.2 us (13%)
  matrix products  33.4 us (12%)
  starting transfers between devices  30.5 us (11%)
  other arithmetic  9.67 us (3%)
    pallas_call x4, Pallas kernels, block_chol(): pl.pallas_call(block_chol_kernel, out_shape=(jax.ShapeDtypeStruct((n, n),...  56.7 us
    pallas_call x2, Pallas kernels, columns_out(): pl.pallas_call(functools.partial(columns_out_kernel, count=count, group=g...  40.7 us
    all_to_all x1, waiting for transfers between devices, local(): lax.all_to_all(send_buffer, 'wide', split_axis=0, concat_axis=0, tiled=True)  38.2 us
    all_to_all x1, waiting for transfers between devices, local(): lax.all_to_all(contribution, 'narrow', split_axis=2, concat_axis=0, tiled...  20.8 us
    all_to_all x1, starting transfers between devices, local(): lax.all_to_all(send_buffer, 'wide', split_axis=0, concat_axis=0, tiled=True)  15.1 us
    all_to_all x1, waiting for transfers between devices, local(): lax.all_to_all(diag_block, 'narrow', split_axis=0, concat_axis=2, tiled=T...  10.5 us
    dot_general x1, matrix products, local(): jnp.einsum('siac,sjbc->sijab', blocks, blocks, precision=lax.Precision.HI...  8.97 us
    dot_general x6, matrix products, mm_t(): return jnp.einsum('sik,sjk->sij', a, b, precision=lax.Precision.HIGHEST)  7.51 us
  transfers between devices with their start and end apart: 5, of which 4 were waited for; matrix products, arithmetic and copies ran while one was open for 11% of the time, Pallas kernels for 34%

profile of v4, /device:TPU:9, one launch (start us, length us, event | category | flops | bytes accessed | tf_op | source)
XLA Modules:
  0.0 285.6 jit_solution(984776031375335261)
XLA Ops:
  0.7 4.2 %all-to-all-start = ((f32[4,512,128]{2,1,0:T(8,128)}), f32[4,512,128]{2,1,0:T(8,128)S(1)}, u32[]{:S(2)}, u32[]{:S(2)}) async-start(f32[4,512,128]{2,1,0:T(8,128)} %param.10), calls=%async_computation | async-start | bytes 2097152 | tf_op jit(solution)/shard_map/all_to_all | solution.py:181
  4.8 1.8 copy.68
  8.5 10.5 %all-to-all-done = f32[4,512,128]{2,1,0:T(8,128)S(1)} async-done(((f32[4,512,128]{2,1,0:T(8,128)}), f32[4,512,128]{2,1,0:T(8,128)S(1)}, u32[]{:S(2)}, u32[]{:S(2)}) %all-to-all-start) | async-done | bytes 1048608 | tf_op jit(solution)/shard_map/all_to_all | solution.py:181
  19.0 3.6 %all-to-all-start.1 = ((f32[4,1024,128]{1,2,0:T(8,128)}), f32[4,1024,128]{1,2,0:T(8,128)S(1)}, u32[]{:S(2)}, u32[]{:S(2)}) async-start(f32[4,1024,128]{1,2,0:T(8,128)} %copy.68), calls=%async_computation.1 | async-start | bytes 4194304 | tf_op jit(solution)/shard_map/all_to_all | solution.py:182
  24.4 14.2 %shard_map.103 = (f32[128,128]{1,0:T(8,128)}, f32[128,128]{1,0:T(8,128)}) custom-call(f32[128,128]{1,0:T(8,128)} %slice_bitcast_fusion.10.a_ref), custom_call_target="tpu_custom_call" | custom-call | tf_op jit(solution)/shard_map/pallas_call | solution.py:114
  38.5 1.4 fusion.37
  40.0 1.7 fusion.3
  42.4 14.2 %shard_map.104 = (f32[128,128]{1,0:T(8,128)}, f32[128,128]{1,0:T(8,128)}) custom-call(f32[128,128]{1,0:T(8,128)} %slice_bitcast_fusion.9.a_ref), custom_call_target="tpu_custom_call" | custom-call | tf_op jit(solution)/shard_map/pallas_call | solution.py:114
  62.2 1.5 fusion.72
  67.2 14.2 %shard_map.105 = (f32[128,128]{1,0:T(8,128)}, f32[128,128]{1,0:T(8,128)}) custom-call(f32[128,128]{1,0:T(8,128)} %slice_bitcast_fusion.6.a_ref), custom_call_target="tpu_custom_call" | custom-call | tf_op jit(solution)/shard_map/pallas_call | solution.py:114
  81.4 1.4 convolution_bitcast_fusion.3
  83.9 1.5 fusion.4
  86.1 1.7 fusion.9.a_ref
  87.8 14.2 %shard_map.106 = (f32[128,128]{1,0:T(8,128)}, f32[128,128]{1,0:T(8,128)}) custom-call(f32[128,128]{1,0:T(8,128)} %fusion.9.a_ref), custom_call_target="tpu_custom_call" | custom-call | tf_op jit(solution)/shard_map/pallas_call | solution.py:114
  104.7 5.1 %convolution_multiply_fusion = f32[512,1024]{0,1:T(8,128)S(1)} fusion(f32[1024,512]{0,1:T(8,128)} %bitcast.189, f32[1,128,512]{2,1,0:T(8,128)S(1)} %convolution_bitcast_fusion.2, f32[1,128,512]{2,1,0:T(8,128)S(1)} %convolution_bitcast_fusion.3, f32[1,128,512]{2,1,0:T(8,128)S(1)} %convolution_bitcast_fusion.5, f32[1,128,512]{2,1,0:T(8,128)S(1)} %concatenate.47, ...), kind=kOutput, calls=%fused_computation.12 | convolution fusion | flops 3222536192 | bytes 5246976 | tf_op jit(solution)/shard_map/srk,sck->src/dot_general | solution.py:185
  109.9 9.0 %convolution_bitcast_fusion = f32[1,8,8,128,128]{3,4,1,2,0:T(8,128)} fusion(f32[8,128,512,1]{2,1,3,0:T(8,128)S(1)} %bitcast.180, f32[8,128,512,1]{2,1,0,3:T(8,128)S(1)} %bitcast.181), kind=kOutput, calls=%fused_computation.11 | convolution fusion | flops 6442450944 | bytes 8388608 | tf_op jit(solution)/shard_map/siac,sjbc->sijab/dot_general | solution.py:196
  118.8 5.4 %copy.70 = f32[1,8,8,128,128]{4,3,2,1,0:T(8,128)} copy(f32[1,8,8,128,128]{3,4,1,2,0:T(8,128)} %convolution_bitcast_fusion) | data formatting | bytes 8388608 | tf_op jit(solution)/shard_map/siac,sjbc->sijab/transpose | solution.py:196
  124.2 2.9 %gather_fusion = f32[36,128,128]{2,1,0:T(8,128)S(1)} fusion(f32[64,128,128]{2,1,0:T(8,128)} %bitcast.186, s32[1024]{0:T(1024)S(1)} %pad_clamp_fusion.1), kind=kCustom, calls=%fused_computation | custom fusion | bytes 4718736 | tf_op jit(solution)/shard_map/gather | solution.py:198
  127.1 3.8 %copy.71 = f32[1,36,128,128]{3,0,1,2:T(1,128)} copy(f32[1,36,128,128]{3,2,1,0:T(8,128)S(1)} %bitcast.187) | data formatting | bytes 4718592 | tf_op jit(solution)/shard_map/gather | solution.py:198
  131.0 4.3 %all-to-all-start.2 = ((f32[1,36,128,128]{3,0,1,2:T(1,128)}), f32[1,36,128,128]{3,0,1,2:T(1,128)S(1)}, u32[]{:S(2)}, u32[]{:S(2)}) async-start(f32[1,36,128,128]{3,0,1,2:T(1,128)} %copy.71), calls=%async_computation.2 | async-start | bytes 4718592 | tf_op jit(solution)/shard_map/all_to_all | solution.py:200
  141.3 20.8 %all-to-all-done.2 = f32[1,36,128,128]{3,0,1,2:T(1,128)S(1)} async-done(((f32[1,36,128,128]{3,0,1,2:T(1,128)}), f32[1,36,128,128]{3,0,1,2:T(1,128)S(1)}, u32[]{:S(2)}, u32[]{:S(2)}) %all-to-all-start.2) | async-done | bytes 2359328 | tf_op jit(solution)/shard_map/all_to_all | solution.py:200
  162.7 2.5 gather_fusion.1
  165.2 3.2 %bitcast_select_fusion = f32[64,96,128]{2,1,0:T(8,128)S(1)} fusion(pred[64,96]{1,0:T(8,128)(4,1)S(1)} %copy.64, f32[64,96,128]{2,1,0:T(8,128)} %bitcast.185), kind=kLoop, calls=%fused_computation.9 | loop fusion | flops 786432 | bytes 6297600 | tf_op jit(solution)/shard_map/jit(_where)/select_n | solution.py:222
  168.4 2.0 select_maximum_fusion
  170.3 15.1 %all-to-all-start.3 = ((f32[64,104,128]{2,1,0:T(8,128)}), f32[64,104,128]{2,1,0:T(8,128)S(1)}, u32[]{:S(2)}, u32[]{:S(2)}) async-start(f32[64,104,128]{2,1,0:T(8,128)} %select_maximum_fusion), calls=%async_computation.3 | async-start | bytes 6815744 | tf_op jit(solution)/shard_map/all_to_all | solution.py:229
  185.4 26.4 %shard_map.108 = f32[4,1024,128]{2,1,0:T(8,128)} custom-call(f32[1,1024,512]{2,1,0:T(8,128)} %bitcast.182), custom_call_target="tpu_custom_call" | custom-call | bytes 4194304 | tf_op jit(solution)/shard_map/pallas_call | solution.py:63
  211.9 14.3 %shard_map.107 = f32[4,512,128]{2,1,0:T(8,128)} custom-call(f32[1,512,512]{2,1,0:T(8,128)} %select_maximum_fusion.1.x_ref), custom_call_target="tpu_custom_call" | custom-call | bytes 2097152 | tf_op jit(solution)/shard_map/pallas_call | solution.py:63
  226.2 38.2 %all-to-all-done.3 = f32[64,104,128]{2,1,0:T(8,128)S(1)} async-done(((f32[64,104,128]{2,1,0:T(8,128)}), f32[64,104,128]{2,1,0:T(8,128)S(1)}, u32[]{:S(2)}, u32[]{:S(2)}) %all-to-all-start.3) | async-done | bytes 3407904 | tf_op jit(solution)/shard_map/all_to_all | solution.py:229
  264.4 2.0 slice.118
  268.1 4.8 %fusion = f32[4,2,32,128]{3,0,2,1:T(4,128)S(1)} fusion(f32[192,32,128]{2,1,0:T(8,128)} %bitcast.184, s32[4,2]{0,1:T(2,128)S(1)} %multiply_add_fusion, s32[192]{0:T(256)S(1)} %convert_element_type.46), kind=kOutput, calls=%fused_computation.7 | convolution fusion | flops 75499008 | bytes 3277600 | tf_op jit(solution)/shard_map/ri,rab->iab/dot_general | solution.py:239
  273.6 3.3 %all-to-all-start.4 = ((f32[4,2,32,128]{3,2,1,0:T(8,128)}), f32[4,2,32,128]{3,2,1,0:T(8,128)S(1)}, u32[]{:S(2)}, u32[]{:S(2)}) async-start(f32[4,2,32,128]{3,2,1,0:T(8,128)} %copy.76), calls=%async_computation.4 | async-start | bytes 262144 | tf_op jit(solution)/shard_map/all_to_all | solution.py:241
  276.9 5.7 %all-to-all-done.4 = f32[4,2,32,128]{3,2,1,0:T(8,128)S(1)} async-done(((f32[4,2,32,128]{3,2,1,0:T(8,128)}), f32[4,2,32,128]{3,2,1,0:T(8,128)S(1)}, u32[]{:S(2)}, u32[]{:S(2)}) %all-to-all-start.4) | async-done | bytes 131104 | tf_op jit(solution)/shard_map/all_to_all | solution.py:241
  (95 shorter events, 29.6 us)
Async XLA Ops:
  0.6 7.2 %copy-start.16 = (s32[36]{0:T(128)S(1)}, s32[36]{0:T(128)}, u32[]{:S(2)}) copy-start(s32[36]{0:T(128)} %constant.104) | copy-start | bytes 436
  0.6 4.2 %copy-start.5 = (f32[4,1024,128]{2,1,0:T(8,128)S(1)}, f32[4,1024,128]{2,1,0:T(8,128)}, u32[]{:S(2)}) copy-start(f32[4,1024,128]{2,1,0:T(8,128)} %param.11) | copy-start | bytes 6291460
  0.7 6.0 %copy-start.17 = (s32[4]{0:T(128)S(1)}, s32[4]{0:T(128)}, u32[]{:S(2)}) copy-start(s32[4]{0:T(128)} %param.12) | copy-start | bytes 52
  0.7 18.3 %all-to-all-start = ((f32[4,512,128]{2,1,0:T(8,128)}), f32[4,512,128]{2,1,0:T(8,128)S(1)}, u32[]{:S(2)}, u32[]{:S(2)}) async-start(f32[4,512,128]{2,1,0:T(8,128)} %param.10), calls=%async_computation | async-start | bytes 2097152 | tf_op jit(solution)/shard_map/all_to_all | solution.py:181
  19.0 84.4 %all-to-all-start.1 = ((f32[4,1024,128]{1,2,0:T(8,128)}), f32[4,1024,128]{1,2,0:T(8,128)S(1)}, u32[]{:S(2)}, u32[]{:S(2)}) async-start(f32[4,1024,128]{1,2,0:T(8,128)} %copy.68), calls=%async_computation.1 | async-start | bytes 4194304 | tf_op jit(solution)/shard_map/all_to_all | solution.py:182
  22.8 1.0 copy-start.4
  38.5 22.3 %copy-start.8 = (f32[128,128]{1,0:T(8,128)S(1)}, f32[128,128]{1,0:T(8,128)}, u32[]{:S(2)}) copy-start(f32[128,128]{1,0:T(8,128)} %get-tuple-element.29) | copy-start | bytes 196612
  65.9 0.7 copy-start.7
  103.4 1.3 copy-start.1
  109.9 9.0 %copy-start = (f32[512,1024]{0,1:T(8,128)}, f32[512,1024]{0,1:T(8,128)S(1)}, u32[]{:S(2)}) copy-start(f32[512,1024]{0,1:T(8,128)S(1)} %convolution_multiply_fusion) | copy-start | bytes 6291460
  131.0 4.4 %copy-start.14 = (s32[144,1]{0,1:T(1,128)S(1)}, s32[144,1]{0,1:T(1,128)}, u32[]{:S(2)}) copy-start(s32[144,1]{0,1:T(1,128)} %param.13) | copy-start | bytes 1732
  131.0 7.9 %copy-start.15 = (s32[144]{0:T(256)S(1)}, s32[144]{0:T(256)}, u32[]{:S(2)}) copy-start(s32[144]{0:T(256)} %param.14) | copy-start | bytes 1732
  131.0 9.2 %copy-start.6 = (f32[256,128]{1,0:T(8,128)S(1)}, f32[256,128]{1,0:T(8,128)}, u32[]{:S(2)}) copy-start(f32[256,128]{1,0:T(8,128)} %copy.67) | copy-start | bytes 393220
  131.0 9.2 %copy-start.10 = (f32[128,128]{1,0:T(8,128)S(1)}, f32[128,128]{1,0:T(8,128)}, u32[]{:S(2)}) copy-start(f32[128,128]{1,0:T(8,128)} %get-tuple-element.33) | copy-start | bytes 196612
  131.0 9.2 %copy-start.11 = (f32[128,128]{1,0:T(8,128)S(1)}, f32[128,128]{1,0:T(8,128)}, u32[]{:S(2)}) copy-start(f32[128,128]{1,0:T(8,128)} %get-tuple-element.34) | copy-start | bytes 196612
  131.0 9.2 %copy-start.12 = (f32[128,128]{1,0:T(8,128)S(1)}, f32[128,128]{1,0:T(8,128)}, u32[]{:S(2)}) copy-start(f32[128,128]{1,0:T(8,128)} %get-tuple-element.35) | copy-start | bytes 196612
  131.0 9.2 %copy-start.13 = (f32[128,128]{1,0:T(8,128)S(1)}, f32[128,128]{1,0:T(8,128)}, u32[]{:S(2)}) copy-start(f32[128,128]{1,0:T(8,128)} %get-tuple-element.36) | copy-start | bytes 196612
  131.0 31.1 %all-to-all-start.2 = ((f32[1,36,128,128]{3,0,1,2:T(1,128)}), f32[1,36,128,128]{3,0,1,2:T(1,128)S(1)}, u32[]{:S(2)}, u32[]{:S(2)}) async-start(f32[1,36,128,128]{3,0,1,2:T(1,128)} %copy.71), calls=%async_computation.2 | async-start | bytes 4718592 | tf_op jit(solution)/shard_map/all_to_all | solution.py:200
  170.3 94.0 %all-to-all-start.3 = ((f32[64,104,128]{2,1,0:T(8,128)}), f32[64,104,128]{2,1,0:T(8,128)S(1)}, u32[]{:S(2)}, u32[]{:S(2)}) async-start(f32[64,104,128]{2,1,0:T(8,128)} %select_maximum_fusion), calls=%async_computation.3 | async-start | bytes 6815744 | tf_op jit(solution)/shard_map/all_to_all | solution.py:229
  266.4 16.2 %copy-start.9 = (f32[2,128,128]{2,1,0:T(8,128)S(1)}, f32[2,128,128]{2,1,0:T(8,128)}, u32[]{:S(2)}) copy-start(f32[2,128,128]{2,1,0:T(8,128)} %param.15) | copy-start | bytes 393220
  267.1 16.2 %copy-start.3 = (f32[4,512,128]{2,1,0:T(8,128)S(1)}, f32[4,512,128]{2,1,0:T(8,128)}, u32[]{:S(2)}) copy-start(f32[4,512,128]{2,1,0:T(8,128)} %shard_map.107) | copy-start | bytes 3145732
  268.1 16.2 %copy-start.2 = (f32[4,1024,128]{2,1,0:T(8,128)S(1)}, f32[4,1024,128]{2,1,0:T(8,128)}, u32[]{:S(2)}) copy-start(f32[4,1024,128]{2,1,0:T(8,128)} %shard_map.108) | copy-start | bytes 6291460
  273.6 9.1 %all-to-all-start.4 = ((f32[4,2,32,128]{3,2,1,0:T(8,128)}), f32[4,2,32,128]{3,2,1,0:T(8,128)S(1)}, u32[]{:S(2)}, u32[]{:S(2)}) async-start(f32[4,2,32,128]{3,2,1,0:T(8,128)} %copy.76), calls=%async_computation.4 | async-start | bytes 262144 | tf_op jit(solution)/shard_map/all_to_all | solution.py:241

commit v5 on v4

--- a/solution.py
+++ b/solution.py
@@ -131,10 +131,8 @@
 def blocked_cholesky(matrix):
     batch, size, _ = matrix.shape
     nblk = size // B
-    eye = jnp.broadcast_to(jnp.eye(B, dtype=jnp.float32), (batch, B, B))
     trailing = matrix
     diag_l, diag_inv, below = [], [], []
-    inverse_rows = []
     for k in range(nblk):
         head = trailing[:, :B, :B]
         pieces = [block_chol(head[b]) for b in range(batch)]
@@ -142,15 +140,6 @@
         i_kk = jnp.stack([p[1] for p in pieces])
         diag_l.append(l_kk)
         diag_inv.append(i_kk)
-        if k > 0:
-            left = jnp.concatenate([below[j][:, (k - j - 1) * B:(k - j) * B, :] for j in range(k)], axis=2)
-            upper = jnp.concatenate(inverse_rows, axis=1)
-            rest = -mm(left, upper)
-            rest = jnp.concatenate([rest[:, :, :k * B], eye, rest[:, :, (k + 1) * B:]], axis=2)
-            inverse_rows.append(mm(i_kk, rest))
-        else:
-            inverse_rows.append(jnp.concatenate(
-                [i_kk, jnp.zeros((batch, B, size - B), jnp.float32)], axis=2))
         if k < nblk - 1:
             panel_k = mm_t(trailing[:, B:, :B], i_kk)
             below.append(panel_k)
@@ -165,8 +154,20 @@
             parts.append(below[k])
         columns.append(jnp.concatenate(parts, axis=1))
     factor = jnp.concatenate(columns, axis=2)
-    inverse = jnp.concatenate(inverse_rows, axis=1)
-    return factor, inverse
+    return factor, diag_inv, below
+
+
+def solve_panel(panel, diag_inv, below):
+    done = []
+    for k, i_kk in enumerate(diag_inv):
+        rhs = panel[:, :, k * B:(k + 1) * B]
+        if k > 0:
+            left = jnp.concatenate(
+                [below[j][:, (k - j - 1) * B:(k - j) * B, :] for j in range(k)], axis=2
+            )
+            rhs = rhs - mm_t(jnp.concatenate(done, axis=2), left)
+        done.append(mm_t(rhs, i_kk))
+    return jnp.concatenate(done, axis=2)
 
 
 def local(diag_block, panel, panel_count, pair_owner, pair_slot, ancestor):
@@ -181,10 +182,8 @@
     whole_diag = lax.all_to_all(diag_block, "narrow", split_axis=0, concat_axis=2, tiled=True)
     whole_panel = lax.all_to_all(panel, "narrow", split_axis=0, concat_axis=2, tiled=True)
 
-    factor, inverse = blocked_cholesky(whole_diag)
-    lower_panel = jnp.einsum(
-        "srk,sck->src", whole_panel, inverse, precision=lax.Precision.HIGHEST
-    )
+    factor, diag_inv, below = blocked_cholesky(whole_diag)
+    lower_panel = solve_panel(whole_panel, diag_inv, below)
     counts = lax.dynamic_slice_in_dim(panel_count, narrow_index * group, group)
     block_index = jnp.arange(P_SIZE * B, dtype=jnp.int32) // B
     live = (block_index[None, :] < counts[:, None]).astype(jnp.float32)

time: 287 us -> 294 us (1.024)
  matrix products: 33.4 us -> 37.8 us
  waiting for transfers between devices: 75.3 us -> 71.7 us
  other arithmetic: 9.67 us -> 13.2 us
    dot_general x7 -> x0, matrix products: 12.2 us -> none  [the longest x6 7.06 us: mm(): return jnp.einsum('sik,skj->sij', a, b, precision=lax.Precision.HIGHEST)]
    dot_general x6 -> x13, matrix products: 7.51 us -> 17.1 us  [mm_t(): return jnp.einsum('sik,sjk->sij', a, b, precision=lax.Precision.HIGHEST)]
    dot_general x1, matrix products: 8.97 us -> 16 us  [local(): jnp.einsum('siac,sjbc->sijab', blocks, blocks, precision=lax.Precision.HI...]
    all_to_all x1, waiting for transfers between devices: 20.8 us -> 14.8 us  [local(): lax.all_to_all(contribution, 'narrow', split_axis=2, concat_axis=0, tiled...]
    dot_general x2 -> x6, local copies, waits for them, and re-layouts: 0.88 us -> 6.57 us  [mm_t(): return jnp.einsum('sik,sjk->sij', a, b, precision=lax.Precision.HIGHEST)]
    slice x6 -> x1, local copies, waits for them, and re-layouts: 4.81 us -> 0.68 us  [solve_panel(): below[j][:, (k - j - 1) * B:(k - j) * B, :]]
    unnamed x39 -> x29, local copies, waits for them, and re-layouts: 7.14 us -> 3.59 us
  transfers between devices with their start and end apart: 5 -> 5, of which waited for: 4 -> 4; matrix products, arithmetic and copies ran while one was open for 11% -> 7% of each run, Pallas kernels for 34% -> 33%
where the time goes in v5:
time: 294 us; the launch traced here: 293 us
  Pallas kernels  97.3 us (33%)
  waiting for transfers between devices  71.7 us (24%)
  local copies, waits for them, and re-layouts  40.1 us (14%)
  matrix products  37.8 us (13%)
  starting transfers between devices  31.5 us (11%)
  other arithmetic  13.2 us (4%)
    pallas_call x4, Pallas kernels, block_chol(): pl.pallas_call(block_chol_kernel, out_shape=(jax.ShapeDtypeStruct((n, n),...  56.6 us
    pallas_call x2, Pallas kernels, columns_out(): pl.pallas_call(functools.partial(columns_out_kernel, count=count, group=g...  40.7 us
    all_to_all x1, waiting for transfers between devices, local(): lax.all_to_all(send_buffer, 'wide', split_axis=0, concat_axis=0, tiled=True)  38.2 us
    dot_general x13, matrix products, mm_t(): return jnp.einsum('sik,sjk->sij', a, b, precision=lax.Precision.HIGHEST)  17.1 us
    dot_general x1, matrix products, local(): jnp.einsum('siac,sjbc->sijab', blocks, blocks, precision=lax.Precision.HI...  16 us
    all_to_all x1, starting transfers between devices, local(): lax.all_to_all(send_buffer, 'wide', split_axis=0, concat_axis=0, tiled=True)  15.1 us
    all_to_all x1, waiting for transfers between devices, local(): lax.all_to_all(contribution, 'narrow', split_axis=2, concat_axis=0, tiled...  14.8 us
    all_to_all x1, waiting for transfers between devices, local(): lax.all_to_all(diag_block, 'narrow', split_axis=0, concat_axis=2, tiled=T...  12.9 us
  transfers between devices with their start and end apart: 5, of which 4 were waited for; matrix products, arithmetic and copies ran while one was open for 7% of the time, Pallas kernels for 33%

profile of v5, /device:TPU:9, one launch (start us, length us, event | category | flops | bytes accessed | tf_op | source)
XLA Modules:
  0.0 292.6 jit_solution(18027732024479108843)
XLA Ops:
  0.7 4.2 %all-to-all-start.1 = ((f32[4,512,128]{2,1,0:T(8,128)}), f32[4,512,128]{2,1,0:T(8,128)S(1)}, u32[]{:S(2)}, u32[]{:S(2)}) async-start(f32[4,512,128]{2,1,0:T(8,128)} %param.10), calls=%async_computation.1 | async-start | bytes 2097152 | tf_op jit(solution)/shard_map/all_to_all | solution.py:182
  6.1 12.9 %all-to-all-done.1 = f32[4,512,128]{2,1,0:T(8,128)S(1)} async-done(((f32[4,512,128]{2,1,0:T(8,128)}), f32[4,512,128]{2,1,0:T(8,128)S(1)}, u32[]{:S(2)}, u32[]{:S(2)}) %all-to-all-start.1) | async-done | bytes 1048608 | tf_op jit(solution)/shard_map/all_to_all | solution.py:182
  19.0 4.4 %all-to-all-start = ((f32[4,1024,128]{2,1,0:T(8,128)}), f32[4,1024,128]{2,1,0:T(8,128)}, u32[]{:S(2)}, u32[]{:S(2)}) async-start(f32[4,1024,128]{2,1,0:T(8,128)} %param.11), calls=%async_computation | async-start | bytes 4194304 | tf_op jit(solution)/shard_map/all_to_all | solution.py:183
  24.2 14.2 %shard_map.103 = (f32[128,128]{1,0:T(8,128)}, f32[128,128]{1,0:T(8,128)}) custom-call(f32[128,128]{1,0:T(8,128)} %slice_bitcast_fusion.12.a_ref), custom_call_target="tpu_custom_call" | custom-call | tf_op jit(solution)/shard_map/pallas_call | solution.py:114
  41.1 14.2 %shard_map.104 = (f32[128,128]{1,0:T(8,128)}, f32[128,128]{1,0:T(8,128)}) custom-call(f32[128,128]{1,0:T(8,128)} %slice_bitcast_fusion.9.a_ref), custom_call_target="tpu_custom_call" | custom-call | tf_op jit(solution)/shard_map/pallas_call | solution.py:114
  57.5 14.2 %shard_map.105 = (f32[128,128]{1,0:T(8,128)}, f32[128,128]{1,0:T(8,128)}) custom-call(f32[128,128]{1,0:T(8,128)} %slice_bitcast_fusion.8.a_ref), custom_call_target="tpu_custom_call" | custom-call | tf_op jit(solution)/shard_map/pallas_call | solution.py:114
  73.7 14.2 %shard_map.106 = (f32[128,128]{1,0:T(8,128)}, f32[128,128]{1,0:T(8,128)}) custom-call(f32[128,128]{1,0:T(8,128)} %fusion.21.a_ref), custom_call_target="tpu_custom_call" | custom-call | tf_op jit(solution)/shard_map/pallas_call | solution.py:114
  93.0 2.4 fusion.59
  95.5 2.1 copy.90
  97.5 2.1 fusion.18
  101.1 2.1 copy.92
  103.1 2.7 fusion.16
  109.9 16.0 %convolution_bitcast_fusion = f32[1,8,8,128,128]{3,4,1,2,0:T(8,128)} fusion(f32[8,128,512]{2,1,0:T(8,128)} %copy.94, f32[8,128,512,1]{1,0,2,3:T(8,128)S(1)} %bitcast.202), kind=kOutput, calls=%fused_computation.11 | convolution fusion | flops 6442450944 | bytes 8388608 | tf_op jit(solution)/shard_map/siac,sjbc->sijab/dot_general | solution.py:195
  125.9 5.4 %copy.95 = f32[1,8,8,128,128]{4,3,2,1,0:T(8,128)} copy(f32[1,8,8,128,128]{3,4,1,2,0:T(8,128)} %convolution_bitcast_fusion) | data formatting | bytes 8388608 | tf_op jit(solution)/shard_map/siac,sjbc->sijab/transpose | solution.py:195
  131.3 2.9 gather_fusion
  134.2 3.8 %copy.96 = f32[1,36,128,128]{3,0,1,2:T(1,128)} copy(f32[1,36,128,128]{3,2,1,0:T(8,128)S(1)} %bitcast.207) | data formatting | bytes 4718592 | tf_op jit(solution)/shard_map/gather | solution.py:197
  138.0 4.3 %all-to-all-start.2 = ((f32[1,36,128,128]{3,0,1,2:T(1,128)}), f32[1,36,128,128]{3,0,1,2:T(1,128)S(1)}, u32[]{:S(2)}, u32[]{:S(2)}) async-start(f32[1,36,128,128]{3,0,1,2:T(1,128)} %copy.96), calls=%async_computation.2 | async-start | bytes 4718592 | tf_op jit(solution)/shard_map/all_to_all | solution.py:199
  147.4 2.0 select_maximum_fusion.1.x_ref
  149.3 2.0 copy.100
  151.4 2.9 maximum_multiply_fusion.1.x_ref
  154.3 14.8 %all-to-all-done.2 = f32[1,36,128,128]{3,0,1,2:T(1,128)S(1)} async-done(((f32[1,36,128,128]{3,0,1,2:T(1,128)}), f32[1,36,128,128]{3,0,1,2:T(1,128)S(1)}, u32[]{:S(2)}, u32[]{:S(2)}) %all-to-all-start.2) | async-done | bytes 2359328 | tf_op jit(solution)/shard_map/all_to_all | solution.py:199
  169.6 2.6 gather_fusion.1
  172.2 3.2 %bitcast_select_fusion = f32[64,96,128]{2,1,0:T(8,128)S(1)} fusion(pred[64,96]{1,0:T(8,128)(4,1)S(1)} %copy.85, f32[64,96,128]{2,1,0:T(8,128)} %bitcast.205), kind=kLoop, calls=%fused_computation.9 | loop fusion | flops 786432 | bytes 6297600 | tf_op jit(solution)/shard_map/jit(_where)/select_n | solution.py:221
  175.4 2.0 select_maximum_fusion
  177.3 15.1 %all-to-all-start.3 = ((f32[64,104,128]{2,1,0:T(8,128)}), f32[64,104,128]{2,1,0:T(8,128)S(1)}, u32[]{:S(2)}, u32[]{:S(2)}) async-start(f32[64,104,128]{2,1,0:T(8,128)} %select_maximum_fusion), calls=%async_computation.3 | async-start | bytes 6815744 | tf_op jit(solution)/shard_map/all_to_all | solution.py:228
  192.5 15.2 %shard_map.107 = f32[4,512,128]{2,1,0:T(8,128)} custom-call(f32[1,512,512]{2,1,0:T(8,128)} %select_maximum_fusion.1.x_ref), custom_call_target="tpu_custom_call" | custom-call | bytes 2097152 | tf_op jit(solution)/shard_map/pallas_call | solution.py:63
  207.7 25.5 %shard_map.108 = f32[4,1024,128]{2,1,0:T(8,128)} custom-call(f32[1,1024,512]{2,1,0:T(8,128)} %maximum_multiply_fusion.1.x_ref), custom_call_target="tpu_custom_call" | custom-call | bytes 4194304 | tf_op jit(solution)/shard_map/pallas_call | solution.py:63
  233.2 38.2 %all-to-all-done.3 = f32[64,104,128]{2,1,0:T(8,128)S(1)} async-done(((f32[64,104,128]{2,1,0:T(8,128)}), f32[64,104,128]{2,1,0:T(8,128)S(1)}, u32[]{:S(2)}, u32[]{:S(2)}) %all-to-all-start.3) | async-done | bytes 3407904 | tf_op jit(solution)/shard_map/all_to_all | solution.py:228
  271.4 2.1 slice.114
  275.1 4.7 %fusion = f32[4,2,32,128]{3,0,2,1:T(4,128)S(1)} fusion(f32[192,32,128]{2,1,0:T(8,128)} %bitcast.204, s32[4,2]{0,1:T(2,128)S(1)} %multiply_add_fusion, s32[192]{0:T(256)S(1)} %convert_element_type.31), kind=kOutput, calls=%fused_computation.7 | convolution fusion | flops 75499008 | bytes 3277600 | tf_op jit(solution)/shard_map/ri,rab->iab/dot_general | solution.py:238
  280.5 3.5 %all-to-all-start.4 = ((f32[4,2,32,128]{3,2,1,0:T(8,128)}), f32[4,2,32,128]{3,2,1,0:T(8,128)S(1)}, u32[]{:S(2)}, u32[]{:S(2)}) async-start(f32[4,2,32,128]{3,2,1,0:T(8,128)} %copy.102), calls=%async_computation.4 | async-start | bytes 262144 | tf_op jit(solution)/shard_map/all_to_all | solution.py:240
  283.9 5.7 %all-to-all-done.4 = f32[4,2,32,128]{3,2,1,0:T(8,128)S(1)} async-done(((f32[4,2,32,128]{3,2,1,0:T(8,128)}), f32[4,2,32,128]{3,2,1,0:T(8,128)S(1)}, u32[]{:S(2)}, u32[]{:S(2)}) %all-to-all-start.4) | async-done | bytes 131104 | tf_op jit(solution)/shard_map/all_to_all | solution.py:240
  (86 shorter events, 30.2 us)
Async XLA Ops:
  0.6 5.4 %copy-start.11 = (s32[36]{0:T(128)S(1)}, s32[36]{0:T(128)}, u32[]{:S(2)}) copy-start(s32[36]{0:T(128)} %constant.101) | copy-start | bytes 436
  0.6 4.2 %copy-start.12 = (s32[4]{0:T(128)S(1)}, s32[4]{0:T(128)}, u32[]{:S(2)}) copy-start(s32[4]{0:T(128)} %param.12) | copy-start | bytes 52
  0.7 18.3 %all-to-all-start.1 = ((f32[4,512,128]{2,1,0:T(8,128)}), f32[4,512,128]{2,1,0:T(8,128)S(1)}, u32[]{:S(2)}, u32[]{:S(2)}) async-start(f32[4,512,128]{2,1,0:T(8,128)} %param.10), calls=%async_computation.1 | async-start | bytes 2097152 | tf_op jit(solution)/shard_map/all_to_all | solution.py:182
  19.0 69.5 %all-to-all-start = ((f32[4,1024,128]{2,1,0:T(8,128)}), f32[4,1024,128]{2,1,0:T(8,128)}, u32[]{:S(2)}, u32[]{:S(2)}) async-start(f32[4,1024,128]{2,1,0:T(8,128)} %param.11), calls=%async_computation | async-start | bytes 4194304 | tf_op jit(solution)/shard_map/all_to_all | solution.py:183
  88.5 1.9 copy-start.5
  97.5 2.1 copy-start.6
  103.1 2.7 copy-start.8
  103.1 4.2 %copy-start.2 = (f32[1024,128]{0,1:T(8,128)S(1)}, f32[1024,128]{0,1:T(8,128)}, u32[]{:S(2)}) copy-start(f32[1024,128]{0,1:T(8,128)} %fusion.59) | copy-start | bytes 1572868
  103.1 4.2 %copy-start.3 = (f32[1024,128]{0,1:T(8,128)S(1)}, f32[1024,128]{0,1:T(8,128)}, u32[]{:S(2)}) copy-start(f32[1024,128]{0,1:T(8,128)} %fusion.60) | copy-start | bytes 1572868
  106.5 0.8 copy-start.1
  138.0 4.3 %copy-start.9 = (s32[144,1]{0,1:T(1,128)S(1)}, s32[144,1]{0,1:T(1,128)}, u32[]{:S(2)}) copy-start(s32[144,1]{0,1:T(1,128)} %param.13) | copy-start | bytes 1732
  138.0 5.2 %copy-start.10 = (s32[144]{0:T(256)S(1)}, s32[144]{0:T(256)}, u32[]{:S(2)}) copy-start(s32[144]{0:T(256)} %param.14) | copy-start | bytes 1732
  138.0 31.1 %all-to-all-start.2 = ((f32[1,36,128,128]{3,0,1,2:T(1,128)}), f32[1,36,128,128]{3,0,1,2:T(1,128)S(1)}, u32[]{:S(2)}, u32[]{:S(2)}) async-start(f32[1,36,128,128]{3,0,1,2:T(1,128)} %copy.96), calls=%async_computation.2 | async-start | bytes 4718592 | tf_op jit(solution)/shard_map/all_to_all | solution.py:199
  177.3 94.0 %all-to-all-start.3 = ((f32[64,104,128]{2,1,0:T(8,128)}), f32[64,104,128]{2,1,0:T(8,128)S(1)}, u32[]{:S(2)}, u32[]{:S(2)}) async-start(f32[64,104,128]{2,1,0:T(8,128)} %select_maximum_fusion), calls=%async_computation.3 | async-start | bytes 6815744 | tf_op jit(solution)/shard_map/all_to_all | solution.py:228
  273.5 16.2 %copy-start.7 = (f32[2,128,128]{2,1,0:T(8,128)S(1)}, f32[2,128,128]{2,1,0:T(8,128)}, u32[]{:S(2)}) copy-start(f32[2,128,128]{2,1,0:T(8,128)} %param.15) | copy-start | bytes 393220
  275.1 15.3 %copy-start.4 = (f32[4,512,128]{2,1,0:T(8,128)S(1)}, f32[4,512,128]{2,1,0:T(8,128)}, u32[]{:S(2)}) copy-start(f32[4,512,128]{2,1,0:T(8,128)} %shard_map.107) | copy-start | bytes 3145732
  279.8 11.5 %copy-start = (f32[4,1024,128]{2,1,0:T(8,128)S(1)}, f32[4,1024,128]{2,1,0:T(8,128)}, u32[]{:S(2)}) copy-start(f32[4,1024,128]{2,1,0:T(8,128)} %shard_map.108) | copy-start | bytes 6291460
  280.5 9.2 %all-to-all-start.4 = ((f32[4,2,32,128]{3,2,1,0:T(8,128)}), f32[4,2,32,128]{3,2,1,0:T(8,128)S(1)}, u32[]{:S(2)}, u32[]{:S(2)}) async-start(f32[4,2,32,128]{3,2,1,0:T(8,128)} %copy.102), calls=%async_computation.4 | async-start | bytes 262144 | tf_op jit(solution)/shard_map/all_to_all | solution.py:240

commit v6 on v4

--- a/solution.py
+++ b/solution.py
@@ -118,6 +118,51 @@
         out_specs=(pl.BlockSpec(memory_space=pltpu.VMEM), pl.BlockSpec(memory_space=pltpu.VMEM)),
         scratch_shapes=[pltpu.VMEM((n, n), jnp.float32)] * 3,
     )(a)
+
+
+def chunks_out_kernel(x_ref, y_ref, send_sem, recv_sem, own_sem, *, count):
+    me = lax.axis_index("narrow")
+    wide = lax.axis_index("wide")
+    barrier = pltpu.get_barrier_semaphore()
+    for d in range(1, count):
+        peer = lax.rem(me + d, count)
+        pl.semaphore_signal(barrier, inc=1, device_id=(wide, peer), device_id_type=MESH)
+    pl.semaphore_wait(barrier, count - 1)
+    own = pltpu.make_async_copy(x_ref.at[me], y_ref.at[me], own_sem)
+    own.start()
+    copies = []
+    for d in range(1, count):
+        peer = lax.rem(me + d, count)
+        copy = pltpu.make_async_remote_copy(
+            src_ref=x_ref.at[peer],
+            dst_ref=y_ref.at[me],
+            send_sem=send_sem.at[d - 1],
+            recv_sem=recv_sem.at[d - 1],
+            device_id=(wide, peer),
+            device_id_type=MESH,
+        )
+        copy.start()
+        copies.append(copy)
+    own.wait()
+    for copy in copies:
+        copy.wait()
+
+
+def chunks_out(x, collective_id):
+    count = x.shape[0]
+    return pl.pallas_call(
+        functools.partial(chunks_out_kernel, count=count),
+        out_shape=jax.ShapeDtypeStruct(x.shape, x.dtype),
+        in_specs=[pl.BlockSpec(memory_space=pl.ANY)],
+        out_specs=pl.BlockSpec(memory_space=pl.ANY),
+        scratch_shapes=[
+            pltpu.SemaphoreType.DMA((count - 1,)),
+            pltpu.SemaphoreType.DMA((count - 1,)),
+            pltpu.SemaphoreType.DMA,
+        ],
+        compiler_params=pltpu.CompilerParams(collective_id=collective_id, has_side_effects=True),
+        cost_estimate=pl.CostEstimate(flops=0, bytes_accessed=2 * x.size * 4, transcendentals=0),
+    )(x)
 
 
 def mm(a, b):
@@ -238,8 +283,8 @@
     )
     slot_sums = jnp.einsum("ri,rab->iab", slot_table, received, precision=lax.Precision.HIGHEST)
     slot_sums = slot_sums.reshape(narrow_count, T_DEV, quarter_rows, B)
-    summed = lax.all_to_all(slot_sums, "narrow", split_axis=0, concat_axis=2, tiled=True)
-    summed = summed.reshape(T_DEV, B, B)
+    arrived = chunks_out(slot_sums, 2)
+    summed = jnp.swapaxes(arrived, 0, 1).reshape(T_DEV, B, B)
     return (factor_back, lower_back, ancestor - summed)
 
 

time: 287 us -> 285 us (level)
  waiting for transfers between devices: 75.3 us -> 69.5 us
  Pallas kernels: 97.4 us -> 103 us
  starting transfers between devices: 30.5 us -> 27.2 us
    pallas_call x0 -> x1, Pallas kernels: none -> 5.95 us  [chunks_out(): pl.pallas_call(functools.partial(chunks_out_kernel, count=count), out_sha...]
    all_to_all x1 -> x0, waiting for transfers between devices: 5.74 us -> none  [local(): lax.all_to_all(slot_sums, 'narrow', split_axis=0, concat_axis=2, tiled=True)]
    all_to_all x1 -> x0, starting transfers between devices: 3.33 us -> none  [local(): lax.all_to_all(slot_sums, 'narrow', split_axis=0, concat_axis=2, tiled=True)]
  transfers between devices with their start and end apart: 5 -> 4, of which waited for: 4 -> 3; matrix products, arithmetic and copies ran while one was open for 11% -> 11% of each run, Pallas kernels for 34% -> 34%
where the time goes in v6:
time: 285 us; the launch traced here: 283 us
  Pallas kernels  103 us (36%)
  waiting for transfers between devices  69.5 us (24%)
  local copies, waits for them, and re-layouts  39.1 us (14%)
  matrix products  33.4 us (12%)
  starting transfers between devices  27.2 us (10%)
  other arithmetic  9.66 us (3%)
    pallas_call x4, Pallas kernels, block_chol(): pl.pallas_call(block_chol_kernel, out_shape=(jax.ShapeDtypeStruct((n, n),...  56.6 us
    pallas_call x2, Pallas kernels, columns_out(): pl.pallas_call(functools.partial(columns_out_kernel, count=count, group=g...  40.7 us
    all_to_all x1, waiting for transfers between devices, local(): lax.all_to_all(send_buffer, 'wide', split_axis=0, concat_axis=0, tiled=True)  38.2 us
    all_to_all x1, waiting for transfers between devices, local(): lax.all_to_all(contribution, 'narrow', split_axis=2, concat_axis=0, tiled...  20.8 us
    all_to_all x1, starting transfers between devices, local(): lax.all_to_all(send_buffer, 'wide', split_axis=0, concat_axis=0, tiled=True)  15.1 us
    all_to_all x1, waiting for transfers between devices, local(): lax.all_to_all(diag_block, 'narrow', split_axis=0, concat_axis=2, tiled=T...  10.5 us
    dot_general x1, matrix products, local(): jnp.einsum('siac,sjbc->sijab', blocks, blocks, precision=lax.Precision.HI...  8.96 us
    dot_general x6, matrix products, mm_t(): return jnp.einsum('sik,sjk->sij', a, b, precision=lax.Precision.HIGHEST)  7.49 us
  transfers between devices with their start and end apart: 4, of which 3 were waited for; matrix products, arithmetic and copies ran while one was open for 11% of the time, Pallas kernels for 34%

profile of v6, /device:TPU:9, one launch (start us, length us, event | category | flops | bytes accessed | tf_op | source)
XLA Modules:
  0.0 283.4 jit_solution(15392072731526106046)
XLA Ops:
  0.7 4.2 %all-to-all-start = ((f32[4,512,128]{2,1,0:T(8,128)}), f32[4,512,128]{2,1,0:T(8,128)S(1)}, u32[]{:S(2)}, u32[]{:S(2)}) async-start(f32[4,512,128]{2,1,0:T(8,128)} %param.10), calls=%async_computation | async-start | bytes 2097152 | tf_op jit(solution)/shard_map/all_to_all | solution.py:226
  4.8 1.8 copy.70
  8.5 10.5 %all-to-all-done = f32[4,512,128]{2,1,0:T(8,128)S(1)} async-done(((f32[4,512,128]{2,1,0:T(8,128)}), f32[4,512,128]{2,1,0:T(8,128)S(1)}, u32[]{:S(2)}, u32[]{:S(2)}) %all-to-all-start) | async-done | bytes 1048608 | tf_op jit(solution)/shard_map/all_to_all | solution.py:226
  19.0 3.6 %all-to-all-start.1 = ((f32[4,1024,128]{1,2,0:T(8,128)}), f32[4,1024,128]{1,2,0:T(8,128)S(1)}, u32[]{:S(2)}, u32[]{:S(2)}) async-start(f32[4,1024,128]{1,2,0:T(8,128)} %copy.70), calls=%async_computation.1 | async-start | bytes 4194304 | tf_op jit(solution)/shard_map/all_to_all | solution.py:227
  24.4 14.2 %shard_map.103 = (f32[128,128]{1,0:T(8,128)}, f32[128,128]{1,0:T(8,128)}) custom-call(f32[128,128]{1,0:T(8,128)} %slice_bitcast_fusion.10.a_ref), custom_call_target="tpu_custom_call" | custom-call | tf_op jit(solution)/shard_map/pallas_call | solution.py:114
  38.5 1.4 fusion.37
  40.0 1.7 fusion.3
  42.4 14.2 %shard_map.104 = (f32[128,128]{1,0:T(8,128)}, f32[128,128]{1,0:T(8,128)}) custom-call(f32[128,128]{1,0:T(8,128)} %slice_bitcast_fusion.9.a_ref), custom_call_target="tpu_custom_call" | custom-call | tf_op jit(solution)/shard_map/pallas_call | solution.py:114
  62.2 1.6 fusion.72
  67.2 14.2 %shard_map.105 = (f32[128,128]{1,0:T(8,128)}, f32[128,128]{1,0:T(8,128)}) custom-call(f32[128,128]{1,0:T(8,128)} %slice_bitcast_fusion.6.a_ref), custom_call_target="tpu_custom_call" | custom-call | tf_op jit(solution)/shard_map/pallas_call | solution.py:114
  81.4 1.4 convolution_bitcast_fusion.3
  83.9 1.5 fusion.4
  86.1 1.7 fusion.9.a_ref
  87.8 14.2 %shard_map.106 = (f32[128,128]{1,0:T(8,128)}, f32[128,128]{1,0:T(8,128)}) custom-call(f32[128,128]{1,0:T(8,128)} %fusion.9.a_ref), custom_call_target="tpu_custom_call" | custom-call | tf_op jit(solution)/shard_map/pallas_call | solution.py:114
  102.0 1.4 convolution_bitcast_fusion.2
  104.7 5.1 %convolution_multiply_fusion = f32[512,1024]{0,1:T(8,128)S(1)} fusion(f32[1024,512]{0,1:T(8,128)} %bitcast.186, f32[1,128,512]{2,1,0:T(8,128)S(1)} %convolution_bitcast_fusion.2, f32[1,128,512]{2,1,0:T(8,128)S(1)} %convolution_bitcast_fusion.3, f32[1,128,512]{2,1,0:T(8,128)S(1)} %convolution_bitcast_fusion.5, f32[1,128,512]{2,1,0:T(8,128)S(1)} %concatenate.47, ...), kind=kOutput, calls=%fused_computation.12 | convolution fusion | flops 3222536192 | bytes 5246976 | tf_op jit(solution)/shard_map/srk,sck->src/dot_general | solution.py:230
  109.9 9.0 %convolution_bitcast_fusion = f32[1,8,8,128,128]{3,4,1,2,0:T(8,128)} fusion(f32[8,128,512,1]{2,1,3,0:T(8,128)S(1)} %bitcast.177, f32[8,128,512,1]{2,1,0,3:T(8,128)S(1)} %bitcast.178), kind=kOutput, calls=%fused_computation.11 | convolution fusion | flops 6442450944 | bytes 8388608 | tf_op jit(solution)/shard_map/siac,sjbc->sijab/dot_general | solution.py:241
  118.8 5.4 %copy.72 = f32[1,8,8,128,128]{4,3,2,1,0:T(8,128)} copy(f32[1,8,8,128,128]{3,4,1,2,0:T(8,128)} %convolution_bitcast_fusion) | data formatting | bytes 8388608 | tf_op jit(solution)/shard_map/siac,sjbc->sijab/transpose | solution.py:241
  124.2 2.9 %gather_fusion = f32[36,128,128]{2,1,0:T(8,128)S(1)} fusion(f32[64,128,128]{2,1,0:T(8,128)} %bitcast.183, s32[1024]{0:T(1024)S(1)} %pad_clamp_fusion.1), kind=kCustom, calls=%fused_computation | custom fusion | bytes 4718736 | tf_op jit(solution)/shard_map/gather | solution.py:243
  127.1 3.8 %copy.73 = f32[1,36,128,128]{3,0,1,2:T(1,128)} copy(f32[1,36,128,128]{3,2,1,0:T(8,128)S(1)} %bitcast.184) | data formatting | bytes 4718592 | tf_op jit(solution)/shard_map/gather | solution.py:243
  131.0 4.3 %all-to-all-start.2 = ((f32[1,36,128,128]{3,0,1,2:T(1,128)}), f32[1,36,128,128]{3,0,1,2:T(1,128)S(1)}, u32[]{:S(2)}, u32[]{:S(2)}) async-start(f32[1,36,128,128]{3,0,1,2:T(1,128)} %copy.73), calls=%async_computation.2 | async-start | bytes 4718592 | tf_op jit(solution)/shard_map/all_to_all | solution.py:245
  141.3 20.8 %all-to-all-done.2 = f32[1,36,128,128]{3,0,1,2:T(1,128)S(1)} async-done(((f32[1,36,128,128]{3,0,1,2:T(1,128)}), f32[1,36,128,128]{3,0,1,2:T(1,128)S(1)}, u32[]{:S(2)}, u32[]{:S(2)}) %all-to-all-start.2) | async-done | bytes 2359328 | tf_op jit(solution)/shard_map/all_to_all | solution.py:245
  162.6 2.6 gather_fusion.1
  165.2 3.2 %bitcast_select_fusion = f32[64,96,128]{2,1,0:T(8,128)S(1)} fusion(pred[64,96]{1,0:T(8,128)(4,1)S(1)} %copy.66, f32[64,96,128]{2,1,0:T(8,128)} %bitcast.182), kind=kLoop, calls=%fused_computation.9 | loop fusion | flops 786432 | bytes 6297600 | tf_op jit(solution)/shard_map/jit(_where)/select_n | solution.py:267
  168.4 1.9 select_maximum_fusion
  170.3 15.1 %all-to-all-start.3 = ((f32[64,104,128]{2,1,0:T(8,128)}), f32[64,104,128]{2,1,0:T(8,128)S(1)}, u32[]{:S(2)}, u32[]{:S(2)}) async-start(f32[64,104,128]{2,1,0:T(8,128)} %select_maximum_fusion), calls=%async_computation.3 | async-start | bytes 6815744 | tf_op jit(solution)/shard_map/all_to_all | solution.py:274
  185.4 26.4 %shard_map.108 = f32[4,1024,128]{2,1,0:T(8,128)} custom-call(f32[1,1024,512]{2,1,0:T(8,128)} %bitcast.179), custom_call_target="tpu_custom_call" | custom-call | bytes 4194304 | tf_op jit(solution)/shard_map/pallas_call | solution.py:63
  211.9 14.3 %shard_map.107 = f32[4,512,128]{2,1,0:T(8,128)} custom-call(f32[1,512,512]{2,1,0:T(8,128)} %select_maximum_fusion.1.x_ref), custom_call_target="tpu_custom_call" | custom-call | bytes 2097152 | tf_op jit(solution)/shard_map/pallas_call | solution.py:63
  226.1 38.2 %all-to-all-done.3 = f32[64,104,128]{2,1,0:T(8,128)S(1)} async-done(((f32[64,104,128]{2,1,0:T(8,128)}), f32[64,104,128]{2,1,0:T(8,128)S(1)}, u32[]{:S(2)}, u32[]{:S(2)}) %all-to-all-start.3) | async-done | bytes 3407904 | tf_op jit(solution)/shard_map/all_to_all | solution.py:274
  264.4 2.0 slice.118
  268.1 4.8 %fusion = f32[4,2,32,128]{3,0,2,1:T(4,128)S(1)} fusion(f32[192,32,128]{2,1,0:T(8,128)} %bitcast.181, s32[4,2]{0,1:T(2,128)S(1)} %multiply_add_fusion, s32[192]{0:T(256)S(1)} %convert_element_type.46), kind=kOutput, calls=%fused_computation.7 | convolution fusion | flops 75499008 | bytes 3277600 | tf_op jit(solution)/shard_map/ri,rab->iab/dot_general | solution.py:284
  273.5 5.9 %shard_map.109 = f32[4,2,32,128]{3,2,1,0:T(8,128)} custom-call(f32[4,2,32,128]{3,2,1,0:T(8,128)} %copy.78.x_ref), custom_call_target="tpu_custom_call" | custom-call | bytes 262144 | tf_op jit(solution)/shard_map/pallas_call | solution.py:153
  (94 shorter events, 29.1 us)
Async XLA Ops:
  0.6 7.2 %copy-start.16 = (s32[36]{0:T(128)S(1)}, s32[36]{0:T(128)}, u32[]{:S(2)}) copy-start(s32[36]{0:T(128)} %constant.104) | copy-start | bytes 436
  0.6 4.2 %copy-start.5 = (f32[4,1024,128]{2,1,0:T(8,128)S(1)}, f32[4,1024,128]{2,1,0:T(8,128)}, u32[]{:S(2)}) copy-start(f32[4,1024,128]{2,1,0:T(8,128)} %param.11) | copy-start | bytes 6291460
  0.7 6.0 %copy-start.17 = (s32[4]{0:T(128)S(1)}, s32[4]{0:T(128)}, u32[]{:S(2)}) copy-start(s32[4]{0:T(128)} %param.12) | copy-start | bytes 52
  0.7 18.3 %all-to-all-start = ((f32[4,512,128]{2,1,0:T(8,128)}), f32[4,512,128]{2,1,0:T(8,128)S(1)}, u32[]{:S(2)}, u32[]{:S(2)}) async-start(f32[4,512,128]{2,1,0:T(8,128)} %param.10), calls=%async_computation | async-start | bytes 2097152 | tf_op jit(solution)/shard_map/all_to_all | solution.py:226
  19.0 84.4 %all-to-all-start.1 = ((f32[4,1024,128]{1,2,0:T(8,128)}), f32[4,1024,128]{1,2,0:T(8,128)S(1)}, u32[]{:S(2)}, u32[]{:S(2)}) async-start(f32[4,1024,128]{1,2,0:T(8,128)} %copy.70), calls=%async_computation.1 | async-start | bytes 4194304 | tf_op jit(solution)/shard_map/all_to_all | solution.py:227
  22.8 1.0 copy-start.4
  38.5 22.3 %copy-start.8 = (f32[128,128]{1,0:T(8,128)S(1)}, f32[128,128]{1,0:T(8,128)}, u32[]{:S(2)}) copy-start(f32[128,128]{1,0:T(8,128)} %get-tuple-element.29) | copy-start | bytes 196612
  65.9 0.7 copy-start.7
  103.4 1.3 copy-start.1
  109.8 9.0 %copy-start = (f32[512,1024]{0,1:T(8,128)}, f32[512,1024]{0,1:T(8,128)S(1)}, u32[]{:S(2)}) copy-start(f32[512,1024]{0,1:T(8,128)S(1)} %convolution_multiply_fusion) | copy-start | bytes 6291460
  130.9 4.4 %copy-start.14 = (s32[144,1]{0,1:T(1,128)S(1)}, s32[144,1]{0,1:T(1,128)}, u32[]{:S(2)}) copy-start(s32[144,1]{0,1:T(1,128)} %param.13) | copy-start | bytes 1732
  130.9 7.9 %copy-start.15 = (s32[144]{0:T(256)S(1)}, s32[144]{0:T(256)}, u32[]{:S(2)}) copy-start(s32[144]{0:T(256)} %param.14) | copy-start | bytes 1732
  130.9 9.2 %copy-start.6 = (f32[256,128]{1,0:T(8,128)S(1)}, f32[256,128]{1,0:T(8,128)}, u32[]{:S(2)}) copy-start(f32[256,128]{1,0:T(8,128)} %copy.69) | copy-start | bytes 393220
  130.9 9.2 %copy-start.10 = (f32[128,128]{1,0:T(8,128)S(1)}, f32[128,128]{1,0:T(8,128)}, u32[]{:S(2)}) copy-start(f32[128,128]{1,0:T(8,128)} %get-tuple-element.33) | copy-start | bytes 196612
  131.0 9.2 %copy-start.11 = (f32[128,128]{1,0:T(8,128)S(1)}, f32[128,128]{1,0:T(8,128)}, u32[]{:S(2)}) copy-start(f32[128,128]{1,0:T(8,128)} %get-tuple-element.34) | copy-start | bytes 196612
  131.0 9.2 %copy-start.12 = (f32[128,128]{1,0:T(8,128)S(1)}, f32[128,128]{1,0:T(8,128)}, u32[]{:S(2)}) copy-start(f32[128,128]{1,0:T(8,128)} %get-tuple-element.35) | copy-start | bytes 196612
  131.0 9.2 %copy-start.13 = (f32[128,128]{1,0:T(8,128)S(1)}, f32[128,128]{1,0:T(8,128)}, u32[]{:S(2)}) copy-start(f32[128,128]{1,0:T(8,128)} %get-tuple-element.36) | copy-start | bytes 196612
  131.0 31.1 %all-to-all-start.2 = ((f32[1,36,128,128]{3,0,1,2:T(1,128)}), f32[1,36,128,128]{3,0,1,2:T(1,128)S(1)}, u32[]{:S(2)}, u32[]{:S(2)}) async-start(f32[1,36,128,128]{3,0,1,2:T(1,128)} %copy.73), calls=%async_computation.2 | async-start | bytes 4718592 | tf_op jit(solution)/shard_map/all_to_all | solution.py:245
  170.3 94.0 %all-to-all-start.3 = ((f32[64,104,128]{2,1,0:T(8,128)}), f32[64,104,128]{2,1,0:T(8,128)S(1)}, u32[]{:S(2)}, u32[]{:S(2)}) async-start(f32[64,104,128]{2,1,0:T(8,128)} %select_maximum_fusion), calls=%async_computation.3 | async-start | bytes 6815744 | tf_op jit(solution)/shard_map/all_to_all | solution.py:274
  266.4 14.0 %copy-start.9 = (f32[2,128,128]{2,1,0:T(8,128)S(1)}, f32[2,128,128]{2,1,0:T(8,128)}, u32[]{:S(2)}) copy-start(f32[2,128,128]{2,1,0:T(8,128)} %param.15) | copy-start | bytes 393220
  267.1 14.0 %copy-start.3 = (f32[4,512,128]{2,1,0:T(8,128)S(1)}, f32[4,512,128]{2,1,0:T(8,128)}, u32[]{:S(2)}) copy-start(f32[4,512,128]{2,1,0:T(8,128)} %shard_map.107) | copy-start | bytes 3145732
  268.1 14.0 %copy-start.2 = (f32[4,1024,128]{2,1,0:T(8,128)S(1)}, f32[4,1024,128]{2,1,0:T(8,128)}, u32[]{:S(2)}) copy-start(f32[4,1024,128]{2,1,0:T(8,128)} %shard_map.108) | copy-start | bytes 6291460

commit v7 on v6

--- a/solution.py
+++ b/solution.py
@@ -153,6 +153,55 @@
     return pl.pallas_call(
         functools.partial(chunks_out_kernel, count=count),
         out_shape=jax.ShapeDtypeStruct(x.shape, x.dtype),
+        in_specs=[pl.BlockSpec(memory_space=pl.ANY)],
+        out_specs=pl.BlockSpec(memory_space=pl.ANY),
+        scratch_shapes=[
+            pltpu.SemaphoreType.DMA((count - 1,)),
+            pltpu.SemaphoreType.DMA((count - 1,)),
+            pltpu.SemaphoreType.DMA,
+        ],
+        compiler_params=pltpu.CompilerParams(collective_id=collective_id, has_side_effects=True),
+        cost_estimate=pl.CostEstimate(flops=0, bytes_accessed=2 * x.size * 4, transcendentals=0),
+    )(x)
+
+
+def quarters_out_kernel(x_ref, y_ref, send_sem, recv_sem, own_sem, *, count, group, height):
+    me = lax.axis_index("narrow")
+    wide = lax.axis_index("wide")
+    barrier = pltpu.get_barrier_semaphore()
+    for d in range(1, count):
+        peer = lax.rem(me + d, count)
+        pl.semaphore_signal(barrier, inc=1, device_id=(wide, peer), device_id_type=MESH)
+    pl.semaphore_wait(barrier, count - 1)
+    mine = y_ref.at[pl.ds(me * group, group)]
+    own = pltpu.make_async_copy(
+        x_ref.at[:, :, pl.ds(pl.multiple_of(me * height, height), height), :], mine, own_sem
+    )
+    own.start()
+    copies = []
+    for d in range(1, count):
+        peer = lax.rem(me + d, count)
+        copy = pltpu.make_async_remote_copy(
+            src_ref=x_ref.at[:, :, pl.ds(pl.multiple_of(peer * height, height), height), :],
+            dst_ref=mine,
+            send_sem=send_sem.at[d - 1],
+            recv_sem=recv_sem.at[d - 1],
+            device_id=(wide, peer),
+            device_id_type=MESH,
+        )
+        copy.start()
+        copies.append(copy)
+    own.wait()
+    for copy in copies:
+        copy.wait()
+
+
+def quarters_out(x, count, collective_id):
+    group, pairs, rows, width = x.shape
+    height = rows // count
+    return pl.pallas_call(
+        functools.partial(quarters_out_kernel, count=count, group=group, height=height),
+        out_shape=jax.ShapeDtypeStruct((group * count, pairs, height, width), x.dtype),
         in_specs=[pl.BlockSpec(memory_space=pl.ANY)],
         out_specs=pl.BlockSpec(memory_space=pl.ANY),
         scratch_shapes=[
@@ -242,7 +291,7 @@
     gram = gram.reshape(group, P_SIZE * P_SIZE, B, B)
     contribution = gram[:, first * P_SIZE + second]
 
-    quarters = lax.all_to_all(contribution, "narrow", split_axis=2, concat_axis=0, tiled=True)
+    quarters = quarters_out(contribution, narrow_count, 3)
     quarter_rows = quarters.shape[2]
     pair_rows = supers_here * npair
     quarters = quarters.reshape(pair_rows, quarter_rows, B)

time: 285 us -> 278 us (0.975)
  Pallas kernels: 103 us -> 134 us
  waiting for transfers between devices: 69.5 us -> 39.2 us
  starting transfers between devices: 27.2 us -> 21.6 us
    pallas_call x0 -> x1, Pallas kernels: none -> 29 us  [quarters_out(): pl.pallas_call(functools.partial(quarters_out_kernel, count=count, group=...]
    all_to_all x1 -> x0, waiting for transfers between devices: 20.8 us -> none  [local(): lax.all_to_all(contribution, 'narrow', split_axis=2, concat_axis=0, tiled...]
    all_to_all x1, waiting for transfers between devices: 10.5 us -> 2.5 us  [local(): lax.all_to_all(diag_block, 'narrow', split_axis=0, concat_axis=2, tiled=T...]
    all_to_all x1 -> x0, starting transfers between devices: 4.35 us -> none  [local(): lax.all_to_all(contribution, 'narrow', split_axis=2, concat_axis=0, tiled...]
    gather x2 -> x1, local copies, waits for them, and re-layouts: 6.72 us -> 4.44 us  [local(): contribution = gram[:, first * P_SIZE + second]]
    unnamed x39 -> x29, local copies, waits for them, and re-layouts: 7.14 us -> 7.13 us
  transfers between devices with their start and end apart: 4 -> 3, of which waited for: 3 -> 2; matrix products, arithmetic and copies ran while one was open for 11% -> 13% of each run, Pallas kernels for 34% -> 36%
where the time goes in v7:
time: 278 us; the launch traced here: 277 us
  Pallas kernels  134 us (48%)
  waiting for transfers between devices  39.2 us (14%)
  local copies, waits for them, and re-layouts  36.7 us (13%)
  matrix products  33.3 us (12%)
  starting transfers between devices  21.6 us (8%)
  other arithmetic  11.3 us (4%)
    pallas_call x4, Pallas kernels, block_chol(): pl.pallas_call(block_chol_kernel, out_shape=(jax.ShapeDtypeStruct((n, n),...  56.6 us
    pallas_call x2, Pallas kernels, columns_out(): pl.pallas_call(functools.partial(columns_out_kernel, count=count, group=g...  42.2 us
    all_to_all x1, waiting for transfers between devices, local(): lax.all_to_all(send_buffer, 'wide', split_axis=0, concat_axis=0, tiled=True)  36.7 us
    pallas_call x1, Pallas kernels, quarters_out(): pl.pallas_call(functools.partial(quarters_out_kernel, count=count, group=...  29 us
    all_to_all x1, starting transfers between devices, local(): lax.all_to_all(send_buffer, 'wide', split_axis=0, concat_axis=0, tiled=True)  13.9 us
    dot_general x1, matrix products, local(): jnp.einsum('siac,sjbc->sijab', blocks, blocks, precision=lax.Precision.HI...  8.88 us
    dot_general x6, matrix products, mm_t(): return jnp.einsum('sik,sjk->sij', a, b, precision=lax.Precision.HIGHEST)  7.48 us
    unnamed x29, local copies, waits for them, and re-layouts  7.13 us
  transfers between devices with their start and end apart: 3, of which 2 were waited for; matrix products, arithmetic and copies ran while one was open for 13% of the time, Pallas kernels for 36%

profile of v7, /device:TPU:9, one launch (start us, length us, event | category | flops | bytes accessed | tf_op | source)
XLA Modules:
  0.0 277.0 jit_solution(4410647840015370630)
XLA Ops:
  0.7 4.2 %all-to-all-start = ((f32[4,512,128]{2,1,0:T(8,128)}), f32[4,512,128]{2,1,0:T(8,128)S(1)}, u32[]{:S(2)}, u32[]{:S(2)}) async-start(f32[4,512,128]{2,1,0:T(8,128)} %param.10), calls=%async_computation | async-start | bytes 2097152 | tf_op jit(solution)/shard_map/all_to_all | solution.py:275
  7.9 1.8 copy.23
  16.5 2.5 all-to-all-done
  19.0 3.6 %all-to-all-start.1 = ((f32[4,1024,128]{1,2,0:T(8,128)}), f32[4,1024,128]{1,2,0:T(8,128)S(1)}, u32[]{:S(2)}, u32[]{:S(2)}) async-start(f32[4,1024,128]{1,2,0:T(8,128)} %copy.23), calls=%async_computation.1 | async-start | bytes 4194304 | tf_op jit(solution)/shard_map/all_to_all | solution.py:276
  24.4 14.2 %shard_map.103 = (f32[128,128]{1,0:T(8,128)}, f32[128,128]{1,0:T(8,128)}) custom-call(f32[128,128]{1,0:T(8,128)} %slice_bitcast_fusion.10.a_ref), custom_call_target="tpu_custom_call" | custom-call | tf_op jit(solution)/shard_map/pallas_call | solution.py:114
  38.5 1.4 fusion.37
  42.4 1.7 fusion.3
  44.8 14.2 %shard_map.104 = (f32[128,128]{1,0:T(8,128)}, f32[128,128]{1,0:T(8,128)}) custom-call(f32[128,128]{1,0:T(8,128)} %slice_bitcast_fusion.9.a_ref), custom_call_target="tpu_custom_call" | custom-call | tf_op jit(solution)/shard_map/pallas_call | solution.py:114
  60.8 1.3 convolution_bitcast_fusion.5
  62.2 1.5 fusion.72
  67.2 14.2 %shard_map.105 = (f32[128,128]{1,0:T(8,128)}, f32[128,128]{1,0:T(8,128)}) custom-call(f32[128,128]{1,0:T(8,128)} %slice_bitcast_fusion.6.a_ref), custom_call_target="tpu_custom_call" | custom-call | tf_op jit(solution)/shard_map/pallas_call | solution.py:114
  81.3 1.4 convolution_bitcast_fusion.3
  83.8 1.5 fusion.4
  86.0 1.7 fusion.9.a_ref
  87.8 14.2 %shard_map.106 = (f32[128,128]{1,0:T(8,128)}, f32[128,128]{1,0:T(8,128)}) custom-call(f32[128,128]{1,0:T(8,128)} %fusion.9.a_ref), custom_call_target="tpu_custom_call" | custom-call | tf_op jit(solution)/shard_map/pallas_call | solution.py:114
  101.9 1.4 convolution_bitcast_fusion.2
  103.3 2.1 select_maximum_fusion.1.x_ref
  106.7 5.1 %convolution_multiply_fusion = f32[512,1024]{0,1:T(8,128)S(1)} fusion(f32[1024,512]{0,1:T(8,128)} %bitcast.182, f32[1,128,512]{2,1,0:T(8,128)S(1)} %convolution_bitcast_fusion.2, f32[1,128,512]{2,1,0:T(8,128)S(1)} %convolution_bitcast_fusion.3, f32[1,128,512]{2,1,0:T(8,128)S(1)} %convolution_bitcast_fusion.5, f32[1,128,512]{2,1,0:T(8,128)S(1)} %concatenate.47, ...), kind=kOutput, calls=%fused_computation.12 | convolution fusion | flops 3222536192 | bytes 5246976 | tf_op jit(solution)/shard_map/srk,sck->src/dot_general | solution.py:279
  111.9 8.9 %convolution_bitcast_fusion = f32[1,8,8,128,128]{3,4,1,2,0:T(8,128)} fusion(f32[8,128,512,1]{2,1,3,0:T(8,128)S(1)} %bitcast.174, f32[8,128,512,1]{2,1,0,3:T(8,128)S(1)} %bitcast.175), kind=kOutput, calls=%fused_computation.11 | convolution fusion | flops 6442450944 | bytes 8388608 | tf_op jit(solution)/shard_map/siac,sjbc->sijab/dot_general | solution.py:290
  120.8 5.4 %copy.25 = f32[1,8,8,128,128]{4,3,2,1,0:T(8,128)} copy(f32[1,8,8,128,128]{3,4,1,2,0:T(8,128)} %convolution_bitcast_fusion) | data formatting | bytes 8388608 | tf_op jit(solution)/shard_map/siac,sjbc->sijab/transpose | solution.py:290
  126.1 4.4 %gather_fusion = f32[36,128,128]{2,1,0:T(8,128)} fusion(f32[64,128,128]{2,1,0:T(8,128)} %bitcast.180, s32[1024]{0:T(1024)} %pad_clamp_fusion.1), kind=kCustom, calls=%fused_computation | custom fusion | bytes 4718736 | tf_op jit(solution)/shard_map/gather | solution.py:292
  130.6 29.0 %shard_map.107 = f32[4,36,32,128]{3,2,1,0:T(8,128)} custom-call(f32[1,36,128,128]{3,2,1,0:T(8,128)} %bitcast.181), custom_call_target="tpu_custom_call" | custom-call | bytes 4718592 | tf_op jit(solution)/shard_map/pallas_call | solution.py:202
  159.6 2.4 gather_fusion.1
  163.2 2.0 select_maximum_fusion
  165.1 13.9 %all-to-all-start.2 = ((f32[64,104,128]{2,1,0:T(8,128)}), f32[64,104,128]{2,1,0:T(8,128)S(1)}, u32[]{:S(2)}, u32[]{:S(2)}) async-start(f32[64,104,128]{2,1,0:T(8,128)} %select_maximum_fusion), calls=%async_computation.2 | async-start | bytes 6815744 | tf_op jit(solution)/shard_map/all_to_all | solution.py:323
  179.0 26.4 %shard_map.109 = f32[4,1024,128]{2,1,0:T(8,128)} custom-call(f32[1,1024,512]{2,1,0:T(8,128)} %bitcast.176), custom_call_target="tpu_custom_call" | custom-call | bytes 4194304 | tf_op jit(solution)/shard_map/pallas_call | solution.py:63
  205.4 15.8 %shard_map.108 = f32[4,512,128]{2,1,0:T(8,128)} custom-call(f32[1,512,512]{2,1,0:T(8,128)} %select_maximum_fusion.1.x_ref), custom_call_target="tpu_custom_call" | custom-call | bytes 2097152 | tf_op jit(solution)/shard_map/pallas_call | solution.py:63
  221.2 36.7 %all-to-all-done.2 = f32[64,104,128]{2,1,0:T(8,128)S(1)} async-done(((f32[64,104,128]{2,1,0:T(8,128)}), f32[64,104,128]{2,1,0:T(8,128)S(1)}, u32[]{:S(2)}, u32[]{:S(2)}) %all-to-all-start.2) | async-done | bytes 3407904 | tf_op jit(solution)/shard_map/all_to_all | solution.py:323
  257.9 2.1 slice.118
  261.7 4.8 %fusion = f32[4,2,32,128]{3,0,2,1:T(4,128)S(1)} fusion(f32[192,32,128]{2,1,0:T(8,128)} %bitcast.178, s32[4,2]{0,1:T(2,128)S(1)} %multiply_add_fusion, s32[192]{0:T(256)S(1)} %convert_element_type.46), kind=kOutput, calls=%fused_computation.7 | convolution fusion | flops 75499008 | bytes 3277600 | tf_op jit(solution)/shard_map/ri,rab->iab/dot_general | solution.py:333
  267.1 5.9 %shard_map.110 = f32[4,2,32,128]{3,2,1,0:T(8,128)} custom-call(f32[4,2,32,128]{3,2,1,0:T(8,128)} %copy.28.x_ref), custom_call_target="tpu_custom_call" | custom-call | bytes 262144 | tf_op jit(solution)/shard_map/pallas_call | solution.py:153
  275.7 1.3 copy.47
  (80 shorter events, 29.2 us)
Async XLA Ops:
  0.6 14.6 %copy-start.11 = (s32[36]{0:T(128)S(1)}, s32[36]{0:T(128)}, u32[]{:S(2)}) copy-start(s32[36]{0:T(128)} %constant.104) | copy-start | bytes 436
  0.6 7.2 %copy-start.5 = (f32[4,1024,128]{2,1,0:T(8,128)S(1)}, f32[4,1024,128]{2,1,0:T(8,128)}, u32[]{:S(2)}) copy-start(f32[4,1024,128]{2,1,0:T(8,128)} %param.11) | copy-start | bytes 6291460
  0.7 11.6 %copy-start.10 = (s32[144]{0:T(256)S(1)}, s32[144]{0:T(256)}, u32[]{:S(2)}) copy-start(s32[144]{0:T(256)} %param.14) | copy-start | bytes 1732
  0.7 13.4 %copy-start.12 = (s32[4]{0:T(128)S(1)}, s32[4]{0:T(128)}, u32[]{:S(2)}) copy-start(s32[4]{0:T(128)} %param.12) | copy-start | bytes 52
  0.7 18.3 %all-to-all-start = ((f32[4,512,128]{2,1,0:T(8,128)}), f32[4,512,128]{2,1,0:T(8,128)S(1)}, u32[]{:S(2)}, u32[]{:S(2)}) async-start(f32[4,512,128]{2,1,0:T(8,128)} %param.10), calls=%async_computation | async-start | bytes 2097152 | tf_op jit(solution)/shard_map/all_to_all | solution.py:275
  19.0 86.4 %all-to-all-start.1 = ((f32[4,1024,128]{1,2,0:T(8,128)}), f32[4,1024,128]{1,2,0:T(8,128)S(1)}, u32[]{:S(2)}, u32[]{:S(2)}) async-start(f32[4,1024,128]{1,2,0:T(8,128)} %copy.23), calls=%async_computation.1 | async-start | bytes 4194304 | tf_op jit(solution)/shard_map/all_to_all | solution.py:276
  22.8 1.0 copy-start.4
  38.5 22.3 %copy-start.7 = (f32[128,128]{1,0:T(8,128)S(1)}, f32[128,128]{1,0:T(8,128)}, u32[]{:S(2)}) copy-start(f32[128,128]{1,0:T(8,128)} %get-tuple-element.29) | copy-start | bytes 196612
  65.9 0.7 copy-start.6
  105.4 1.3 copy-start.1
  111.9 8.9 %copy-start = (f32[512,1024]{0,1:T(8,128)}, f32[512,1024]{0,1:T(8,128)S(1)}, u32[]{:S(2)}) copy-start(f32[512,1024]{0,1:T(8,128)S(1)} %convolution_multiply_fusion) | copy-start | bytes 6291460
  162.0 1.2 copy-start.8
  165.1 92.8 %all-to-all-start.2 = ((f32[64,104,128]{2,1,0:T(8,128)}), f32[64,104,128]{2,1,0:T(8,128)S(1)}, u32[]{:S(2)}, u32[]{:S(2)}) async-start(f32[64,104,128]{2,1,0:T(8,128)} %select_maximum_fusion), calls=%async_computation.2 | async-start | bytes 6815744 | tf_op jit(solution)/shard_map/all_to_all | solution.py:323
  260.0 14.0 %copy-start.9 = (f32[2,128,128]{2,1,0:T(8,128)S(1)}, f32[2,128,128]{2,1,0:T(8,128)}, u32[]{:S(2)}) copy-start(f32[2,128,128]{2,1,0:T(8,128)} %param.15) | copy-start | bytes 393220
  260.7 14.0 %copy-start.3 = (f32[4,512,128]{2,1,0:T(8,128)S(1)}, f32[4,512,128]{2,1,0:T(8,128)}, u32[]{:S(2)}) copy-start(f32[4,512,128]{2,1,0:T(8,128)} %shard_map.108) | copy-start | bytes 3145732
  261.7 14.0 %copy-start.2 = (f32[4,1024,128]{2,1,0:T(8,128)S(1)}, f32[4,1024,128]{2,1,0:T(8,128)}, u32[]{:S(2)}) copy-start(f32[4,1024,128]{2,1,0:T(8,128)} %shard_map.109) | copy-start | bytes 6291460

commit v8 on v7

--- a/solution.py
+++ b/solution.py
@@ -287,9 +287,9 @@
     first, second = pair_lists(P_SIZE)
     npair = len(first)
     blocks = lower_panel.reshape(group, P_SIZE, B, W)
-    gram = jnp.einsum("siac,sjbc->sijab", blocks, blocks, precision=lax.Precision.HIGHEST)
-    gram = gram.reshape(group, P_SIZE * P_SIZE, B, B)
-    contribution = gram[:, first * P_SIZE + second]
+    gram = jnp.einsum("sxc,syc->sxy", lower_panel, lower_panel, precision=lax.Precision.HIGHEST)
+    gram = gram.reshape(group, P_SIZE, B, P_SIZE, B)
+    contribution = jnp.moveaxis(gram[:, first, :, second, :], 0, 1)
 
     quarters = quarters_out(contribution, narrow_count, 3)
     quarter_rows = quarters.shape[2]

time: 278 us -> 272 us (0.978)
  local copies, waits for them, and re-layouts: 36.7 us -> 30.8 us
    transpose x1 -> x0, local copies, waits for them, and re-layouts: 5.36 us -> none  [local(): jnp.einsum('siac,sjbc->sijab', blocks, blocks, precision=lax.Precision.HI...]
    unnamed x29 -> x35, local copies, waits for them, and re-layouts: 7.13 us -> 7.14 us
  transfers between devices with their start and end apart: 3 -> 3, of which waited for: 2 -> 2; matrix products, arithmetic and copies ran while one was open for 13% -> 12% of each run, Pallas kernels for 36% -> 36%
where the time goes in v8:
time: 272 us; the launch traced here: 271 us
  Pallas kernels  134 us (49%)
  waiting for transfers between devices  41.8 us (15%)
  matrix products  33.4 us (12%)
  local copies, waits for them, and re-layouts  30.8 us (11%)
  starting transfers between devices  21.6 us (8%)
  other arithmetic  8.57 us (3%)
    pallas_call x4, Pallas kernels, block_chol(): pl.pallas_call(block_chol_kernel, out_shape=(jax.ShapeDtypeStruct((n, n),...  56.6 us
    pallas_call x2, Pallas kernels, columns_out(): pl.pallas_call(functools.partial(columns_out_kernel, count=count, group=g...  42.2 us
    all_to_all x1, waiting for transfers between devices, local(): lax.all_to_all(send_buffer, 'wide', split_axis=0, concat_axis=0, tiled=True)  36.7 us
    pallas_call x1, Pallas kernels, quarters_out(): pl.pallas_call(functools.partial(quarters_out_kernel, count=count, group=...  29 us
    all_to_all x1, starting transfers between devices, local(): lax.all_to_all(send_buffer, 'wide', split_axis=0, concat_axis=0, tiled=True)  13.9 us
    dot_general x1, matrix products, local(): jnp.einsum('sxc,syc->sxy', lower_panel, lower_panel, precision=lax.Precis...  8.97 us
    dot_general x6, matrix products, mm_t(): return jnp.einsum('sik,sjk->sij', a, b, precision=lax.Precision.HIGHEST)  7.51 us
    unnamed x35, local copies, waits for them, and re-layouts  7.14 us
  transfers between devices with their start and end apart: 3, of which 2 were waited for; matrix products, arithmetic and copies ran while one was open for 12% of the time, Pallas kernels for 36%

profile of v8, /device:TPU:9, one launch (start us, length us, event | category | flops | bytes accessed | tf_op | source)
XLA Modules:
  0.0 271.1 jit_solution(3547732454948945624)
XLA Ops:
  0.7 4.2 %all-to-all-start = ((f32[4,512,128]{2,1,0:T(8,128)}), f32[4,512,128]{2,1,0:T(8,128)S(1)}, u32[]{:S(2)}, u32[]{:S(2)}) async-start(f32[4,512,128]{2,1,0:T(8,128)} %param.12), calls=%async_computation | async-start | bytes 2097152 | tf_op jit(solution)/shard_map/all_to_all | solution.py:275
  4.8 1.8 copy.25
  13.9 5.1 %all-to-all-done = f32[4,512,128]{2,1,0:T(8,128)S(1)} async-done(((f32[4,512,128]{2,1,0:T(8,128)}), f32[4,512,128]{2,1,0:T(8,128)S(1)}, u32[]{:S(2)}, u32[]{:S(2)}) %all-to-all-start) | async-done | bytes 1048608 | tf_op jit(solution)/shard_map/all_to_all | solution.py:275
  19.0 3.6 %all-to-all-start.1 = ((f32[4,1024,128]{1,2,0:T(8,128)}), f32[4,1024,128]{1,2,0:T(8,128)S(1)}, u32[]{:S(2)}, u32[]{:S(2)}) async-start(f32[4,1024,128]{1,2,0:T(8,128)} %copy.25), calls=%async_computation.1 | async-start | bytes 4194304 | tf_op jit(solution)/shard_map/all_to_all | solution.py:276
  24.4 14.2 %shard_map.121 = (f32[128,128]{1,0:T(8,128)}, f32[128,128]{1,0:T(8,128)}) custom-call(f32[128,128]{1,0:T(8,128)} %slice_bitcast_fusion.10.a_ref), custom_call_target="tpu_custom_call" | custom-call | tf_op jit(solution)/shard_map/pallas_call | solution.py:114
  38.5 1.4 fusion.37
  39.9 1.7 fusion.3
  44.8 14.2 %shard_map.122 = (f32[128,128]{1,0:T(8,128)}, f32[128,128]{1,0:T(8,128)}) custom-call(f32[128,128]{1,0:T(8,128)} %slice_bitcast_fusion.9.a_ref), custom_call_target="tpu_custom_call" | custom-call | tf_op jit(solution)/shard_map/pallas_call | solution.py:114
  60.9 1.3 convolution_bitcast_fusion.4
  62.2 1.5 fusion.72
  67.2 14.2 %shard_map.123 = (f32[128,128]{1,0:T(8,128)}, f32[128,128]{1,0:T(8,128)}) custom-call(f32[128,128]{1,0:T(8,128)} %slice_bitcast_fusion.6.a_ref), custom_call_target="tpu_custom_call" | custom-call | tf_op jit(solution)/shard_map/pallas_call | solution.py:114
  82.5 1.7 fusion.9.a_ref
  84.3 14.2 %shard_map.124 = (f32[128,128]{1,0:T(8,128)}, f32[128,128]{1,0:T(8,128)}) custom-call(f32[128,128]{1,0:T(8,128)} %fusion.9.a_ref), custom_call_target="tpu_custom_call" | custom-call | tf_op jit(solution)/shard_map/pallas_call | solution.py:114
  98.4 1.4 convolution_bitcast_fusion.2
  99.8 1.5 fusion.4
  101.4 1.2 convolution_bitcast_fusion.1
  102.7 2.0 select_maximum_fusion.1.x_ref
  104.7 1.3 copy-done.1
  106.0 5.1 %convolution_multiply_fusion = f32[512,1024]{0,1:T(8,128)S(1)} fusion(f32[1024,512]{0,1:T(8,128)} %bitcast.176, f32[1,128,512]{2,1,0:T(8,128)S(1)} %convolution_bitcast_fusion.1, f32[1,128,512]{2,1,0:T(8,128)S(1)} %convolution_bitcast_fusion.2, f32[1,128,512]{2,1,0:T(8,128)S(1)} %convolution_bitcast_fusion.4, f32[1,128,512]{2,1,0:T(8,128)S(1)} %concatenate.50, ...), kind=kOutput, calls=%fused_computation.11 | convolution fusion | flops 3222536192 | bytes 5246976 | tf_op jit(solution)/shard_map/srk,sck->src/dot_general | solution.py:279
  111.2 9.0 %fusion.74 = f32[8,128,8,128]{3,1,2,0:T(8,128)} fusion(f32[8,128,512,1]{2,1,3,0:T(8,128)S(1)} %bitcast.169, f32[8,128,512,1]{2,1,0,3:T(8,128)S(1)} %bitcast.170), kind=kOutput, calls=%fused_computation.131 | convolution fusion | flops 6442450944 | bytes 8388608 | tf_op jit(solution)/shard_map/sxc,syc->sxy/dot_general | solution.py:290
  120.1 4.5 %gather_fusion = f32[36,128,128]{2,1,0:T(8,128)} fusion(f32[8,128,8,128]{3,1,2,0:T(8,128)} %fusion.74, s32[36]{0:T(128)S(1)} %copy-done.6), kind=kCustom, calls=%fused_computation | custom fusion | bytes 4718880 | tf_op jit(solution)/shard_map/gather | solution.py:292
  124.6 29.0 %shard_map.125 = f32[4,36,32,128]{3,2,1,0:T(8,128)} custom-call(f32[1,36,128,128]{3,2,1,0:T(8,128)} %bitcast.175), custom_call_target="tpu_custom_call" | custom-call | bytes 4718592 | tf_op jit(solution)/shard_map/pallas_call | solution.py:202
  153.6 2.4 gather_fusion.1
  157.2 2.0 select_maximum_fusion
  159.2 13.9 %all-to-all-start.2 = ((f32[64,104,128]{2,1,0:T(8,128)}), f32[64,104,128]{2,1,0:T(8,128)S(1)}, u32[]{:S(2)}, u32[]{:S(2)}) async-start(f32[64,104,128]{2,1,0:T(8,128)} %select_maximum_fusion), calls=%async_computation.2 | async-start | bytes 6815744 | tf_op jit(solution)/shard_map/all_to_all | solution.py:323
  173.1 26.4 %shard_map.127 = f32[4,1024,128]{2,1,0:T(8,128)} custom-call(f32[1,1024,512]{2,1,0:T(8,128)} %bitcast.171), custom_call_target="tpu_custom_call" | custom-call | bytes 4194304 | tf_op jit(solution)/shard_map/pallas_call | solution.py:63
  199.5 15.8 %shard_map.126 = f32[4,512,128]{2,1,0:T(8,128)} custom-call(f32[1,512,512]{2,1,0:T(8,128)} %select_maximum_fusion.1.x_ref), custom_call_target="tpu_custom_call" | custom-call | bytes 2097152 | tf_op jit(solution)/shard_map/pallas_call | solution.py:63
  215.3 36.7 %all-to-all-done.2 = f32[64,104,128]{2,1,0:T(8,128)S(1)} async-done(((f32[64,104,128]{2,1,0:T(8,128)}), f32[64,104,128]{2,1,0:T(8,128)S(1)}, u32[]{:S(2)}, u32[]{:S(2)}) %all-to-all-start.2) | async-done | bytes 3407904 | tf_op jit(solution)/shard_map/all_to_all | solution.py:323
  252.0 2.1 slice.118
  255.8 4.8 %fusion = f32[4,2,32,128]{3,0,2,1:T(4,128)S(1)} fusion(f32[192,32,128]{2,1,0:T(8,128)} %bitcast.173, s32[4,2]{0,1:T(2,128)S(1)} %multiply_add_fusion, s32[192]{0:T(256)S(1)} %convert_element_type.46), kind=kOutput, calls=%fused_computation.7 | convolution fusion | flops 75499008 | bytes 3277600 | tf_op jit(solution)/shard_map/ri,rab->iab/dot_general | solution.py:333
  261.2 5.9 %shard_map.128 = f32[4,2,32,128]{3,2,1,0:T(8,128)} custom-call(f32[4,2,32,128]{3,2,1,0:T(8,128)} %copy.29.x_ref), custom_call_target="tpu_custom_call" | custom-call | bytes 262144 | tf_op jit(solution)/shard_map/pallas_call | solution.py:153
  269.7 1.3 copy.48
  (84 shorter events, 24.6 us)
Async XLA Ops:
  0.6 4.2 %copy-start.5 = (f32[4,1024,128]{2,1,0:T(8,128)S(1)}, f32[4,1024,128]{2,1,0:T(8,128)}, u32[]{:S(2)}) copy-start(f32[4,1024,128]{2,1,0:T(8,128)} %param.13) | copy-start | bytes 6291460
  0.6 6.0 %copy-start.13 = (s32[144,1]{0,1:T(1,128)S(1)}, s32[144,1]{0,1:T(1,128)}, u32[]{:S(2)}) copy-start(s32[144,1]{0,1:T(1,128)} %param.15) | copy-start | bytes 1732
  0.7 9.5 %copy-start.14 = (s32[144]{0:T(256)S(1)}, s32[144]{0:T(256)}, u32[]{:S(2)}) copy-start(s32[144]{0:T(256)} %param.16) | copy-start | bytes 1732
  0.7 11.4 %copy-start.15 = (s32[4]{0:T(128)S(1)}, s32[4]{0:T(128)}, u32[]{:S(2)}) copy-start(s32[4]{0:T(128)} %param.14) | copy-start | bytes 52
  0.7 18.3 %all-to-all-start = ((f32[4,512,128]{2,1,0:T(8,128)}), f32[4,512,128]{2,1,0:T(8,128)S(1)}, u32[]{:S(2)}, u32[]{:S(2)}) async-start(f32[4,512,128]{2,1,0:T(8,128)} %param.12), calls=%async_computation | async-start | bytes 2097152 | tf_op jit(solution)/shard_map/all_to_all | solution.py:275
  19.0 85.7 %all-to-all-start.1 = ((f32[4,1024,128]{1,2,0:T(8,128)}), f32[4,1024,128]{1,2,0:T(8,128)S(1)}, u32[]{:S(2)}, u32[]{:S(2)}) async-start(f32[4,1024,128]{1,2,0:T(8,128)} %copy.25), calls=%async_computation.1 | async-start | bytes 4194304 | tf_op jit(solution)/shard_map/all_to_all | solution.py:276
  22.8 1.0 copy-start.4
  38.5 22.3 %copy-start.8 = (f32[128,128]{1,0:T(8,128)S(1)}, f32[128,128]{1,0:T(8,128)}, u32[]{:S(2)}) copy-start(f32[128,128]{1,0:T(8,128)} %get-tuple-element.29) | copy-start | bytes 196612
  65.9 0.7 copy-start.7
  98.4 4.2 %copy-start.11 = (f32[128,128]{1,0:T(8,128)S(1)}, f32[128,128]{1,0:T(8,128)}, u32[]{:S(2)}) copy-start(f32[128,128]{1,0:T(8,128)} %get-tuple-element.35) | copy-start | bytes 196612
  98.4 4.2 %copy-start.12 = (f32[128,128]{1,0:T(8,128)S(1)}, f32[128,128]{1,0:T(8,128)}, u32[]{:S(2)}) copy-start(f32[128,128]{1,0:T(8,128)} %get-tuple-element.36) | copy-start | bytes 196612
  104.7 1.3 copy-start.1
  111.1 9.0 %copy-start = (f32[512,1024]{0,1:T(8,128)}, f32[512,1024]{0,1:T(8,128)S(1)}, u32[]{:S(2)}) copy-start(f32[512,1024]{0,1:T(8,128)S(1)} %convolution_multiply_fusion) | copy-start | bytes 6291460
  111.2 9.0 %copy-start.6 = (s32[36]{0:T(128)S(1)}, s32[36]{0:T(128)}, u32[]{:S(2)}) copy-start(s32[36]{0:T(128)} %constant.129) | copy-start | bytes 436
  156.0 1.2 copy-start.9
  159.2 92.8 %all-to-all-start.2 = ((f32[64,104,128]{2,1,0:T(8,128)}), f32[64,104,128]{2,1,0:T(8,128)S(1)}, u32[]{:S(2)}, u32[]{:S(2)}) async-start(f32[64,104,128]{2,1,0:T(8,128)} %select_maximum_fusion), calls=%async_computation.2 | async-start | bytes 6815744 | tf_op jit(solution)/shard_map/all_to_all | solution.py:323
  254.1 14.0 %copy-start.10 = (f32[2,128,128]{2,1,0:T(8,128)S(1)}, f32[2,128,128]{2,1,0:T(8,128)}, u32[]{:S(2)}) copy-start(f32[2,128,128]{2,1,0:T(8,128)} %param.17) | copy-start | bytes 393220
  254.8 14.0 %copy-start.3 = (f32[4,512,128]{2,1,0:T(8,128)S(1)}, f32[4,512,128]{2,1,0:T(8,128)}, u32[]{:S(2)}) copy-start(f32[4,512,128]{2,1,0:T(8,128)} %shard_map.126) | copy-start | bytes 3145732
  255.8 14.0 %copy-start.2 = (f32[4,1024,128]{2,1,0:T(8,128)S(1)}, f32[4,1024,128]{2,1,0:T(8,128)}, u32[]{:S(2)}) copy-start(f32[4,1024,128]{2,1,0:T(8,128)} %shard_map.127) | copy-start | bytes 6291460

commit v9 on v8

--- a/solution.py
+++ b/solution.py
@@ -330,7 +330,7 @@
     slot_table = (got_slots[:, None] == jnp.arange(row_slots, dtype=jnp.int32)[None, :]).astype(
         jnp.float32
     )
-    slot_sums = jnp.einsum("ri,rab->iab", slot_table, received, precision=lax.Precision.HIGHEST)
+    slot_sums = jnp.sum(slot_table.T[:, :, None, None] * received[None], axis=1)
     slot_sums = slot_sums.reshape(narrow_count, T_DEV, quarter_rows, B)
     arrived = chunks_out(slot_sums, 2)
     summed = jnp.swapaxes(arrived, 0, 1).reshape(T_DEV, B, B)

time: 272 us -> 271 us (level)
  other arithmetic: 8.57 us -> 16.1 us
  matrix products: 33.4 us -> 28.5 us
    reduce_sum x0 -> x1, other arithmetic: none -> 5.45 us  [local(): slot_sums = jnp.sum(slot_table.T[:, :, None, None] * received[None], axis=1)]
    dot_general x1 -> x0, matrix products: 4.77 us -> none  [local(): jnp.einsum('ri,rab->iab', slot_table, received, precision=lax.Precision.H...]
    unnamed x35 -> x31, local copies, waits for them, and re-layouts: 7.14 us -> 7.13 us
  transfers between devices with their start and end apart: 3 -> 3, of which waited for: 2 -> 2; matrix products, arithmetic and copies ran while one was open for 12% -> 13% of each run, Pallas kernels for 36% -> 37%
where the time goes in v9:
time: 271 us; the launch traced here: 269 us
  Pallas kernels  134 us (49%)
  waiting for transfers between devices  39.1 us (14%)
  local copies, waits for them, and re-layouts  29.2 us (11%)
  matrix products  28.5 us (11%)
  starting transfers between devices  21.6 us (8%)
  other arithmetic  16.1 us (6%)
    pallas_call x4, Pallas kernels, block_chol(): pl.pallas_call(block_chol_kernel, out_shape=(jax.ShapeDtypeStruct((n, n),...  56.6 us
    pallas_call x2, Pallas kernels, columns_out(): pl.pallas_call(functools.partial(columns_out_kernel, count=count, group=g...  42.2 us
    all_to_all x1, waiting for transfers between devices, local(): lax.all_to_all(send_buffer, 'wide', split_axis=0, concat_axis=0, tiled=True)  36.7 us
    pallas_call x1, Pallas kernels, quarters_out(): pl.pallas_call(functools.partial(quarters_out_kernel, count=count, group=...  29 us
    all_to_all x1, starting transfers between devices, local(): lax.all_to_all(send_buffer, 'wide', split_axis=0, concat_axis=0, tiled=True)  13.9 us
    dot_general x1, matrix products, local(): jnp.einsum('sxc,syc->sxy', lower_panel, lower_panel, precision=lax.Precis...  8.89 us
    dot_general x6, matrix products, mm_t(): return jnp.einsum('sik,sjk->sij', a, b, precision=lax.Precision.HIGHEST)  7.48 us
    unnamed x31, local copies, waits for them, and re-layouts  7.13 us
  transfers between devices with their start and end apart: 3, of which 2 were waited for; matrix products, arithmetic and copies ran while one was open for 13% of the time, Pallas kernels for 37%

profile of v9, /device:TPU:9, one launch (start us, length us, event | category | flops | bytes accessed | tf_op | source)
XLA Modules:
  0.0 269.5 jit_solution(15844900371908336230)
XLA Ops:
  0.7 4.2 %all-to-all-start = ((f32[4,512,128]{2,1,0:T(8,128)}), f32[4,512,128]{2,1,0:T(8,128)S(1)}, u32[]{:S(2)}, u32[]{:S(2)}) async-start(f32[4,512,128]{2,1,0:T(8,128)} %param.12), calls=%async_computation | async-start | bytes 2097152 | tf_op jit(solution)/shard_map/all_to_all | solution.py:275
  12.9 1.8 copy.44
  16.6 2.4 all-to-all-done
  19.0 3.6 %all-to-all-start.1 = ((f32[4,1024,128]{1,2,0:T(8,128)}), f32[4,1024,128]{1,2,0:T(8,128)S(1)}, u32[]{:S(2)}, u32[]{:S(2)}) async-start(f32[4,1024,128]{1,2,0:T(8,128)} %copy.44), calls=%async_computation.1 | async-start | bytes 4194304 | tf_op jit(solution)/shard_map/all_to_all | solution.py:276
  24.4 14.2 %shard_map.121 = (f32[128,128]{1,0:T(8,128)}, f32[128,128]{1,0:T(8,128)}) custom-call(f32[128,128]{1,0:T(8,128)} %slice_bitcast_fusion.10.a_ref), custom_call_target="tpu_custom_call" | custom-call | tf_op jit(solution)/shard_map/pallas_call | solution.py:114
  38.5 1.4 fusion.34
  39.9 1.7 fusion
  44.8 14.2 %shard_map.122 = (f32[128,128]{1,0:T(8,128)}, f32[128,128]{1,0:T(8,128)}) custom-call(f32[128,128]{1,0:T(8,128)} %slice_bitcast_fusion.9.a_ref), custom_call_target="tpu_custom_call" | custom-call | tf_op jit(solution)/shard_map/pallas_call | solution.py:114
  60.9 1.3 convolution_bitcast_fusion.4
  62.2 1.5 fusion.66
  67.2 14.2 %shard_map.123 = (f32[128,128]{1,0:T(8,128)}, f32[128,128]{1,0:T(8,128)}) custom-call(f32[128,128]{1,0:T(8,128)} %slice_bitcast_fusion.6.a_ref), custom_call_target="tpu_custom_call" | custom-call | tf_op jit(solution)/shard_map/pallas_call | solution.py:114
  82.5 1.7 fusion.6.a_ref
  84.2 14.2 %shard_map.124 = (f32[128,128]{1,0:T(8,128)}, f32[128,128]{1,0:T(8,128)}) custom-call(f32[128,128]{1,0:T(8,128)} %fusion.6.a_ref), custom_call_target="tpu_custom_call" | custom-call | tf_op jit(solution)/shard_map/pallas_call | solution.py:114
  98.4 1.4 convolution_bitcast_fusion.2
  99.8 1.5 fusion.1
  101.3 1.2 convolution_bitcast_fusion.1
  102.6 2.0 select_maximum_fusion.1.x_ref
  104.6 1.3 copy-done.1
  105.9 5.1 %convolution_multiply_fusion = f32[512,1024]{0,1:T(8,128)S(1)} fusion(f32[1024,512]{0,1:T(8,128)} %bitcast.172, f32[1,128,512]{2,1,0:T(8,128)S(1)} %convolution_bitcast_fusion.1, f32[1,128,512]{2,1,0:T(8,128)S(1)} %convolution_bitcast_fusion.2, f32[1,128,512]{2,1,0:T(8,128)S(1)} %convolution_bitcast_fusion.4, f32[1,128,512]{2,1,0:T(8,128)S(1)} %concatenate.50, ...), kind=kOutput, calls=%fused_computation.9 | convolution fusion | flops 3222536192 | bytes 5246976 | tf_op jit(solution)/shard_map/srk,sck->src/dot_general | solution.py:279
  111.1 8.9 %fusion.68 = f32[8,128,8,128]{3,1,2,0:T(8,128)} fusion(f32[8,128,512,1]{2,1,3,0:T(8,128)S(1)} %bitcast.165, f32[8,128,512,1]{2,1,0,3:T(8,128)S(1)} %bitcast.166), kind=kOutput, calls=%fused_computation.126 | convolution fusion | flops 6442450944 | bytes 8388608 | tf_op jit(solution)/shard_map/sxc,syc->sxy/dot_general | solution.py:290
  120.0 4.5 %gather_fusion = f32[36,128,128]{2,1,0:T(8,128)} fusion(f32[8,128,8,128]{3,1,2,0:T(8,128)} %fusion.68, s32[36]{0:T(128)S(1)} %copy-done.6), kind=kCustom, calls=%fused_computation | custom fusion | bytes 4718880 | tf_op jit(solution)/shard_map/gather | solution.py:292
  124.5 29.0 %shard_map.125 = f32[4,36,32,128]{3,2,1,0:T(8,128)} custom-call(f32[1,36,128,128]{3,2,1,0:T(8,128)} %bitcast.171), custom_call_target="tpu_custom_call" | custom-call | bytes 4718592 | tf_op jit(solution)/shard_map/pallas_call | solution.py:202
  153.5 2.4 gather_fusion.1
  157.1 2.0 select_maximum_fusion
  159.0 13.9 %all-to-all-start.2 = ((f32[64,104,128]{2,1,0:T(8,128)}), f32[64,104,128]{2,1,0:T(8,128)S(1)}, u32[]{:S(2)}, u32[]{:S(2)}) async-start(f32[64,104,128]{2,1,0:T(8,128)} %select_maximum_fusion), calls=%async_computation.2 | async-start | bytes 6815744 | tf_op jit(solution)/shard_map/all_to_all | solution.py:323
  172.9 15.2 %shard_map.126 = f32[4,512,128]{2,1,0:T(8,128)} custom-call(f32[1,512,512]{2,1,0:T(8,128)} %select_maximum_fusion.1.x_ref), custom_call_target="tpu_custom_call" | custom-call | bytes 2097152 | tf_op jit(solution)/shard_map/pallas_call | solution.py:63
  188.1 27.0 %shard_map.127 = f32[4,1024,128]{2,1,0:T(8,128)} custom-call(f32[1,1024,512]{2,1,0:T(8,128)} %bitcast.167), custom_call_target="tpu_custom_call" | custom-call | bytes 4194304 | tf_op jit(solution)/shard_map/pallas_call | solution.py:63
  215.1 36.7 %all-to-all-done.2 = f32[64,104,128]{2,1,0:T(8,128)S(1)} async-done(((f32[64,104,128]{2,1,0:T(8,128)}), f32[64,104,128]{2,1,0:T(8,128)S(1)}, u32[]{:S(2)}, u32[]{:S(2)}) %all-to-all-start.2) | async-done | bytes 3407904 | tf_op jit(solution)/shard_map/all_to_all | solution.py:323
  252.0 2.1 slice.118
  254.2 5.4 %multiply_reduce_fusion = f32[8,32,128]{2,1,0:T(8,128)} fusion(f32[192,32,128]{2,1,0:T(8,128)} %bitcast.169, f32[8,192]{1,0:T(8,128)S(1)} %fusion.47), kind=kLoop, calls=%fused_computation.5 | loop fusion | flops 12550144 | bytes 3282944 | tf_op jit(solution)/shard_map/reduce_sum | solution.py:333
  259.6 5.9 %shard_map.128 = f32[4,2,32,128]{3,2,1,0:T(8,128)} custom-call(f32[4,2,32,128]{3,2,1,0:T(8,128)} %bitcast.182), custom_call_target="tpu_custom_call" | custom-call | bytes 262144 | tf_op jit(solution)/shard_map/pallas_call | solution.py:153
  268.2 1.3 copy.59
  (79 shorter events, 25.2 us)
Async XLA Ops:
  0.6 12.2 %copy-start.5 = (f32[4,1024,128]{2,1,0:T(8,128)S(1)}, f32[4,1024,128]{2,1,0:T(8,128)}, u32[]{:S(2)}) copy-start(f32[4,1024,128]{2,1,0:T(8,128)} %param.13) | copy-start | bytes 6291460
  0.6 14.0 %copy-start.13 = (s32[4]{0:T(128)S(1)}, s32[4]{0:T(128)}, u32[]{:S(2)}) copy-start(s32[4]{0:T(128)} %param.14) | copy-start | bytes 52
  0.7 18.3 %all-to-all-start = ((f32[4,512,128]{2,1,0:T(8,128)}), f32[4,512,128]{2,1,0:T(8,128)S(1)}, u32[]{:S(2)}, u32[]{:S(2)}) async-start(f32[4,512,128]{2,1,0:T(8,128)} %param.12), calls=%async_computation | async-start | bytes 2097152 | tf_op jit(solution)/shard_map/all_to_all | solution.py:275
  19.0 85.6 %all-to-all-start.1 = ((f32[4,1024,128]{1,2,0:T(8,128)}), f32[4,1024,128]{1,2,0:T(8,128)S(1)}, u32[]{:S(2)}, u32[]{:S(2)}) async-start(f32[4,1024,128]{1,2,0:T(8,128)} %copy.44), calls=%async_computation.1 | async-start | bytes 4194304 | tf_op jit(solution)/shard_map/all_to_all | solution.py:276
  22.7 1.0 copy-start.4
  38.5 22.3 %copy-start.8 = (f32[128,128]{1,0:T(8,128)S(1)}, f32[128,128]{1,0:T(8,128)}, u32[]{:S(2)}) copy-start(f32[128,128]{1,0:T(8,128)} %get-tuple-element.29) | copy-start | bytes 196612
  65.8 0.7 copy-start.7
  98.4 4.2 %copy-start.11 = (f32[128,128]{1,0:T(8,128)S(1)}, f32[128,128]{1,0:T(8,128)}, u32[]{:S(2)}) copy-start(f32[128,128]{1,0:T(8,128)} %get-tuple-element.35) | copy-start | bytes 196612
  98.4 4.2 %copy-start.12 = (f32[128,128]{1,0:T(8,128)S(1)}, f32[128,128]{1,0:T(8,128)}, u32[]{:S(2)}) copy-start(f32[128,128]{1,0:T(8,128)} %get-tuple-element.36) | copy-start | bytes 196612
  104.6 1.3 copy-start.1
  111.1 8.9 %copy-start = (f32[512,1024]{0,1:T(8,128)}, f32[512,1024]{0,1:T(8,128)S(1)}, u32[]{:S(2)}) copy-start(f32[512,1024]{0,1:T(8,128)S(1)} %convolution_multiply_fusion) | copy-start | bytes 6291460
  111.1 8.9 %copy-start.6 = (s32[36]{0:T(128)S(1)}, s32[36]{0:T(128)}, u32[]{:S(2)}) copy-start(s32[36]{0:T(128)} %constant.127) | copy-start | bytes 436
  155.9 1.2 copy-start.9
  159.0 92.8 %all-to-all-start.2 = ((f32[64,104,128]{2,1,0:T(8,128)}), f32[64,104,128]{2,1,0:T(8,128)S(1)}, u32[]{:S(2)}, u32[]{:S(2)}) async-start(f32[64,104,128]{2,1,0:T(8,128)} %select_maximum_fusion), calls=%async_computation.2 | async-start | bytes 6815744 | tf_op jit(solution)/shard_map/all_to_all | solution.py:323
  254.0 12.5 %copy-start.10 = (f32[2,128,128]{2,1,0:T(8,128)S(1)}, f32[2,128,128]{2,1,0:T(8,128)}, u32[]{:S(2)}) copy-start(f32[2,128,128]{2,1,0:T(8,128)} %param.17) | copy-start | bytes 393220
  254.0 13.2 %copy-start.3 = (f32[4,512,128]{2,1,0:T(8,128)S(1)}, f32[4,512,128]{2,1,0:T(8,128)}, u32[]{:S(2)}) copy-start(f32[4,512,128]{2,1,0:T(8,128)} %shard_map.126) | copy-start | bytes 3145732
  254.2 14.0 %copy-start.2 = (f32[4,1024,128]{2,1,0:T(8,128)S(1)}, f32[4,1024,128]{2,1,0:T(8,128)}, u32[]{:S(2)}) copy-start(f32[4,1024,128]{2,1,0:T(8,128)} %shard_map.127) | copy-start | bytes 6291460
